TPU v7x, 512 devices: a whole 4x8x8 slice. The times are simulated.
512 devices in a mesh: dom: 32 (over y, x), orient: 16 (over z, core).
Axes of the slice: x: 4, y: 8, z: 8, core: 2. Of those that a mesh axis runs over, the one named last changes fastest.
Arguments:
- particles: bfloat16 [256, 2, 8192], P('dom'), may hold values from -4 to 4
- references: bfloat16 [256, 2, 8192], P('orient'), may hold values from -1.7 to 1.7
- phases: float32 [16, 8192], replicated, may hold values from -3.1416 to 3.1416
- mask: int32 [256, 256], P('dom', 'orient'), may hold values from 0 to 1, as said below
- ctf_group: int32 [256], replicated, may hold values from 0 to 63
- ctf_table: float32 [64, 64], replicated, may hold values from 0.1 to 1
- shell_index: int32 [8192], replicated, may hold values from 0 to 63
- sigma2: float32 [64], replicated, may hold values from 8 to 32
Outputs:
- posterior: float32 [256, 16, 256], P('dom', None, 'orient')
- image_sums: float32 [256, 2, 8192], P('orient', None, 'dom')
- ctf_weights: float32 [256, 64], P('orient')
- shell_noise: float32 [64], replicated
Inputs may be any that keep to these rules, and one draw needn't show every extreme that they name: `mask`: every particle allows at least one orientation.
All inputs are finite; a program needn't handle non-finite values.
Results may differ from a plain program's by a relative error of at most 0.0041.
Values may be sent and summed in bfloat16 or wider, within the bound.
A program may use at most 192 MiB of HBM per device.

v0:
```python
import jax
import jax.numpy as jnp
from jax import lax
from jax.sharding import PartitionSpec as P

trans_block = 2


def make_images(planes, ctf_pix, cosine, sine_part):
    real_part = planes[:, 0][:, None, :]
    imag_part = planes[:, 1][:, None, :]
    shifted_real = real_part * cosine[None] - imag_part * sine_part[None]
    shifted_imag = real_part * sine_part[None] + imag_part * cosine[None]
    factor = ctf_pix[:, None, :]
    return jnp.stack([factor * shifted_real, factor * shifted_imag], axis=2).astype(jnp.bfloat16)


def on_device(particles, references, phases, mask, ctf_group, ctf_table, shell_index, sigma2):
    highest = lax.Precision.HIGHEST
    part_dev = particles.shape[0]
    ori_dev = references.shape[0]
    pixels = shell_index.shape[0]
    shells = ctf_table.shape[1]
    trans_count = phases.shape[0]
    blocks = trans_count // trans_block
    dom_size = lax.axis_size("dom")
    width = pixels // dom_size
    dom_index = lax.axis_index("dom")
    shell_pick = (shell_index[:, None] == jnp.arange(shells, dtype=jnp.int32)[None, :]).astype(
        jnp.float32
    )
    group_pick = (
        ctf_group[:, None] == jnp.arange(ctf_table.shape[0], dtype=jnp.int32)[None, :]
    ).astype(jnp.float32)
    ctf_all = jnp.dot(group_pick, ctf_table, precision=highest)
    ctf_rows = lax.dynamic_slice_in_dim(ctf_all, dom_index * part_dev, part_dev, 0)
    ctf_pix = jnp.dot(ctf_rows, shell_pick.T, precision=highest)
    sigma_pix = jnp.dot(shell_pick, sigma2, precision=highest)
    refs_wide = references.astype(jnp.float32)
    weighted = (refs_wide / sigma_pix).astype(jnp.bfloat16)
    ref_norm = jnp.dot(jnp.sum(refs_wide * refs_wide, axis=1), shell_pick, precision=highest)
    energy = ref_norm / sigma2
    ctf_square = ctf_rows * ctf_rows
    quadratic = 0.5 * jnp.dot(ctf_square, energy.T, precision=highest)
    planes = particles.astype(jnp.float32)
    cosines = jnp.cos(phases)
    sine_rows = jnp.sin(phases)

    def score_block(index):
        first = index * trans_block
        images = make_images(
            planes,
            ctf_pix,
            lax.dynamic_slice_in_dim(cosines, first, trans_block, 0),
            lax.dynamic_slice_in_dim(sine_rows, first, trans_block, 0),
        )
        cross = jnp.einsum("ptcx,ocx->pto", images, weighted, preferred_element_type=jnp.float32)
        return cross - quadratic[:, None, :]

    stacked = lax.map(score_block, jnp.arange(blocks, dtype=jnp.int32))
    scores = jnp.moveaxis(stacked, 0, 1).reshape(part_dev, trans_count, ori_dev)
    scores = jnp.where((mask == 1)[:, None, :], scores, -1e30)
    local_peak = jnp.max(scores, axis=(1, 2))
    peak = lax.pmax(local_peak, "orient")
    total = lax.psum(jnp.sum(jnp.exp(scores - peak[:, None, None]), axis=(1, 2)), "orient")
    posterior = jnp.exp(scores - peak[:, None, None]) / total[:, None, None]
    post_half = posterior.astype(jnp.bfloat16)
    weight_rows = jnp.sum(posterior, axis=1)
    ctf_part = jnp.dot(weight_rows.T, ctf_square, precision=highest)
    part_norm = jnp.dot(jnp.sum(planes * planes, axis=1), shell_pick, precision=highest)
    term_one = jnp.sum(part_norm * jnp.sum(weight_rows, axis=1)[:, None], axis=0)
    term_three = jnp.sum(ctf_part * ref_norm, axis=0)
    start_pix = dom_index * width
    pick_cols = lax.dynamic_slice_in_dim(shell_pick, start_pix, width, 0)

    def add_block(index, running):
        first = index * trans_block
        images = make_images(
            planes,
            ctf_pix,
            lax.dynamic_slice_in_dim(cosines, first, trans_block, 0),
            lax.dynamic_slice_in_dim(sine_rows, first, trans_block, 0),
        )
        weights = lax.dynamic_slice_in_dim(post_half, first, trans_block, 1)
        return running + jnp.einsum(
            "pto,ptcx->ocx", weights, images, preferred_element_type=jnp.float32
        )

    partial_sums = lax.fori_loop(0, blocks, add_block, jnp.zeros((ori_dev, 2, pixels), jnp.float32))
    image_sums = lax.psum_scatter(partial_sums, "dom", scatter_dimension=2, tiled=True)
    ref_cols = lax.dynamic_slice_in_dim(refs_wide, start_pix, width, 2)
    term_two = -2.0 * jnp.dot(
        jnp.sum(image_sums * ref_cols, axis=(0, 1)), pick_cols, precision=highest
    )
    ctf_weights = lax.psum(ctf_part, "dom")
    shell_total = lax.psum(term_one + term_two + term_three, ("dom", "orient"))
    divisor = part_dev * dom_size * pixels / shells
    return (posterior, image_sums, ctf_weights, shell_total / divisor)


def solution(mesh):
    return jax.shard_map(
        on_device,
        mesh=mesh,
        in_specs=(
            P("dom", None, None),
            P("orient", None, None),
            P(),
            P("dom", "orient"),
            P(),
            P(),
            P(),
            P(),
        ),
        out_specs=(P("dom", None, "orient"), P("orient", None, "dom"), P("orient", None), P()),
        check_vma=False,
    )
```

profile of v0, /device:TPU:1, one launch (start us, length us, event | category | flops | bytes accessed | tf_op | source)
XLA Modules:
  0.0 511.5 jit_solution(465495128250471743)
XLA Ops:
  7.3 0.7 broadcast_compare_fusion
  8.0 1.1 copy_convert_fusion
  9.1 2.8 fusion.46
  12.0 0.7 fusion.15
  12.7 1.9 multiply_reduce_fusion
  14.6 1.1 copy.23
  15.7 1.1 fusion.14
  17.1 0.7 fusion.16
  18.0 21.1 %while.24 = (s32[]{:T(128)}, f32[8,8,2,16]{3,1,2,0:T(8,128)S(1)}, f32[8,8192]{1,0:T(8,128)S(1)}, f32[8,2,8192]{2,0,1:T(8,128)S(1)}, s32[8]{0:T(128)S(1)}, /*inde...) while((s32[]{:T(128)}, f32[8,8,2,16]{3,1,2,0:T(8,128)S(1)}, ...), condition=%wide.region_2.3_spmd, body=%wide.region_1.2_spmd.sunk | while | flops 9961734 | bytes 5910755 | solution.py:60
  19.5 0.8 copy-done.4
  22.2 0.8 copy-done.4
  24.8 0.8 copy-done.4
  27.4 0.8 copy-done.4
  30.1 0.8 copy-done.4
  32.7 0.8 copy-done.4
  35.3 0.8 copy-done.4
  38.0 0.8 copy-done.4
  39.2 30.6 %pmax.7 = f32[8]{0:T(128)S(1)} all-reduce(f32[8]{0:T(128)S(1)} %select_reduce_fusion), channel_id=1, replica_groups=mesh['dom'=32,'orient'=16] {'orient'}, use_global_device_ids=true, to_apply=%region_4.5 | all-reduce | flops 8 | bytes 64 | tf_op jit(solution)/shard_map/pmax | solution.py:64
  70.0 25.8 %psum.21 = f32[8]{0:T(128)S(1)} all-reduce(f32[8]{0:T(128)S(1)} %fusion.30), channel_id=1, replica_groups=mesh['dom'=32,'orient'=16] {'orient'}, use_global_device_ids=true, to_apply=%region_6.7 | all-reduce | flops 8 | bytes 64 | tf_op jit(solution)/shard_map/psum | solution.py:65
  95.9 0.7 fusion.45
  96.6 6.0 %while.25 = (s32[]{:T(128)}, f32[16,2,8192]{2,0,1:T(8,128)S(1)}, bf16[8,16,16]{2,1,0:T(8,128)(2,1)S(1)}, f32[8,8192]{1,0:T(8,128)S(1)}, f32[8,2,8192]{2,0,1:T(8,...) while((s32[]{:T(128)}, f32[16,2,8192]{2,0,1:T(8,128)S(1)}, ...), condition=%wide.region_8.9_spmd.clone, body=%wide.region_7.8_spmd.clone.sunk | while | flops 11272199 | bytes 5375669 | solution.py:89
  102.6 31.4 %copy.29 = f32[16,2,8192]{1,0,2:T(8,128)} copy(f32[16,2,8192]{2,0,1:T(8,128)S(1)} %get-tuple-element.176) | data formatting | bytes 2097152
  134.0 46.1 %reshape.85 = f32[8192,32]{1,0:T(8,128)} reshape(f32[8192,16,2]{2,1,0:T(8,128)} %bitcast.18) | data formatting | bytes 2097152
  181.0 0.9 multiply_reduce_fusion.3
  182.3 63.1 %psum.22 = f32[16,64]{1,0:T(8,128)} all-reduce(f32[16,64]{1,0:T(8,128)S(1)} %get-tuple-element.302), channel_id=1, replica_groups=mesh['dom'=32,'orient'=16] {'dom'}, use_global_device_ids=true, to_apply=%region_11.12 | all-reduce | flops 1024 | bytes 8192 | tf_op jit(solution)/shard_map/psum | solution.py:95
  245.5 1.1 fusion.18
  246.6 1.1 iota_compare_fusion
  247.7 150.6 %reduce-scatter.4.cloned.1.call-done = f32[256,32]{1,0:T(8,128)} async-done(((f32[8192,32]{1,0:T(8,128)}), f32[256,32]{1,0:T(8,128)}) %reduce-scatter.4.cloned.1.call-update) | async-done | bytes 32784
  398.3 2.1 reshape.86
  400.5 1.0 copy.30
  401.6 0.8 fusion.21
  402.4 101.8 %psum.23 = f32[64]{0:T(128)S(1)} all-reduce(f32[64]{0:T(128)S(1)} %fusion.21), channel_id=1, replica_groups=mesh['dom'=32,'orient'=16] {'dom','orient'}, use_global_device_ids=true, to_apply=%region_17.18 | all-reduce | flops 64 | bytes 512 | tf_op jit(solution)/shard_map/psum | solution.py:96
  (127 shorter events, 17.8 us)
Async XLA Ops:
  7.2 9.6 %copy-start = (f32[64,64]{1,0:T(8,128)S(1)}, f32[64,64]{1,0:T(8,128)}, u32[]{:S(2)}) copy-start(f32[64,64]{1,0:T(8,128)} %param.17) | copy-start | bytes 49156
  7.2 4.7 copy-start.7
  7.2 4.7 copy-start.12
  7.2 5.5 %copy-start.1 = (bf16[16,2,8192]{2,1,0:T(2,128)(2,1)S(1)}, bf16[16,2,8192]{2,1,0:T(2,128)(2,1)}, u32[]{:S(2)}) copy-start(bf16[16,2,8192]{2,1,0:T(2,128)(2,1)} %param.13) | copy-start | bytes 1572868
  7.2 391.1 %reduce-scatter.4.cloned.1.call-start = ((), (), s32[]{:S(2)}) async-start(), calls=%async_computation.1 | async-start | bytes 4325376
  11.9 4.9 copy-start.11
  17.1 0.9 copy-start.5
  19.2 1.0 copy-start.4
  21.9 1.0 copy-start.4
  24.5 1.0 copy-start.4
  27.2 1.0 copy-start.4
  29.8 1.0 copy-start.4
  32.4 1.0 copy-start.4
  35.0 1.0 copy-start.4
  37.7 1.0 copy-start.4
  95.8 0.8 copy-start.9
  180.1 0.7 copy-start.10
  180.1 1.8 copy-start.2
  180.1 65.3 %copy-start.3 = (bf16[8,2,8192]{2,1,0:T(2,128)(2,1)S(1)}, bf16[8,2,8192]{2,1,0:T(2,128)(2,1)}, u32[]{:S(2)}) copy-start(bf16[8,2,8192]{2,1,0:T(2,128)(2,1)} %param.12) | copy-start | bytes 786436
  180.8 64.8 %copy-start.8 = (s32[8192]{0:T(1024)S(1)}, s32[8192]{0:T(1024)}, u32[]{:S(2)}) copy-start(s32[8192]{0:T(1024)} %param.18) | copy-start | bytes 98308
  401.5 103.2 %copy-start.6 = (f32[16,2,256]{2,1,0:T(2,128)}, f32[16,2,256]{2,1,0:T(2,128)S(1)}, u32[]{:S(2)}) copy-start(f32[16,2,256]{2,1,0:T(2,128)S(1)} %copy.30) | copy-start | bytes 98308
Sparse Core Ops, SparseCore 0:
  180.3 218.0 reduce-scatter.3
where the time goes:
time: 513 us; the launch traced here: 512 us
  blocking collectives  221 us (43%)
  waiting for transfers between devices  151 us (29%)
  local copies, waits for them, and re-layouts  97.7 us (19%)
  between operations  14.2 us (3%)
  matrix products  11.8 us (2%)
  other arithmetic  9.8 us (2%)
  loops' own time  6.02 us (1%)
    unnamed x2, waiting for transfers between devices  151 us
    psum x1, blocking collectives, on_device(): shell_total = lax.psum(term_one + term_two + term_three, ('dom', 'orient'))  102 us
    unnamed x28, local copies, waits for them, and re-layouts  81.4 us
    psum x1, blocking collectives, on_device(): ctf_weights = lax.psum(ctf_part, 'dom')  63.1 us
    pmax x1, blocking collectives, on_device(): peak = lax.pmax(local_peak, 'orient')  30.6 us
    psum x1, blocking collectives, on_device(): lax.psum(jnp.sum(jnp.exp(scores - peak[:, None, None]), axis=(1, 2)), 'or...  25.8 us
  transfers between devices with their start and end apart: 1, of which 1 were waited for; matrix products, arithmetic and copies ran while one was open for 1% of the time, Pallas kernels for 0%

commit v1 on v0

v1 whole, which is shorter than its diff:
```python
import functools

import jax
import jax.numpy as jnp
from jax import lax
from jax.experimental import pallas as pl
from jax.experimental.pallas import tpu as pltpu
from jax.sharding import PartitionSpec as P

MESH_ID = pl.DeviceIdType.MESH


def _exchange_kernel(axis, n, width, x_ref, o_ref, held, send_sem, recv_sem):
    me = lax.axis_index(axis)
    barrier = pltpu.get_barrier_semaphore()

    def greet(k, carry):
        peer = lax.rem(me + k, n)
        pl.semaphore_signal(barrier, inc=1, device_id={axis: peer}, device_id_type=MESH_ID)
        return carry

    lax.fori_loop(1, n, greet, 0)
    pl.semaphore_wait(barrier, n - 1)

    def source(peer):
        if width is None:
            return x_ref
        return x_ref.at[:, pl.ds(pl.multiple_of(peer * width, width), width)]

    def copy(k):
        peer = lax.rem(me + k, n)
        return pltpu.make_async_remote_copy(
            src_ref=source(peer),
            dst_ref=held.at[me],
            send_sem=send_sem.at[k],
            recv_sem=recv_sem.at[k],
            device_id={axis: peer},
            device_id_type=MESH_ID,
        )

    def start(k, carry):
        copy(k).start()
        return carry

    lax.fori_loop(1, n, start, 0)
    if width is None:
        held[me] = x_ref[...]
    else:
        held[me] = x_ref[:, pl.ds(pl.multiple_of(me * width, width), width)]

    def finish(k, carry):
        copy(k).wait()
        return carry

    lax.fori_loop(1, n, finish, 0)
    o_ref[...] = held[...]


def exchange(x, axis, n, collective_id, width=None):
    block = x.shape if width is None else (x.shape[0], width)
    gathered = (n,) + block
    return pl.pallas_call(
        functools.partial(_exchange_kernel, axis, n, width),
        out_shape=jax.ShapeDtypeStruct(gathered, x.dtype),
        in_specs=[pl.BlockSpec(memory_space=pltpu.VMEM)],
        out_specs=pl.BlockSpec(memory_space=pltpu.VMEM),
        scratch_shapes=[
            pltpu.VMEM(gathered, x.dtype),
            pltpu.SemaphoreType.DMA((n,)),
            pltpu.SemaphoreType.DMA((n,)),
        ],
        compiler_params=pltpu.CompilerParams(collective_id=collective_id, has_side_effects=True),
    )(x)


def make_images(planes, ctf_pix, cosine, sine_part):
    real_part = planes[:, 0][:, None, :]
    imag_part = planes[:, 1][:, None, :]
    shifted_real = real_part * cosine[None] - imag_part * sine_part[None]
    shifted_imag = real_part * sine_part[None] + imag_part * cosine[None]
    factor = ctf_pix[:, None, :]
    return jnp.stack([factor * shifted_real, factor * shifted_imag], axis=2).astype(jnp.bfloat16)


def pad_rows(rows, lanes):
    r, c = rows.shape
    height = -(-r // 8) * 8
    return jnp.pad(rows, ((0, height - r), (0, lanes - c)))


def on_device(particles, references, phases, mask, ctf_group, ctf_table, shell_index, sigma2):
    highest = lax.Precision.HIGHEST
    part_dev = particles.shape[0]
    ori_dev = references.shape[0]
    pixels = shell_index.shape[0]
    shells = ctf_table.shape[1]
    trans_count = phases.shape[0]
    dom_size = lax.axis_size("dom")
    orient_size = lax.axis_size("orient")
    width = pixels // dom_size
    dom_index = lax.axis_index("dom")

    columns = exchange(particles.reshape(part_dev * 2, pixels), "dom", dom_size, 0, width=width)

    shell_pick = (shell_index[:, None] == jnp.arange(shells, dtype=jnp.int32)[None, :]).astype(
        jnp.float32
    )
    group_pick = (
        ctf_group[:, None] == jnp.arange(ctf_table.shape[0], dtype=jnp.int32)[None, :]
    ).astype(jnp.float32)
    ctf_all = jnp.dot(group_pick, ctf_table, precision=highest)
    ctf_rows = lax.dynamic_slice_in_dim(ctf_all, dom_index * part_dev, part_dev, 0)
    ctf_pix = jnp.dot(ctf_rows, shell_pick.T, precision=highest)
    sigma_pix = jnp.dot(shell_pick, sigma2, precision=highest)
    refs_wide = references.astype(jnp.float32)
    weighted = (refs_wide / sigma_pix).astype(jnp.bfloat16)
    ref_norm = jnp.dot(jnp.sum(refs_wide * refs_wide, axis=1), shell_pick, precision=highest)
    energy = ref_norm / sigma2
    ctf_square = ctf_rows * ctf_rows
    quadratic = 0.5 * jnp.dot(ctf_square, energy.T, precision=highest)
    planes = particles.astype(jnp.float32)
    cosines = jnp.cos(phases)
    sine_rows = jnp.sin(phases)

    images = make_images(planes, ctf_pix, cosines, sine_rows)
    cross = jnp.einsum("itpk,jpk->itj", images, weighted, preferred_element_type=jnp.float32)
    scores = cross - quadratic[:, None, :]
    scores = jnp.where((mask == 1)[:, None, :], scores, -1e30)
    local_peak = jnp.max(scores, axis=(1, 2))
    local_total = jnp.sum(jnp.exp(scores - local_peak[:, None, None]), axis=(1, 2))

    stats = exchange(pad_rows(jnp.stack([local_peak, local_total]), 128), "orient", orient_size, 1)
    peaks = stats[:, 0, :part_dev]
    totals = stats[:, 1, :part_dev]
    peak = jnp.max(peaks, axis=0)
    total = jnp.sum(totals * jnp.exp(peaks - peak[None, :]), axis=0)
    posterior = jnp.exp(scores - peak[:, None, None]) / total[:, None, None]
    post_half = posterior.astype(jnp.bfloat16)

    weight_rows = jnp.sum(posterior, axis=1)
    ctf_part = jnp.dot(weight_rows.T, ctf_square, precision=highest)
    part_norm = jnp.dot(jnp.sum(planes * planes, axis=1), shell_pick, precision=highest)
    term_one = jnp.sum(part_norm * jnp.sum(weight_rows, axis=1)[:, None], axis=0)
    term_three = jnp.sum(ctf_part * ref_norm, axis=0)
    local_sums = jnp.einsum("itj,itpk->jpk", post_half, images, preferred_element_type=jnp.float32)
    term_two = -2.0 * jnp.dot(jnp.sum(local_sums * refs_wide, axis=(0, 1)), shell_pick, precision=highest)
    terms = term_one + term_two + term_three

    lanes = trans_count * ori_dev
    post_rows = posterior.reshape(part_dev, lanes)
    packed = jnp.concatenate([post_rows, jnp.pad(terms, (0, lanes - shells))[None]], axis=0)
    packed = pad_rows(packed, lanes)
    gathered = exchange(packed, "dom", dom_size, 2)
    post_all = gathered[:, :part_dev, :].reshape(dom_size * part_dev, trans_count, ori_dev)
    dom_terms = jnp.sum(gathered[:, part_dev, :shells], axis=0)

    orient_terms = exchange(pad_rows(dom_terms[None], 128), "orient", orient_size, 3)
    shell_total = jnp.sum(orient_terms[:, 0, :shells], axis=0)

    ctf_weights = jnp.dot(jnp.sum(post_all, axis=1).T, ctf_all * ctf_all, precision=highest)

    start_pix = dom_index * width
    pick_cols = lax.dynamic_slice_in_dim(shell_pick, start_pix, width, 0)
    ctf_cols = jnp.dot(ctf_all, pick_cols.T, precision=highest)
    cos_cols = lax.dynamic_slice_in_dim(cosines, start_pix, width, 1)
    sin_cols = lax.dynamic_slice_in_dim(sine_rows, start_pix, width, 1)
    col_planes = columns.reshape(dom_size * part_dev, 2, width).astype(jnp.float32)
    col_images = make_images(col_planes, ctf_cols, cos_cols, sin_cols)
    image_sums = jnp.einsum(
        "itj,itpk->jpk", post_all.astype(jnp.bfloat16), col_images, preferred_element_type=jnp.float32
    )

    divisor = part_dev * dom_size * pixels / shells
    return (posterior, image_sums, ctf_weights, shell_total / divisor)


def solution(mesh):
    return jax.shard_map(
        on_device,
        mesh=mesh,
        in_specs=(
            P("dom", None, None),
            P("orient", None, None),
            P(),
            P("dom", "orient"),
            P(),
            P(),
            P(),
            P(),
        ),
        out_specs=(P("dom", None, "orient"), P("orient", None, "dom"), P("orient", None), P()),
        check_vma=False,
    )
```

time: 513 us -> 110 us (0.21)
  blocking collectives: 221 us -> 0 us
  waiting for transfers between devices: 151 us -> 0 us
  local copies, waits for them, and re-layouts: 97.7 us -> 14.4 us
  Pallas kernels: 0 us -> 67.8 us
  between operations: 14.2 us -> 0.95 us
  loops' own time: 6.02 us -> 0 us
    psum x3 -> x0, blocking collectives: 191 us -> none  [the longest x1 102 us: on_device(): shell_total = lax.psum(term_one + term_two + term_three, ('dom', 'orient'))]
    unnamed x2 -> x0, waiting for transfers between devices: 151 us -> none
    unnamed x28 -> x26, local copies, waits for them, and re-layouts: 81.4 us -> 2.12 us
    pallas_call x0 -> x4, Pallas kernels: none -> 67.8 us  [exchange(): pl.pallas_call(functools.partial(_exchange_kernel, axis, n, width), out_s...]
    pmax x1 -> x0, blocking collectives: 30.6 us -> none  [on_device(): peak = lax.pmax(local_peak, 'orient')]
    while x17 -> x0, local copies, waits for them, and re-layouts: 7.17 us -> none
    another operation x2 -> x0, loops' own time: 6.02 us -> none  [the longest x1 5.52 us: on_device(): stacked = lax.map(score_block, jnp.arange(blocks, dtype=jnp.int32))]
    dynamic_slice x32 -> x1, local copies, waits for them, and re-layouts: 5.76 us -> 0.01 us  [on_device(): sin_cols = lax.dynamic_slice_in_dim(sine_rows, start_pix, width, 1)]
  transfers between devices with their start and end apart: 1 -> 0, of which waited for: 1 -> 0; matrix products, arithmetic and copies ran while one was open for 1% -> 0% of each run, Pallas kernels for 0% -> 0%
where the time goes in v1:
time: 110 us; the launch traced here: 109 us
  Pallas kernels  67.8 us (62%)
  local copies, waits for them, and re-layouts  14.4 us (13%)
  matrix products  14.1 us (13%)
  other arithmetic  11.9 us (11%)
    pallas_call x4, Pallas kernels, exchange(): pl.pallas_call(functools.partial(_exchange_kernel, axis, n, width), out_s...  67.8 us
    reshape x2, local copies, waits for them, and re-layouts, on_device(): gathered[:, :part_dev, :].reshape(dom_size * part_dev, trans_count, ori_dev)  3.07 us
    cos x1, local copies, waits for them, and re-layouts, on_device(): cosines = jnp.cos(phases)  2.8 us
    dot_general x1, matrix products, on_device(): jnp.einsum('itj,itpk->jpk', post_half, images, preferred_element_type=jnp...  2.78 us
    another operation x2, other arithmetic  2.67 us

profile of v1, /device:TPU:1, one launch (start us, length us, event | category | flops | bytes accessed | tf_op | source)
XLA Modules:
  0.0 109.2 jit_solution(10767951577072645059)
XLA Ops:
  0.7 0.7 copy-done
  1.4 1.0 fusion.38
  2.4 1.6 %fusion.10 = f32[8,8192]{1,0:T(8,128)S(1)} fusion(s32[8192]{0:T(1024)} %param.14, f32[256,64]{0,1:T(8,128)S(1)} %fusion.38, s32[]{:T(128)S(6)} %select_n.12), kind=kOutput, calls=%fused_computation.17 | convolution fusion | flops 50855936 | bytes 327684 | tf_op jit(solution)/shard_map/dot_general | solution.py:113
  3.9 2.8 %fusion.66 = (f32[16,8192]{1,0:T(8,128)S(1)}, f32[16,8192]{1,0:T(8,128)S(1)}) fusion(f32[16,8192]{1,0:T(8,128)} %param.10), kind=kLoop, calls=%fused_computation.96 | loop fusion | bytes 1572864 | tf_op jit(solution)/shard_map/cos | solution.py:122
  7.0 1.3 %multiply_convert_fusion.3 = (bf16[8,16,1,8192]{3,1,2,0:T(8,128)(2,1)S(1)}, bf16[8,16,1,8192]{3,1,2,0:T(8,128)(2,1)S(1)}) fusion(f32[16,8192]{1,0:T(8,128)S(1)} %get-tuple-element.28, f32[8,8192]{1,0:T(8,128)S(1)} %get-tuple-element.26, f32[16,8192]{1,0:T(8,128)S(1)} %get-tuple-element.27, f32[8,8192]{1,0:T(8,128)S(1)} %get-tuple-element.25, ...), kind=kLoop, calls=%fused_computation.10 | loop fusion | flops 10485760 | bytes 6029312 | tf_op jit(solution)/shard_map/convert.3
  8.6 1.1 %fusion.8 = f32[16,64]{1,0:T(8,128)S(1)} fusion(f32[16,8192]{1,0:T(8,128)S(1)} %fusion.26, s32[8192]{0:T(1024)S(1)} %copy-done.7), kind=kOutput, calls=%fused_computation.15 | convolution fusion | flops 101187584 | bytes 561152 | tf_op jit(solution)/shard_map/dot_general | solution.py:117
  10.0 0.8 fusion.9
  10.8 1.4 %fusion.67 = (f32[8]{0:T(128)S(1)}, f32[8,16,16]{2,1,0:T(8,128)S(1)}) fusion(f32[8,16]{1,0:T(8,128)S(1)} %convolution_multiply_fusion.1, f32[8192]{0:T(1024)S(1)} %bitcast.79, bf16[16,2,8192]{2,1,0:T(2,128)(2,1)S(1)} %copy-done.3, bf16[8,16,1,8192]{3,1,2,0:T(8,128)(2,1)S(1)} %get-tuple-element.20, bf16[8,16,1,8192]{3,1,2,0:T(8,128)(2,1)S(1)} %get-tuple-element.19, ...), kind=kOutput, calls=%fused_computation.97 | convolution fusion | flops 69998584 | bytes 4760224 | tf_op jit(solution)/shard_map/itpk,jpk->itj/dot_general | solution.py:126
  13.6 17.6 %shard_map.111 = f32[16,8,128]{2,1,0:T(8,128)} custom-call(f32[8,128]{1,0:T(8,128)} %select_maximum_fusion.1.x_ref), custom_call_target="tpu_custom_call" | custom-call | tf_op jit(solution)/shard_map/pallas_call | solution.py:62
  31.3 1.5 %slice_reduce_fusion.2 = (f32[8]{0:T(128)}, f32[16,1,8]{2,1,0:T(1,128)S(1)}, f32[16,1,8]{2,1,0:T(1,128)S(1)}) fusion(f32[16,8,128]{2,1,0:T(8,128)} %shard_map.111), kind=kLoop, calls=%fused_computation.93 | loop fusion | flops 120 | bytes 2080 | tf_op jit(solution)/shard_map/reduce_max | solution.py:135
  32.7 0.7 copy.25
  33.5 0.9 fusion.54
  34.3 1.1 fusion.64
  35.4 2.8 %fusion.11 = f32[8192]{0:T(1024)S(1)} fusion(bf16[8,16,1,8192]{3,1,2,0:T(8,128)(2,1)} %copy-done.2, bf16[8,16,1,8192]{3,1,2,0:T(8,128)(2,1)S(1)} %get-tuple-element.19, bf16[16,2,8192]{2,1,0:T(2,128)(2,1)} %param.9, f32[8,16,16]{2,1,0:T(8,128)S(1)} %get-tuple-element.18), kind=kOutput, calls=%fused_computation.20 | convolution fusion | flops 76277760 | bytes 4759552 | tf_op jit(solution)/shard_map/itj,itpk->jpk/dot_general | solution.py:145
  38.7 1.1 fusion.20
  39.7 1.1 fusion.24
  40.8 0.9 reshape.85
  42.3 22.4 %shard_map.112 = f32[32,16,256]{2,1,0:T(8,128)} custom-call(f32[16,256]{1,0:T(8,128)} %select_maximum_fusion.x_ref), custom_call_target="tpu_custom_call" | custom-call | tf_op jit(solution)/shard_map/pallas_call | solution.py:62
  64.8 1.7 %slice.31 = f32[32,8,256]{2,1,0:T(8,128)} slice(f32[32,16,256]{2,1,0:T(8,128)} %shard_map.112), slice={[0:32], [0:8], [0:256]} | slice | bytes 524288 | tf_op jit(solution)/shard_map/slice | solution.py:154
  66.4 1.7 %reshape.86 = f32[256,16,16]{2,1,0:T(8,128)S(1)} reshape(f32[32,8,256]{2,1,0:T(8,128)} %slice.31) | data formatting | bytes 524288 | tf_op jit(solution)/shard_map/reshape | solution.py:154
  68.1 1.2 %reduce_sum.117 = f32[256,16]{1,0:T(8,128)} reduce(f32[256,16,16]{2,1,0:T(8,128)S(1)} %reshape.86, f32[]{:T(128)} %constant.10.clone.1), dimensions={1}, to_apply=%region_11.12 | reduce | flops 61440 | bytes 278532 | tf_op jit(solution)/shard_map/reduce_sum | solution.py:160
  69.3 1.9 %fusion.39 = f32[16,64]{1,0:T(8,128)} fusion(f32[256,16]{1,0:T(8,128)} %reduce_sum.117, f32[256,64]{0,1:T(8,128)S(1)} %fusion.38), kind=kOutput, calls=%fused_computation.54 | convolution fusion | flops 3162112 | bytes 86016 | tf_op jit(solution)/shard_map/dot_general | solution.py:160
  71.1 1.4 %copy.29 = bf16[256,16,16]{0,2,1:T(8,128)(2,1)} copy(f32[256,16,16]{2,1,0:T(8,128)S(1)} %reshape.86) | data formatting | bytes 393216 | tf_op jit(solution)/shard_map/reshape | solution.py:154
  73.1 0.8 reshape.87.x_ref
  74.0 15.5 %shard_map.113 = bf16[32,16,256]{2,1,0:T(8,128)(2,1)} custom-call(bf16[16,8192]{1,0:T(8,128)(2,1)} %reshape.87.x_ref), custom_call_target="tpu_custom_call" | custom-call | tf_op jit(solution)/shard_map/pallas_call | solution.py:62
  89.5 1.2 %reshape.88 = f32[256,2,256]{2,1,0:T(2,128)S(1)} reshape(bf16[32,16,256]{2,1,0:T(8,128)(2,1)} %shard_map.113) | data formatting | bytes 786432 | tf_op jit(solution)/shard_map/convert_element_type | solution.py:167
  91.2 1.4 %multiply_convert_fusion.1 = (bf16[256,16,1,256]{3,0,1,2:T(8,128)(2,1)S(1)}, bf16[256,16,1,256]{3,0,1,2:T(8,128)(2,1)S(1)}) fusion(f32[16,256]{1,0:T(8,128)S(1)} %get-tuple-element.34, f32[256,256]{1,0:T(8,128)S(1)} %get-tuple-element.36, f32[16,256]{1,0:T(8,128)S(1)} %get-tuple-element.35, f32[256,256]{1,0:T(8,128)S(1)} %get-tuple-element.37, ...), kind=kLoop, calls=%fused_computation.8 | loop fusion | flops 10485760 | bytes 5013504 | tf_op jit(solution)/shard_map/convert.1
  92.6 0.8 fusion.15
  93.4 0.6 copy.30
  94.0 1.0 slice_reduce_fusion
  95.6 12.3 %shard_map.114 = f32[16,8,128]{2,1,0:T(8,128)} custom-call(f32[8,128]{1,0:T(8,128)} %pad.19.x_ref), custom_call_target="tpu_custom_call" | custom-call | tf_op jit(solution)/shard_map/pallas_call | solution.py:62
  107.8 0.9 slice_reduce_fusion.1
  (42 shorter events, 5.5 us)
Async XLA Ops:
  0.6 0.8 copy-start
  0.6 6.1 %copy-start.1 = (bf16[8,2,8192]{2,1,0:T(2,128)(2,1)S(1)}, bf16[8,2,8192]{2,1,0:T(2,128)(2,1)}, u32[]{:S(2)}) copy-start(bf16[8,2,8192]{2,1,0:T(2,128)(2,1)} %param.8) | copy-start | bytes 786436
  6.9 1.3 %copy-start.3 = (bf16[16,2,8192]{2,1,0:T(2,128)(2,1)S(1)}, bf16[16,2,8192]{2,1,0:T(2,128)(2,1)}, u32[]{:S(2)}) copy-start(bf16[16,2,8192]{2,1,0:T(2,128)(2,1)} %param.9) | copy-start | bytes 1572868
  7.0 1.6 %copy-start.7 = (s32[8192]{0:T(1024)S(1)}, s32[8192]{0:T(1024)}, u32[]{:S(2)}) copy-start(s32[8192]{0:T(1024)} %param.14) | copy-start | bytes 98308
  7.0 2.7 %copy-start.11 = (f32[64]{0:T(128)S(1)}, f32[64]{0:T(128)}, u32[]{:S(2)}) copy-start(f32[64]{0:T(128)} %param.15) | copy-start | bytes 772
  8.3 3.9 %copy-start.2 = (bf16[8,16,1,8192]{3,1,2,0:T(8,128)(2,1)}, bf16[8,16,1,8192]{3,1,2,0:T(8,128)(2,1)S(1)}, u32[]{:S(2)}) copy-start(bf16[8,16,1,8192]{3,1,2,0:T(8,128)(2,1)S(1)} %get-tuple-element.20) | copy-start | bytes 6291460
  8.3 2.5 %copy-start.10 = (s32[8,16]{1,0:T(8,128)S(1)}, s32[8,16]{1,0:T(8,128)}, u32[]{:S(2)}) copy-start(s32[8,16]{1,0:T(8,128)} %param.11) | copy-start | bytes 1540
  9.7 1.1 copy-start.8
  12.2 0.6 copy-start.5
  35.4 2.8 %copy-start.4 = (f32[8,16,16]{2,1,0:T(8,128)}, f32[8,16,16]{2,1,0:T(8,128)S(1)}, u32[]{:S(2)}) copy-start(f32[8,16,16]{2,1,0:T(8,128)S(1)} %get-tuple-element.18) | copy-start | bytes 24580
  35.4 2.8 %copy-start.9 = (f32[16,64]{1,0:T(8,128)S(1)}, f32[16,64]{1,0:T(8,128)}, u32[]{:S(2)}) copy-start(f32[16,64]{1,0:T(8,128)} %copy-done.8) | copy-start | bytes 12292
  91.1 1.4 %copy-start.6 = (bf16[256,16,16]{0,2,1:T(8,128)(2,1)S(1)}, bf16[256,16,16]{0,2,1:T(8,128)(2,1)}, u32[]{:S(2)}) copy-start(bf16[256,16,16]{0,2,1:T(8,128)(2,1)} %copy.29) | copy-start | bytes 393220

commit v2 on v1

--- a/solution.py
+++ b/solution.py
@@ -10,7 +10,12 @@
 MESH_ID = pl.DeviceIdType.MESH
 
 
-def _exchange_kernel(axis, n, width, x_ref, o_ref, held, send_sem, recv_sem):
+def _exchange_kernel(axis, n, widths, *refs):
+    count = len(widths)
+    x_refs = refs[:count]
+    o_refs = refs[count : 2 * count]
+    held = refs[2 * count : 3 * count]
+    send_sem, recv_sem = refs[3 * count :]
     me = lax.axis_index(axis)
     barrier = pltpu.get_barrier_semaphore()
 
@@ -22,55 +27,59 @@
     lax.fori_loop(1, n, greet, 0)
     pl.semaphore_wait(barrier, n - 1)
 
-    def source(peer):
+    def part(index, peer):
+        width = widths[index]
         if width is None:
-            return x_ref
-        return x_ref.at[:, pl.ds(pl.multiple_of(peer * width, width), width)]
-
-    def copy(k):
+            return x_refs[index]
+        return x_refs[index].at[:, pl.ds(pl.multiple_of(peer * width, width), width)]
+
+    def copy(index, k):
         peer = lax.rem(me + k, n)
         return pltpu.make_async_remote_copy(
-            src_ref=source(peer),
-            dst_ref=held.at[me],
-            send_sem=send_sem.at[k],
-            recv_sem=recv_sem.at[k],
+            src_ref=part(index, peer),
+            dst_ref=held[index].at[me],
+            send_sem=send_sem.at[index, k],
+            recv_sem=recv_sem.at[index, k],
             device_id={axis: peer},
             device_id_type=MESH_ID,
         )
 
     def start(k, carry):
-        copy(k).start()
+        for index in range(count):
+            copy(index, k).start()
         return carry
 
     lax.fori_loop(1, n, start, 0)
-    if width is None:
-        held[me] = x_ref[...]
-    else:
-        held[me] = x_ref[:, pl.ds(pl.multiple_of(me * width, width), width)]
+    for index in range(count):
+        held[index][me] = part(index, me)[...]
 
     def finish(k, carry):
-        copy(k).wait()
+        for index in range(count):
+            copy(index, k).wait()
         return carry
 
     lax.fori_loop(1, n, finish, 0)
-    o_ref[...] = held[...]
-
-
-def exchange(x, axis, n, collective_id, width=None):
-    block = x.shape if width is None else (x.shape[0], width)
-    gathered = (n,) + block
+    for index in range(count):
+        o_refs[index][...] = held[index][...]
+
+
+def exchange(payloads, axis, n, collective_id):
+    widths = tuple(width for _, width in payloads)
+    shapes = []
+    for x, width in payloads:
+        block = x.shape if width is None else (x.shape[0], width)
+        shapes.append(jax.ShapeDtypeStruct((n,) + block, x.dtype))
+    count = len(payloads)
+    vmem = pl.BlockSpec(memory_space=pltpu.VMEM)
     return pl.pallas_call(
-        functools.partial(_exchange_kernel, axis, n, width),
-        out_shape=jax.ShapeDtypeStruct(gathered, x.dtype),
-        in_specs=[pl.BlockSpec(memory_space=pltpu.VMEM)],
-        out_specs=pl.BlockSpec(memory_space=pltpu.VMEM),
-        scratch_shapes=[
-            pltpu.VMEM(gathered, x.dtype),
-            pltpu.SemaphoreType.DMA((n,)),
-            pltpu.SemaphoreType.DMA((n,)),
-        ],
+        functools.partial(_exchange_kernel, axis, n, widths),
+        out_shape=tuple(shapes),
+        in_specs=[vmem] * count,
+        out_specs=tuple([vmem] * count),
+        scratch_shapes=[pltpu.VMEM(shape.shape, shape.dtype) for shape in shapes]
+        + [pltpu.SemaphoreType.DMA((count, n)), pltpu.SemaphoreType.DMA((count, n))],
         compiler_params=pltpu.CompilerParams(collective_id=collective_id, has_side_effects=True),
-    )(x)
+    )(*[x for x, _ in payloads])
 
 
 def make_images(planes, ctf_pix, cosine, sine_part):
@@ -99,8 +108,6 @@
     orient_size = lax.axis_size("orient")
     width = pixels // dom_size
     dom_index = lax.axis_index("dom")
-
-    columns = exchange(particles.reshape(part_dev * 2, pixels), "dom", dom_size, 0, width=width)
 
     shell_pick = (shell_index[:, None] == jnp.arange(shells, dtype=jnp.int32)[None, :]).astype(
         jnp.float32
@@ -129,7 +136,7 @@
     local_peak = jnp.max(scores, axis=(1, 2))
     local_total = jnp.sum(jnp.exp(scores - local_peak[:, None, None]), axis=(1, 2))
 
-    stats = exchange(pad_rows(jnp.stack([local_peak, local_total]), 128), "orient", orient_size, 1)
+    (stats,) = exchange([(pad_rows(jnp.stack([local_peak, local_total]), 128), None)], "orient", orient_size, 1)
     peaks = stats[:, 0, :part_dev]
     totals = stats[:, 1, :part_dev]
     peak = jnp.max(peaks, axis=0)
@@ -150,11 +157,13 @@
     post_rows = posterior.reshape(part_dev, lanes)
     packed = jnp.concatenate([post_rows, jnp.pad(terms, (0, lanes - shells))[None]], axis=0)
     packed = pad_rows(packed, lanes)
-    gathered = exchange(packed, "dom", dom_size, 2)
+    gathered, columns = exchange(
+        [(packed, None), (particles.reshape(part_dev * 2, pixels), width)], "dom", dom_size, 2
+    )
     post_all = gathered[:, :part_dev, :].reshape(dom_size * part_dev, trans_count, ori_dev)
     dom_terms = jnp.sum(gathered[:, part_dev, :shells], axis=0)
 
-    orient_terms = exchange(pad_rows(dom_terms[None], 128), "orient", orient_size, 3)
+    (orient_terms,) = exchange([(pad_rows(dom_terms[None], 128), None)], "orient", orient_size, 3)
     shell_total = jnp.sum(orient_terms[:, 0, :shells], axis=0)
 
     ctf_weights = jnp.dot(jnp.sum(post_all, axis=1).T, ctf_all * ctf_all, precision=highest)

time: 110 us -> 94.2 us (0.86)
  Pallas kernels: 67.8 us -> 57.6 us
  local copies, waits for them, and re-layouts: 14.4 us -> 9.42 us
    pallas_call x4 -> x3, Pallas kernels: 67.8 us -> 57.6 us  [exchange(): pl.pallas_call(functools.partial(_exchange_kernel, axis, n, widths), out_...]
    reshape x2, local copies, waits for them, and re-layouts: 3.07 us -> 1.4 us  [on_device(): gathered[:, :part_dev, :].reshape(dom_size * part_dev, trans_count, ori_dev)]
    unnamed x26 -> x24, local copies, waits for them, and re-layouts: 2.12 us -> 0.75 us
    dot_general x1, matrix products: 0.79 us -> 2.12 us  [on_device(): sigma_pix = jnp.dot(shell_pick, sigma2, precision=highest)]
where the time goes in v2:
time: 94.2 us; the launch traced here: 93.5 us
  Pallas kernels  57.6 us (61%)
  matrix products  14.6 us (15%)
  other arithmetic  11 us (12%)
  local copies, waits for them, and re-layouts  9.42 us (10%)
    pallas_call x3, Pallas kernels, exchange(): pl.pallas_call(functools.partial(_exchange_kernel, axis, n, widths), out_...  57.6 us
    dot_general x1, matrix products, on_device(): jnp.einsum('itj,itpk->jpk', post_half, images, preferred_element_type=jnp...  2.7 us
    another operation x2, other arithmetic  2.67 us
    dot_general x1, matrix products, on_device(): sigma_pix = jnp.dot(shell_pick, sigma2, precision=highest)  2.12 us
    cos x1, local copies, waits for them, and re-layouts, on_device(): cosines = jnp.cos(phases)  2.04 us

profile of v2, /device:TPU:1, one launch (start us, length us, event | category | flops | bytes accessed | tf_op | source)
XLA Modules:
  0.0 93.5 jit_solution(4459962543187227284)
XLA Ops:
  0.7 0.8 broadcast_compare_fusion
  1.4 2.1 %fusion.9 = f32[1,8192]{1,0:T(1,128)} fusion(s32[8192]{0:T(1024)} %param.14, f32[64]{0:T(128)} %param.15), kind=kOutput, calls=%fused_computation.16 | convolution fusion | flops 6815744 | bytes 65792 | tf_op jit(solution)/shard_map/dot_general | solution.py:121
  3.6 1.0 %fusion.38 = f32[256,64]{0,1:T(8,128)S(1)} fusion(f32[64,64]{1,0:T(8,128)S(1)} %copy-done, s32[256]{0:T(256)} %param.12), kind=kOutput, calls=%fused_computation.53 | convolution fusion | flops 12599296 | bytes 82944 | tf_op jit(solution)/shard_map/dot_general | solution.py:118
  4.5 1.6 %fusion.10 = f32[8,8192]{1,0:T(8,128)S(1)} fusion(s32[8192]{0:T(1024)} %param.14, f32[256,64]{0,1:T(8,128)S(1)} %fusion.38, s32[]{:T(128)S(6)} %select_n.12), kind=kOutput, calls=%fused_computation.17 | convolution fusion | flops 50855936 | bytes 327684 | tf_op jit(solution)/shard_map/dot_general | solution.py:120
  6.2 1.1 %multiply_reduce_fusion = f32[8,8192]{1,0:T(8,128)S(1)} fusion(bf16[8,2,8192]{2,1,0:T(2,128)(2,1)} %param.8), kind=kLoop, calls=%fused_computation.42 | loop fusion | flops 327680 | bytes 524288 | tf_op jit(solution)/shard_map/reduce_sum | solution.py:149
  7.3 1.8 %reshape.86.refs_1_ = bf16[16,8192]{1,0:T(8,128)(2,1)} reshape(bf16[8,2,8192]{2,1,0:T(2,128)(2,1)} %param.8) | data formatting | bytes 524288 | tf_op jit(solution)/shard_map/reshape | solution.py:161
  9.6 1.1 %fusion.8 = f32[16,64]{1,0:T(8,128)S(1)} fusion(f32[16,8192]{1,0:T(8,128)S(1)} %fusion.26, s32[8192]{0:T(1024)S(1)} %copy-done.7), kind=kOutput, calls=%fused_computation.15 | convolution fusion | flops 101187584 | bytes 561152 | tf_op jit(solution)/shard_map/dot_general | solution.py:124
  11.6 2.0 %fusion.66 = (f32[16,8192]{1,0:T(8,128)S(1)}, f32[16,8192]{1,0:T(8,128)S(1)}) fusion(f32[16,8192]{1,0:T(8,128)S(1)} %copy-done.3), kind=kLoop, calls=%fused_computation.96 | loop fusion | bytes 1572864 | tf_op jit(solution)/shard_map/cos | solution.py:129
  13.7 1.3 %multiply_convert_fusion.3 = (bf16[8,16,1,8192]{3,1,2,0:T(8,128)(2,1)S(1)}, bf16[8,16,1,8192]{3,1,2,0:T(8,128)(2,1)S(1)}) fusion(f32[16,8192]{1,0:T(8,128)S(1)} %get-tuple-element.32, f32[8,8192]{1,0:T(8,128)S(1)} %get-tuple-element.30, f32[16,8192]{1,0:T(8,128)S(1)} %get-tuple-element.31, f32[8,8192]{1,0:T(8,128)S(1)} %get-tuple-element.29, ...), kind=kLoop, calls=%fused_computation.10 | loop fusion | flops 10485760 | bytes 6029312 | tf_op jit(solution)/shard_map/convert.3
  15.0 1.4 %fusion.67 = (f32[8]{0:T(128)S(1)}, f32[8,16,16]{2,1,0:T(8,128)S(1)}) fusion(f32[8,16]{1,0:T(8,128)S(1)} %convolution_multiply_fusion.1, f32[8192]{0:T(1024)S(1)} %bitcast.78, bf16[16,2,8192]{2,1,0:T(2,128)(2,1)S(1)} %copy-done.5, bf16[8,16,1,8192]{3,1,2,0:T(8,128)(2,1)S(1)} %get-tuple-element.24, bf16[8,16,1,8192]{3,1,2,0:T(8,128)(2,1)S(1)} %get-tuple-element.23, ...), kind=kOutput, calls=%fused_computation.97 | convolution fusion | flops 69998584 | bytes 4760224 | tf_op jit(solution)/shard_map/itpk,jpk->itj/dot_general | solution.py:133
  16.6 0.6 select_maximum_fusion.1.refs_0_
  17.2 17.6 %shard_map.111 = f32[16,8,128]{2,1,0:T(8,128)} custom-call(f32[8,128]{1,0:T(8,128)} %select_maximum_fusion.1.refs_0_), custom_call_target="tpu_custom_call" | custom-call | tf_op jit(solution)/shard_map/pallas_call | solution.py:74
  34.9 1.0 %slice_reduce_fusion.2 = (f32[8]{0:T(128)S(1)}, f32[16,1,8]{2,1,0:T(1,128)S(1)}, f32[16,1,8]{2,1,0:T(1,128)S(1)}) fusion(f32[16,8,128]{2,1,0:T(8,128)} %shard_map.111), kind=kLoop, calls=%fused_computation.93 | loop fusion | flops 120 | bytes 2080 | tf_op jit(solution)/shard_map/reduce_max | solution.py:142
  36.4 2.7 %fusion.11 = f32[8192]{0:T(1024)S(1)} fusion(bf16[8,16,1,8192]{3,1,2,0:T(8,128)(2,1)} %copy-done.2, bf16[8,16,1,8192]{3,1,2,0:T(8,128)(2,1)S(1)} %get-tuple-element.23, bf16[16,2,8192]{2,1,0:T(2,128)(2,1)S(1)} %copy-done.5, f32[8,16,16]{2,1,0:T(8,128)S(1)} %get-tuple-element.22), kind=kOutput, calls=%fused_computation.20 | convolution fusion | flops 76277760 | bytes 4759552 | tf_op jit(solution)/shard_map/itj,itpk->jpk/dot_general | solution.py:152
  39.4 1.1 %fusion.20 = f32[64]{0:T(128)S(1)} fusion(f32[8,8192]{1,0:T(8,128)S(1)} %multiply_reduce_fusion, s32[8192]{0:T(1024)S(1)} %copy-done.8, f32[8]{0:T(128)S(1)} %get-tuple-element.20), kind=kOutput, calls=%fused_computation.29 | convolution fusion | flops 50856896 | bytes 295200 | tf_op jit(solution)/shard_map/dot_general | solution.py:149
  40.5 1.1 %fusion.24 = f32[64]{0:T(128)S(1)} fusion(f32[64]{0:T(128)S(1)} %fusion.18, f32[64]{0:T(128)S(1)} %fusion.20, f32[8192,1]{0,1:T(1,128)S(1)} %bitcast.79, s32[8192]{0:T(1024)S(1)} %copy-done.8), kind=kOutput, calls=%fused_computation.33 | convolution fusion | flops 6815936 | bytes 66304 | tf_op jit(solution)/shard_map/dot_general | solution.py:153
  41.6 0.6 select_maximum_fusion.refs_0_
  42.2 29.1 %shard_map.112 = (f32[32,16,256]{2,1,0:T(8,128)}, bf16[32,16,256]{2,1,0:T(8,128)(2,1)}) custom-call(f32[16,256]{1,0:T(8,128)} %select_maximum_fusion.refs_0_, bf16[16,8192]{1,0:T(8,128)(2,1)} %reshape.86.refs_1_), custom_call_target="tpu_custom_call" | custom-call | tf_op jit(solution)/shard_map/pallas_call | solution.py:74
  71.4 1.0 %slice_reduce_fusion = f32[64]{0:T(128)S(1)} fusion(f32[32,16,256]{2,1,0:T(8,128)} %get-tuple-element.6), kind=kLoop, calls=%fused_computation.70 | loop fusion | flops 1984 | bytes 8448 | tf_op jit(solution)/shard_map/reduce_sum | solution.py:164
  72.4 1.0 %slice.31 = f32[32,8,256]{2,1,0:T(8,128)S(1)} slice(f32[32,16,256]{2,1,0:T(8,128)} %get-tuple-element.6), slice={[0:32], [0:8], [0:256]} | slice | bytes 524288 | tf_op jit(solution)/shard_map/slice | solution.py:163
  73.3 0.6 pad.19.refs_0_
  73.9 10.8 %shard_map.113 = f32[16,8,128]{2,1,0:T(8,128)} custom-call(f32[8,128]{1,0:T(8,128)} %pad.19.refs_0_), custom_call_target="tpu_custom_call" | custom-call | tf_op jit(solution)/shard_map/pallas_call | solution.py:74
  84.8 0.9 slice_reduce_fusion.1
  85.6 0.5 broadcast_multiply_fusion
  86.1 1.2 %reshape.88 = f32[256,2,256]{2,1,0:T(2,128)S(1)} reshape(bf16[32,16,256]{2,1,0:T(8,128)(2,1)} %get-tuple-element.7) | data formatting | bytes 786432 | tf_op jit(solution)/shard_map/convert_element_type | solution.py:176
  87.8 0.6 reshape.87
  88.5 0.5 reduce_sum.117
  88.9 0.8 copy.29
  89.7 1.0 %fusion.39 = f32[16,64]{1,0:T(8,128)} fusion(f32[256,16]{1,0:T(8,128)S(1)} %reduce_sum.117, f32[256,64]{0,1:T(8,128)S(1)} %fusion.38), kind=kOutput, calls=%fused_computation.54 | convolution fusion | flops 3162112 | bytes 86016 | tf_op jit(solution)/shard_map/dot_general | solution.py:169
  90.6 1.4 %multiply_convert_fusion.1 = (bf16[256,16,1,256]{3,0,1,2:T(8,128)(2,1)S(1)}, bf16[256,16,1,256]{3,0,1,2:T(8,128)(2,1)S(1)}) fusion(f32[16,256]{1,0:T(8,128)S(1)} %get-tuple-element.38, f32[256,256]{1,0:T(8,128)S(1)} %get-tuple-element.40, f32[16,256]{1,0:T(8,128)S(1)} %get-tuple-element.39, f32[256,256]{1,0:T(8,128)S(1)} %get-tuple-element.41, ...), kind=kLoop, calls=%fused_computation.8 | loop fusion | flops 10485760 | bytes 5013504 | tf_op jit(solution)/shard_map/convert.1
  92.0 0.8 fusion.15
  92.8 0.6 copy.30
  (39 shorter events, 3.1 us)
Async XLA Ops:
  0.6 2.9 %copy-start = (f32[64,64]{1,0:T(8,128)S(1)}, f32[64,64]{1,0:T(8,128)}, u32[]{:S(2)}) copy-start(f32[64,64]{1,0:T(8,128)} %param.13) | copy-start | bytes 49156
  0.6 8.7 %copy-start.4 = (bf16[16,2,8192]{2,1,0:T(2,128)(2,1)S(1)}, bf16[16,2,8192]{2,1,0:T(2,128)(2,1)}, u32[]{:S(2)}) copy-start(bf16[16,2,8192]{2,1,0:T(2,128)(2,1)} %param.9) | copy-start | bytes 1572868
  0.7 8.4 %copy-start.1 = (bf16[8,2,8192]{2,1,0:T(2,128)(2,1)S(1)}, bf16[8,2,8192]{2,1,0:T(2,128)(2,1)}, u32[]{:S(2)}) copy-start(bf16[8,2,8192]{2,1,0:T(2,128)(2,1)} %param.8) | copy-start | bytes 786436
  4.5 5.1 %copy-start.7 = (s32[8192]{0:T(1024)S(1)}, s32[8192]{0:T(1024)}, u32[]{:S(2)}) copy-start(s32[8192]{0:T(1024)} %param.14) | copy-start | bytes 98308
  7.3 3.4 %copy-start.9 = (f32[64]{0:T(128)S(1)}, f32[64]{0:T(128)}, u32[]{:S(2)}) copy-start(f32[64]{0:T(128)} %param.15) | copy-start | bytes 772
  9.1 2.5 %copy-start.3 = (f32[16,8192]{1,0:T(8,128)S(1)}, f32[16,8192]{1,0:T(8,128)}, u32[]{:S(2)}) copy-start(f32[16,8192]{1,0:T(8,128)} %param.10) | copy-start | bytes 1572868
  13.7 1.3 %copy-start.5 = (bf16[16,2,8192]{2,1,0:T(2,128)(2,1)S(1)}, bf16[16,2,8192]{2,1,0:T(2,128)(2,1)}, u32[]{:S(2)}) copy-start(bf16[16,2,8192]{2,1,0:T(2,128)(2,1)} %param.9) | copy-start | bytes 1572868
  13.7 1.3 %copy-start.10 = (f32[1,8192]{1,0:T(1,128)S(1)}, f32[1,8192]{1,0:T(1,128)}, u32[]{:S(2)}) copy-start(f32[1,8192]{1,0:T(1,128)} %fusion.9) | copy-start | bytes 98308
  15.0 1.4 %copy-start.2 = (bf16[8,16,1,8192]{3,1,2,0:T(8,128)(2,1)}, bf16[8,16,1,8192]{3,1,2,0:T(8,128)(2,1)S(1)}, u32[]{:S(2)}) copy-start(bf16[8,16,1,8192]{3,1,2,0:T(8,128)(2,1)S(1)} %get-tuple-element.24) | copy-start | bytes 6291460
  36.4 5.1 %copy-start.6 = (f32[8,16,16]{2,1,0:T(8,128)}, f32[8,16,16]{2,1,0:T(8,128)S(1)}, u32[]{:S(2)}) copy-start(f32[8,16,16]{2,1,0:T(8,128)S(1)} %get-tuple-element.22) | copy-start | bytes 24580
  36.4 3.0 %copy-start.8 = (s32[8192]{0:T(1024)S(1)}, s32[8192]{0:T(1024)}, u32[]{:S(2)}) copy-start(s32[8192]{0:T(1024)} %param.14) | copy-start | bytes 98308

commit v3 on v2

--- a/solution.py
+++ b/solution.py
@@ -153,20 +153,28 @@
     term_two = -2.0 * jnp.dot(jnp.sum(local_sums * refs_wide, axis=(0, 1)), shell_pick, precision=highest)
     terms = term_one + term_two + term_three
 
-    lanes = trans_count * ori_dev
-    post_rows = posterior.reshape(part_dev, lanes)
-    packed = jnp.concatenate([post_rows, jnp.pad(terms, (0, lanes - shells))[None]], axis=0)
-    packed = pad_rows(packed, lanes)
-    gathered, columns = exchange(
-        [(packed, None), (particles.reshape(part_dev * 2, pixels), width)], "dom", dom_size, 2
-    )
-    post_all = gathered[:, :part_dev, :].reshape(dom_size * part_dev, trans_count, ori_dev)
-    dom_terms = jnp.sum(gathered[:, part_dev, :shells], axis=0)
+    term_cols = -(-shells // part_dev)
+    term_rows = jnp.pad(terms, (0, term_cols * part_dev - shells)).reshape(part_dev, term_cols)
+    small = jnp.concatenate([weight_rows, term_rows], axis=1)
+    small = jnp.pad(small, ((0, 0), (0, -(-small.shape[1] // 128) * 128 - small.shape[1])))
+    half_rows = post_half.reshape(-1, 128)
+    half_all, small_all, columns = exchange(
+        [(half_rows, None), (small, None), (particles.reshape(part_dev * 2, pixels), width)],
+        "dom",
+        dom_size,
+        2,
+    )
+    post_all = half_all.reshape(dom_size * part_dev, trans_count, ori_dev)
+    weight_all = small_all[:, :, :ori_dev].reshape(dom_size * part_dev, ori_dev)
+    dom_terms = jnp.sum(
+        small_all[:, :, ori_dev : ori_dev + term_cols].reshape(dom_size, part_dev * term_cols)[:, :shells],
+        axis=0,
+    )
 
     (orient_terms,) = exchange([(pad_rows(dom_terms[None], 128), None)], "orient", orient_size, 3)
     shell_total = jnp.sum(orient_terms[:, 0, :shells], axis=0)
 
-    ctf_weights = jnp.dot(jnp.sum(post_all, axis=1).T, ctf_all * ctf_all, precision=highest)
+    ctf_weights = jnp.dot(weight_all.T, ctf_all * ctf_all, precision=highest)
 
     start_pix = dom_index * width
     pick_cols = lax.dynamic_slice_in_dim(shell_pick, start_pix, width, 0)
@@ -176,7 +184,7 @@
     col_planes = columns.reshape(dom_size * part_dev, 2, width).astype(jnp.float32)
     col_images = make_images(col_planes, ctf_cols, cos_cols, sin_cols)
     image_sums = jnp.einsum(
-        "itj,itpk->jpk", post_all.astype(jnp.bfloat16), col_images, preferred_element_type=jnp.float32
+        "itj,itpk->jpk", post_all, col_images, preferred_element_type=jnp.float32
     )
 
     divisor = part_dev * dom_size * pixels / shells

time: 94.2 us -> 93.3 us (level)
  Pallas kernels: 57.6 us -> 53.1 us
  local copies, waits for them, and re-layouts: 9.42 us -> 12.9 us
    pallas_call x3, Pallas kernels: 57.6 us -> 53.1 us  [exchange(): pl.pallas_call(functools.partial(_exchange_kernel, axis, n, widths), out_...]
    unnamed x24 -> x26, local copies, waits for them, and re-layouts: 0.75 us -> 3.46 us
    another operation x2, other arithmetic: 2.67 us -> 4.92 us
    reshape x3 -> x4, local copies, waits for them, and re-layouts: 1.48 us -> 3.35 us  [the longest x2 2.58 us: on_device(): post_all = half_all.reshape(dom_size * part_dev, trans_count, ori_dev)]
    dot_general x2, matrix products: 1.75 us -> 3.23 us  [the longest x1 2.28 us: on_device(): jnp.einsum('itj,itpk->jpk', post_all, col_images, preferred_element_type=...]
    dot_general x1, matrix products: 2.12 us -> 0.79 us  [on_device(): sigma_pix = jnp.dot(shell_pick, sigma2, precision=highest)]
    reduce_sum x2 -> x1, other arithmetic: 1.42 us -> 0.1 us  [on_device(): jnp.sum(small_all[:, :, ori_dev:ori_dev + term_cols].reshape(dom_size, pa...]
    reshape x1, local copies, waits for them, and re-layouts: 1.78 us -> 0.79 us  [on_device(): particles.reshape(part_dev * 2, pixels)]
where the time goes in v3:
time: 93.3 us; the launch traced here: 92.6 us
  Pallas kernels  53.1 us (57%)
  matrix products  14.7 us (16%)
  local copies, waits for them, and re-layouts  12.9 us (14%)
  other arithmetic  11 us (12%)
    pallas_call x3, Pallas kernels, exchange(): pl.pallas_call(functools.partial(_exchange_kernel, axis, n, widths), out_...  53.1 us
    another operation x2, other arithmetic  4.92 us
    unnamed x26, local copies, waits for them, and re-layouts  3.46 us
    cos x1, local copies, waits for them, and re-layouts, on_device(): cosines = jnp.cos(phases)  2.8 us
    dot_general x1, matrix products, on_device(): jnp.einsum('itj,itpk->jpk', post_half, images, preferred_element_type=jnp...  2.75 us
    reshape x2, local copies, waits for them, and re-layouts, on_device(): post_all = half_all.reshape(dom_size * part_dev, trans_count, ori_dev)  2.58 us
    dot_general x1, matrix products, on_device(): jnp.einsum('itj,itpk->jpk', post_all, col_images, preferred_element_type=...  2.28 us

profile of v3, /device:TPU:1, one launch (start us, length us, event | category | flops | bytes accessed | tf_op | source)
XLA Modules:
  0.0 92.6 jit_solution(3250826740282134969)
XLA Ops:
  0.7 0.7 copy-done
  1.4 1.0 %fusion.40 = f32[256,64]{0,1:T(8,128)S(1)} fusion(f32[64,64]{1,0:T(8,128)S(1)} %copy-done, s32[256]{0:T(256)} %param.12), kind=kOutput, calls=%fused_computation.56 | convolution fusion | flops 12599296 | bytes 82944 | tf_op jit(solution)/shard_map/dot_general | solution.py:118
  2.4 1.6 %fusion.10 = f32[8,8192]{1,0:T(8,128)S(1)} fusion(s32[8192]{0:T(1024)} %param.14, f32[256,64]{0,1:T(8,128)S(1)} %fusion.40, s32[]{:T(128)S(6)} %select_n.12), kind=kOutput, calls=%fused_computation.17 | convolution fusion | flops 50855936 | bytes 327684 | tf_op jit(solution)/shard_map/dot_general | solution.py:120
  3.9 2.8 %fusion.66 = (f32[16,8192]{1,0:T(8,128)S(1)}, f32[16,8192]{1,0:T(8,128)S(1)}) fusion(f32[16,8192]{1,0:T(8,128)} %param.10), kind=kLoop, calls=%fused_computation.96 | loop fusion | bytes 1572864 | tf_op jit(solution)/shard_map/cos | solution.py:129
  7.0 1.3 %multiply_convert_fusion.3 = (bf16[8,16,1,8192]{3,1,2,0:T(8,128)(2,1)S(1)}, bf16[8,16,1,8192]{3,1,2,0:T(8,128)(2,1)S(1)}) fusion(f32[16,8192]{1,0:T(8,128)S(1)} %get-tuple-element.34, f32[8,8192]{1,0:T(8,128)S(1)} %get-tuple-element.32, f32[16,8192]{1,0:T(8,128)S(1)} %get-tuple-element.33, f32[8,8192]{1,0:T(8,128)S(1)} %get-tuple-element.31, ...), kind=kLoop, calls=%fused_computation.10 | loop fusion | flops 10485760 | bytes 6029312 | tf_op jit(solution)/shard_map/convert.3
  8.6 1.1 %fusion.8 = f32[16,64]{1,0:T(8,128)S(1)} fusion(f32[16,8192]{1,0:T(8,128)S(1)} %fusion.26, s32[8192]{0:T(1024)S(1)} %copy-done.7), kind=kOutput, calls=%fused_computation.15 | convolution fusion | flops 101187584 | bytes 561152 | tf_op jit(solution)/shard_map/dot_general | solution.py:124
  10.0 0.8 fusion.9
  10.8 1.4 %fusion.67 = (f32[8]{0:T(128)S(1)}, f32[8,16,16]{2,1,0:T(8,128)S(1)}) fusion(f32[8,16]{1,0:T(8,128)S(1)} %convolution_multiply_fusion.1, f32[8192]{0:T(1024)S(1)} %bitcast.77, bf16[16,2,8192]{2,1,0:T(2,128)(2,1)S(1)} %copy-done.3, bf16[8,16,1,8192]{3,1,2,0:T(8,128)(2,1)S(1)} %get-tuple-element.26, bf16[8,16,1,8192]{3,1,2,0:T(8,128)(2,1)S(1)} %get-tuple-element.25, ...), kind=kOutput, calls=%fused_computation.97 | convolution fusion | flops 69998584 | bytes 4760224 | tf_op jit(solution)/shard_map/itpk,jpk->itj/dot_general | solution.py:133
  12.2 0.6 copy-done.6
  13.0 0.6 select_maximum_fusion.1.refs_0_
  13.6 17.6 %shard_map.111 = f32[16,8,128]{2,1,0:T(8,128)} custom-call(f32[8,128]{1,0:T(8,128)} %select_maximum_fusion.1.refs_0_), custom_call_target="tpu_custom_call" | custom-call | tf_op jit(solution)/shard_map/pallas_call | solution.py:74
  31.3 1.0 %slice_reduce_fusion.2 = (f32[8]{0:T(128)S(1)}, f32[16,1,8]{2,1,0:T(1,128)S(1)}, f32[16,1,8]{2,1,0:T(1,128)S(1)}) fusion(f32[16,8,128]{2,1,0:T(8,128)} %shard_map.111), kind=kLoop, calls=%fused_computation.93 | loop fusion | flops 120 | bytes 2080 | tf_op jit(solution)/shard_map/reduce_max | solution.py:142
  32.5 1.1 %fusion.64 = (f32[8]{0:T(128)S(1)}, f32[8,16]{1,0:T(8,128)S(1)}, f32[8,16,16]{2,1,0:T(8,128)S(1)}) fusion(f32[8]{0:T(128)S(1)} %fusion.54, f32[8,16,16]{2,1,0:T(8,128)} %copy-done.6, f32[8]{0:T(128)S(1)} %get-tuple-element.35), kind=kLoop, calls=%fused_computation.94 | loop fusion | flops 8056 | bytes 16992 | tf_op jit(solution)/shard_map/reduce_sum | solution.py:150
  33.6 0.6 copy-done.5
  34.3 2.8 %fusion.11 = f32[8192]{0:T(1024)S(1)} fusion(bf16[8,16,1,8192]{3,1,2,0:T(8,128)(2,1)} %copy-done.2, bf16[8,16,1,8192]{3,1,2,0:T(8,128)(2,1)S(1)} %get-tuple-element.25, bf16[16,2,8192]{2,1,0:T(2,128)(2,1)} %param.9, bf16[8,16,16]{2,1,0:T(8,128)(2,1)S(1)} %convert_element_type.31), kind=kOutput, calls=%fused_computation.20 | convolution fusion | flops 76275712 | bytes 4755456 | tf_op jit(solution)/shard_map/itj,itpk->jpk/dot_general | solution.py:152
  37.2 1.1 %fusion.20 = f32[64]{0:T(128)S(1)} fusion(f32[8,8192]{1,0:T(8,128)S(1)} %multiply_reduce_fusion, s32[8192]{0:T(1024)S(1)} %copy-done.8, f32[8]{0:T(128)S(1)} %get-tuple-element.22), kind=kOutput, calls=%fused_computation.29 | convolution fusion | flops 50856896 | bytes 295200 | tf_op jit(solution)/shard_map/dot_general | solution.py:149
  38.5 1.0 %fusion.24 = f32[64]{0:T(128)S(1)} fusion(f32[64]{0:T(128)S(1)} %fusion.18, f32[64]{0:T(128)S(1)} %fusion.20, f32[8192,1]{0,1:T(1,128)S(1)} %bitcast.76, s32[8192]{0:T(1024)S(1)} %copy-done.8), kind=kOutput, calls=%fused_computation.33 | convolution fusion | flops 6815936 | bytes 66304 | tf_op jit(solution)/shard_map/dot_general | solution.py:153
  39.7 0.7 select_maximum_fusion.refs_1_
  40.4 0.7 reshape.94.refs_0_
  41.0 0.8 reshape.96.refs_2_
  41.8 24.1 %shard_map.112 = (bf16[32,16,128]{2,1,0:T(8,128)(2,1)}, f32[32,8,128]{2,1,0:T(8,128)}, bf16[32,16,256]{2,1,0:T(8,128)(2,1)}) custom-call(bf16[16,128]{1,0:T(8,128)(2,1)} %reshape.94.refs_0_, f32[8,128]{1,0:T(8,128)} %select_maximum_fusion.refs_1_, bf16[16,8192]{1,0:T(8,128)(2,1)} %reshape.96.refs_2_), custom_call_target="tpu_custom_call" | custom-call | tf_op jit(solution)/shard_map/pallas_call | solution.py:74
  65.9 1.2 %reshape.99 = f32[256,2,256]{2,1,0:T(2,128)S(1)} reshape(bf16[32,16,256]{2,1,0:T(8,128)(2,1)} %get-tuple-element.8) | data formatting | bytes 786432 | tf_op jit(solution)/shard_map/convert_element_type | solution.py:184
  67.5 0.8 copy_bitcast_fusion
  68.9 3.7 %multiply_convert_fusion.1 = (bf16[256,16,1,256]{3,0,1,2:T(8,128)(2,1)S(1)}, bf16[256,16,1,256]{3,0,1,2:T(8,128)(2,1)}) fusion(f32[16,256]{1,0:T(8,128)S(1)} %get-tuple-element.40, f32[256,256]{1,0:T(8,128)S(1)} %get-tuple-element.42, f32[16,256]{1,0:T(8,128)S(1)} %get-tuple-element.41, f32[256,256]{1,0:T(8,128)} %get-tuple-element.43, f32[256,256]{1,0:T(8,128)S(1)} %fusion.43), kind=kLoop, calls=%fused_computation.8 | loop fusion | flops 10485760 | bytes 5013504 | tf_op jit(solution)/shard_map/convert.1
  72.5 1.7 %reshape.97 = bf16[256,16,16]{2,1,0:T(8,128)(2,1)S(1)} reshape(bf16[32,16,128]{2,1,0:T(8,128)(2,1)} %get-tuple-element.7) | data formatting | bytes 262144 | tf_op jit(solution)/shard_map/reshape | solution.py:167
  74.3 0.8 copy.29
  75.1 2.3 %fusion.15 = f32[16,2,256]{2,0,1:T(8,128)S(1)} fusion(bf16[256,16,1,256]{3,0,1,2:T(8,128)(2,1)} %get-tuple-element.28, bf16[256,16,1,256]{3,0,1,2:T(8,128)(2,1)S(1)} %get-tuple-element.27, bf16[256,16,16]{0,2,1:T(8,128)(2,1)S(1)} %copy.29), kind=kOutput, calls=%fused_computation.24 | convolution fusion | flops 75497472 | bytes 4358144 | tf_op jit(solution)/shard_map/itj,itpk->jpk/dot_general | solution.py:186
  77.4 0.6 copy.30
  78.2 0.6 pad.14.refs_0_
  78.9 11.4 %shard_map.113 = f32[16,8,128]{2,1,0:T(8,128)} custom-call(f32[8,128]{1,0:T(8,128)} %pad.14.refs_0_), custom_call_target="tpu_custom_call" | custom-call | tf_op jit(solution)/shard_map/pallas_call | solution.py:74
  90.3 0.9 slice_reduce_fusion.1
  91.7 1.0 %fusion.36 = f32[16,64]{1,0:T(8,128)} fusion(f32[32,8,128]{2,1,0:T(8,128)S(1)} %copy-done.4, f32[256,64]{0,1:T(8,128)S(1)} %fusion.40), kind=kOutput, calls=%fused_computation.50 | convolution fusion | flops 3162112 | bytes 200704 | tf_op jit(solution)/shard_map/dot_general | solution.py:177
  (41 shorter events, 3.6 us)
Async XLA Ops:
  0.6 0.8 copy-start
  0.6 6.1 %copy-start.1 = (bf16[8,2,8192]{2,1,0:T(2,128)(2,1)S(1)}, bf16[8,2,8192]{2,1,0:T(2,128)(2,1)}, u32[]{:S(2)}) copy-start(bf16[8,2,8192]{2,1,0:T(2,128)(2,1)} %param.8) | copy-start | bytes 786436
  6.9 1.3 %copy-start.3 = (bf16[16,2,8192]{2,1,0:T(2,128)(2,1)S(1)}, bf16[16,2,8192]{2,1,0:T(2,128)(2,1)}, u32[]{:S(2)}) copy-start(bf16[16,2,8192]{2,1,0:T(2,128)(2,1)} %param.9) | copy-start | bytes 1572868
  7.0 1.6 %copy-start.7 = (s32[8192]{0:T(1024)S(1)}, s32[8192]{0:T(1024)}, u32[]{:S(2)}) copy-start(s32[8192]{0:T(1024)} %param.14) | copy-start | bytes 98308
  7.0 2.7 %copy-start.11 = (f32[64]{0:T(128)S(1)}, f32[64]{0:T(128)}, u32[]{:S(2)}) copy-start(f32[64]{0:T(128)} %param.15) | copy-start | bytes 772
  8.3 3.9 %copy-start.2 = (bf16[8,16,1,8192]{3,1,2,0:T(8,128)(2,1)}, bf16[8,16,1,8192]{3,1,2,0:T(8,128)(2,1)S(1)}, u32[]{:S(2)}) copy-start(bf16[8,16,1,8192]{3,1,2,0:T(8,128)(2,1)S(1)} %get-tuple-element.26) | copy-start | bytes 6291460
  8.3 2.5 %copy-start.10 = (s32[8,16]{1,0:T(8,128)S(1)}, s32[8,16]{1,0:T(8,128)}, u32[]{:S(2)}) copy-start(s32[8,16]{1,0:T(8,128)} %param.11) | copy-start | bytes 1540
  12.2 0.6 copy-start.6
  33.6 0.6 copy-start.5
  34.2 2.9 %copy-start.8 = (s32[8192]{0:T(1024)S(1)}, s32[8192]{0:T(1024)}, u32[]{:S(2)}) copy-start(s32[8192]{0:T(1024)} %param.14) | copy-start | bytes 98308
  38.5 29.8 %copy-start.9 = (s32[8192]{0:T(1024)S(1)}, s32[8192]{0:T(1024)}, u32[]{:S(2)}) copy-start(s32[8192]{0:T(1024)} %param.14) | copy-start | bytes 98308
  75.1 2.9 %copy-start.4 = (f32[32,8,128]{2,1,0:T(8,128)S(1)}, f32[32,8,128]{2,1,0:T(8,128)}, u32[]{:S(2)}) copy-start(f32[32,8,128]{2,1,0:T(8,128)} %get-tuple-element.9) | copy-start | bytes 393220

commit v4 on v3

--- a/solution.py
+++ b/solution.py
@@ -82,6 +82,123 @@
     )(*[x for x, _ in payloads])
 
 
+def _spread_kernel(dom_n, orient_n, width, half_ref, small_ref, part_ref,
+                   half_out, small_out, part_out, terms_out,
+                   half_held, small_held, part_held, summed, terms_held,
+                   send_sem, recv_sem, orient_send, orient_recv):
+    me = lax.axis_index("dom")
+    mine = lax.axis_index("orient")
+    barrier = pltpu.get_barrier_semaphore()
+
+    def greet_dom(k, carry):
+        peer = lax.rem(me + k, dom_n)
+        pl.semaphore_signal(barrier, inc=1, device_id={"dom": peer}, device_id_type=MESH_ID)
+        return carry
+
+    def greet_orient(k, carry):
+        peer = lax.rem(mine + k, orient_n)
+        pl.semaphore_signal(barrier, inc=1, device_id={"orient": peer}, device_id_type=MESH_ID)
+        return carry
+
+    lax.fori_loop(1, dom_n, greet_dom, 0)
+    lax.fori_loop(1, orient_n, greet_orient, 0)
+    pl.semaphore_wait(barrier, dom_n + orient_n - 2)
+
+    def columns(peer):
+        return part_ref.at[:, pl.ds(pl.multiple_of(peer * width, width), width)]
+
+    sources = (lambda peer: half_ref, lambda peer: small_ref, columns)
+    held = (half_held, small_held, part_held)
+
+    def copy(index, k):
+        peer = lax.rem(me + k, dom_n)
+        return pltpu.make_async_remote_copy(
+            src_ref=sources[index](peer),
+            dst_ref=held[index].at[me],
+            send_sem=send_sem.at[index, k],
+            recv_sem=recv_sem.at[index, k],
+            device_id={"dom": peer},
+            device_id_type=MESH_ID,
+        )
+
+    def start(k, carry):
+        for index in (1, 0, 2):
+            copy(index, k).start()
+        return carry
+
+    lax.fori_loop(1, dom_n, start, 0)
+    for index in range(3):
+        held[index][me] = sources[index](me)[...]
+
+    def finish(index):
+        def body(k, carry):
+            copy(index, k).wait()
+            return carry
+
+        lax.fori_loop(1, dom_n, body, 0)
+
+    finish(1)
+    summed[...] = jnp.sum(small_held[...], axis=0)
+    finish(0)
+
+    def orient_copy(k):
+        peer = lax.rem(mine + k, orient_n)
+        return pltpu.make_async_remote_copy(
+            src_ref=summed,
+            dst_ref=terms_held.at[mine],
+            send_sem=orient_send.at[k],
+            recv_sem=orient_recv.at[k],
+            device_id={"orient": peer},
+            device_id_type=MESH_ID,
+        )
+
+    def orient_start(k, carry):
+        orient_copy(k).start()
+        return carry
+
+    lax.fori_loop(1, orient_n, orient_start, 0)
+    terms_held[mine] = summed[...]
+    finish(2)
+
+    def orient_finish(k, carry):
+        orient_copy(k).wait()
+        return carry
+
+    lax.fori_loop(1, orient_n, orient_finish, 0)
+    half_out[...] = half_held[...]
+    small_out[...] = small_held[...]
+    part_out[...] = part_held[...]
+    terms_out[...] = terms_held[...]
+
+
+def spread(half_rows, small, part_rows, dom_n, orient_n, width, collective_id):
+    shapes = (
+        jax.ShapeDtypeStruct((dom_n,) + half_rows.shape, half_rows.dtype),
+        jax.ShapeDtypeStruct((dom_n,) + small.shape, small.dtype),
+        jax.ShapeDtypeStruct((dom_n, part_rows.shape[0], width), part_rows.dtype),
+        jax.ShapeDtypeStruct((orient_n,) + small.shape, small.dtype),
+    )
+    vmem = pl.BlockSpec(memory_space=pltpu.VMEM)
+    return pl.pallas_call(
+        functools.partial(_spread_kernel, dom_n, orient_n, width),
+        out_shape=shapes,
+        in_specs=[vmem] * 3,
+        out_specs=(vmem,) * 4,
+        scratch_shapes=[
+            pltpu.VMEM(shapes[0].shape, shapes[0].dtype),
+            pltpu.VMEM(shapes[1].shape, shapes[1].dtype),
+            pltpu.VMEM(shapes[2].shape, shapes[2].dtype),
+            pltpu.VMEM(small.shape, small.dtype),
+            pltpu.VMEM(shapes[3].shape, shapes[3].dtype),
+            pltpu.SemaphoreType.DMA((3, dom_n)),
+            pltpu.SemaphoreType.DMA((3, dom_n)),
+            pltpu.SemaphoreType.DMA((orient_n,)),
+            pltpu.SemaphoreType.DMA((orient_n,)),
+        ],
+        compiler_params=pltpu.CompilerParams(collective_id=collective_id, has_side_effects=True),
+    )(half_rows, small, part_rows)
+
+
 def make_images(planes, ctf_pix, cosine, sine_part):
     real_part = planes[:, 0][:, None, :]
     imag_part = planes[:, 1][:, None, :]
@@ -158,21 +275,15 @@
     small = jnp.concatenate([weight_rows, term_rows], axis=1)
     small = jnp.pad(small, ((0, 0), (0, -(-small.shape[1] // 128) * 128 - small.shape[1])))
     half_rows = post_half.reshape(-1, 128)
-    half_all, small_all, columns = exchange(
-        [(half_rows, None), (small, None), (particles.reshape(part_dev * 2, pixels), width)],
-        "dom",
-        dom_size,
-        2,
+    half_all, small_all, columns, orient_small = spread(
+        half_rows, small, particles.reshape(part_dev * 2, pixels), dom_size, orient_size, width, 2
     )
     post_all = half_all.reshape(dom_size * part_dev, trans_count, ori_dev)
     weight_all = small_all[:, :, :ori_dev].reshape(dom_size * part_dev, ori_dev)
-    dom_terms = jnp.sum(
-        small_all[:, :, ori_dev : ori_dev + term_cols].reshape(dom_size, part_dev * term_cols)[:, :shells],
+    shell_total = jnp.sum(
+        orient_small[:, :, ori_dev : ori_dev + term_cols].reshape(orient_size, part_dev * term_cols)[:, :shells],
         axis=0,
     )
-
-    (orient_terms,) = exchange([(pad_rows(dom_terms[None], 128), None)], "orient", orient_size, 3)
-    shell_total = jnp.sum(orient_terms[:, 0, :shells], axis=0)
 
     ctf_weights = jnp.dot(weight_all.T, ctf_all * ctf_all, precision=highest)
 

time: 93.3 us -> 88.5 us (0.949)
  Pallas kernels: 53.1 us -> 50 us
  other arithmetic: 11 us -> 9.63 us
    pallas_call x3 -> x1, Pallas kernels: 53.1 us -> 17.6 us  [exchange(): pl.pallas_call(functools.partial(_exchange_kernel, axis, n, widths), out_...]
    pallas_call x0 -> x1, Pallas kernels: none -> 32.3 us  [spread(): pl.pallas_call(functools.partial(_spread_kernel, dom_n, orient_n, width),...]
    unnamed x26 -> x28, local copies, waits for them, and re-layouts: 3.46 us -> 3.47 us
where the time goes in v4:
time: 88.5 us; the launch traced here: 88 us
  Pallas kernels  50 us (56%)
  matrix products  14.7 us (17%)
  local copies, waits for them, and re-layouts  12.8 us (14%)
  other arithmetic  9.63 us (11%)
  between operations  0.89 us (1%)
    pallas_call x1, Pallas kernels, spread(): pl.pallas_call(functools.partial(_spread_kernel, dom_n, orient_n, width),...  32.3 us
    pallas_call x1, Pallas kernels, exchange(): pl.pallas_call(functools.partial(_exchange_kernel, axis, n, widths), out_...  17.6 us
    another operation x2, other arithmetic  4.92 us
    unnamed x28, local copies, waits for them, and re-layouts  3.47 us
    cos x1, local copies, waits for them, and re-layouts, on_device(): cosines = jnp.cos(phases)  2.8 us
    dot_general x1, matrix products, on_device(): jnp.einsum('itj,itpk->jpk', post_half, images, preferred_element_type=jnp...  2.75 us
    reshape x2, local copies, waits for them, and re-layouts, on_device(): post_all = half_all.reshape(dom_size * part_dev, trans_count, ori_dev)  2.58 us
    dot_general x1, matrix products, on_device(): jnp.einsum('itj,itpk->jpk', post_all, col_images, preferred_element_type=...  2.28 us

profile of v4, /device:TPU:1, one launch (start us, length us, event | category | flops | bytes accessed | tf_op | source)
XLA Modules:
  0.0 88.0 jit_solution(3362426738313184456)
XLA Ops:
  0.7 0.7 copy-done
  1.4 1.0 %fusion.40 = f32[256,64]{0,1:T(8,128)S(1)} fusion(f32[64,64]{1,0:T(8,128)S(1)} %copy-done, s32[256]{0:T(256)} %param.12), kind=kOutput, calls=%fused_computation.55 | convolution fusion | flops 12599296 | bytes 82944 | tf_op jit(solution)/shard_map/dot_general | solution.py:235
  2.4 1.6 %fusion.10 = f32[8,8192]{1,0:T(8,128)S(1)} fusion(s32[8192]{0:T(1024)} %param.14, f32[256,64]{0,1:T(8,128)S(1)} %fusion.40, s32[]{:T(128)S(6)} %select_n.12), kind=kOutput, calls=%fused_computation.17 | convolution fusion | flops 50855936 | bytes 327684 | tf_op jit(solution)/shard_map/dot_general | solution.py:237
  3.9 2.8 %fusion.66 = (f32[16,8192]{1,0:T(8,128)S(1)}, f32[16,8192]{1,0:T(8,128)S(1)}) fusion(f32[16,8192]{1,0:T(8,128)} %param.10), kind=kLoop, calls=%fused_computation.95 | loop fusion | bytes 1572864 | tf_op jit(solution)/shard_map/cos | solution.py:246
  7.0 1.3 %multiply_convert_fusion.3 = (bf16[8,16,1,8192]{3,1,2,0:T(8,128)(2,1)S(1)}, bf16[8,16,1,8192]{3,1,2,0:T(8,128)(2,1)S(1)}) fusion(f32[16,8192]{1,0:T(8,128)S(1)} %get-tuple-element.36, f32[8,8192]{1,0:T(8,128)S(1)} %get-tuple-element.34, f32[16,8192]{1,0:T(8,128)S(1)} %get-tuple-element.35, f32[8,8192]{1,0:T(8,128)S(1)} %get-tuple-element.33, ...), kind=kLoop, calls=%fused_computation.10 | loop fusion | flops 10485760 | bytes 6029312 | tf_op jit(solution)/shard_map/convert.3
  8.6 1.1 %fusion.8 = f32[16,64]{1,0:T(8,128)S(1)} fusion(f32[16,8192]{1,0:T(8,128)S(1)} %fusion.26, s32[8192]{0:T(1024)S(1)} %copy-done.8), kind=kOutput, calls=%fused_computation.15 | convolution fusion | flops 101187584 | bytes 561152 | tf_op jit(solution)/shard_map/dot_general | solution.py:241
  10.0 0.8 fusion.9
  10.8 1.4 %fusion.67 = (f32[8]{0:T(128)S(1)}, f32[8,16,16]{2,1,0:T(8,128)S(1)}) fusion(f32[8,16]{1,0:T(8,128)S(1)} %convolution_multiply_fusion.1, f32[8192]{0:T(1024)S(1)} %bitcast.77, bf16[16,2,8192]{2,1,0:T(2,128)(2,1)S(1)} %copy-done.3, bf16[8,16,1,8192]{3,1,2,0:T(8,128)(2,1)S(1)} %get-tuple-element.28, bf16[8,16,1,8192]{3,1,2,0:T(8,128)(2,1)S(1)} %get-tuple-element.27, ...), kind=kOutput, calls=%fused_computation.96 | convolution fusion | flops 69998584 | bytes 4760224 | tf_op jit(solution)/shard_map/itpk,jpk->itj/dot_general | solution.py:250
  12.2 0.6 copy-done.5
  13.0 0.6 select_maximum_fusion.1.refs_0_
  13.6 17.6 %shard_map.111 = f32[16,8,128]{2,1,0:T(8,128)} custom-call(f32[8,128]{1,0:T(8,128)} %select_maximum_fusion.1.refs_0_), custom_call_target="tpu_custom_call" | custom-call | tf_op jit(solution)/shard_map/pallas_call | solution.py:74
  31.3 1.0 %slice_reduce_fusion.1 = (f32[8]{0:T(128)S(1)}, f32[16,1,8]{2,1,0:T(1,128)S(1)}, f32[16,1,8]{2,1,0:T(1,128)S(1)}) fusion(f32[16,8,128]{2,1,0:T(8,128)} %shard_map.111), kind=kLoop, calls=%fused_computation.92 | loop fusion | flops 120 | bytes 2080 | tf_op jit(solution)/shard_map/reduce_max | solution.py:259
  32.5 1.1 %fusion.64 = (f32[8]{0:T(128)S(1)}, f32[8,16]{1,0:T(8,128)S(1)}, f32[8,16,16]{2,1,0:T(8,128)S(1)}) fusion(f32[8]{0:T(128)S(1)} %fusion.54, f32[8,16,16]{2,1,0:T(8,128)} %copy-done.5, f32[8]{0:T(128)S(1)} %get-tuple-element.37), kind=kLoop, calls=%fused_computation.93 | loop fusion | flops 8056 | bytes 16992 | tf_op jit(solution)/shard_map/reduce_sum | solution.py:267
  33.6 0.6 copy-done.4
  34.3 2.8 %fusion.11 = f32[8192]{0:T(1024)S(1)} fusion(bf16[8,16,1,8192]{3,1,2,0:T(8,128)(2,1)} %copy-done.2, bf16[8,16,1,8192]{3,1,2,0:T(8,128)(2,1)S(1)} %get-tuple-element.27, bf16[16,2,8192]{2,1,0:T(2,128)(2,1)} %param.9, bf16[8,16,16]{2,1,0:T(8,128)(2,1)S(1)} %convert_element_type.29), kind=kOutput, calls=%fused_computation.20 | convolution fusion | flops 76275712 | bytes 4755456 | tf_op jit(solution)/shard_map/itj,itpk->jpk/dot_general | solution.py:269
  37.2 1.1 %fusion.20 = f32[64]{0:T(128)S(1)} fusion(f32[8,8192]{1,0:T(8,128)S(1)} %multiply_reduce_fusion, s32[8192]{0:T(1024)S(1)} %copy-done.9, f32[8]{0:T(128)S(1)} %get-tuple-element.24), kind=kOutput, calls=%fused_computation.29 | convolution fusion | flops 50856896 | bytes 295200 | tf_op jit(solution)/shard_map/dot_general | solution.py:266
  38.5 1.0 %fusion.24 = f32[64]{0:T(128)S(1)} fusion(f32[64]{0:T(128)S(1)} %fusion.18, f32[64]{0:T(128)S(1)} %fusion.20, f32[8192,1]{0,1:T(1,128)S(1)} %bitcast.76, s32[8192]{0:T(1024)S(1)} %copy-done.9), kind=kOutput, calls=%fused_computation.33 | convolution fusion | flops 6815936 | bytes 66304 | tf_op jit(solution)/shard_map/dot_general | solution.py:270
  39.7 0.7 select_maximum_fusion.small_ref
  40.4 0.7 reshape.95.half_ref
  41.0 0.8 reshape.97.part_ref
  41.8 32.3 %shard_map.112 = (bf16[32,16,128]{2,1,0:T(8,128)(2,1)}, f32[32,8,128]{2,1,0:T(8,128)}, bf16[32,16,256]{2,1,0:T(8,128)(2,1)}, f32[16,8,128]{2,1,0:T(8,128)}) custom-call(bf16[16,128]{1,0:T(8,128)(2,1)} %reshape.95.half_ref, f32[8,128]{1,0:T(8,128)} %select_maximum_fusion.small_ref, bf16[16,8192]{1,0:T(8,128)(2,1)} %reshape.97.part_ref), custom_call_target="tpu_custom_call" | custom-call | tf_op jit(solution)/shard_map/pallas_call | solution.py:182
  74.2 1.2 %reshape.100 = f32[256,2,256]{2,1,0:T(2,128)S(1)} reshape(bf16[32,16,256]{2,1,0:T(8,128)(2,1)} %get-tuple-element.9) | data formatting | bytes 786432 | tf_op jit(solution)/shard_map/convert_element_type | solution.py:295
  75.4 0.4 fusion.65
  75.8 0.8 copy_bitcast_fusion
  76.8 0.3 fusion.43
  77.2 3.7 %multiply_convert_fusion.1 = (bf16[256,16,1,256]{3,0,1,2:T(8,128)(2,1)S(1)}, bf16[256,16,1,256]{3,0,1,2:T(8,128)(2,1)}) fusion(f32[16,256]{1,0:T(8,128)S(1)} %get-tuple-element.42, f32[256,256]{1,0:T(8,128)S(1)} %get-tuple-element.44, f32[16,256]{1,0:T(8,128)S(1)} %get-tuple-element.43, f32[256,256]{1,0:T(8,128)} %get-tuple-element.45, f32[256,256]{1,0:T(8,128)S(1)} %fusion.43), kind=kLoop, calls=%fused_computation.8 | loop fusion | flops 10485760 | bytes 5013504 | tf_op jit(solution)/shard_map/convert.1
  80.8 1.7 %reshape.98 = bf16[256,16,16]{2,1,0:T(8,128)(2,1)S(1)} reshape(bf16[32,16,128]{2,1,0:T(8,128)(2,1)} %get-tuple-element.8) | data formatting | bytes 262144 | tf_op jit(solution)/shard_map/reshape | solution.py:281
  82.6 0.8 copy.29
  83.4 2.3 %fusion.15 = f32[16,2,256]{2,0,1:T(8,128)S(1)} fusion(bf16[256,16,1,256]{3,0,1,2:T(8,128)(2,1)} %get-tuple-element.30, bf16[256,16,1,256]{3,0,1,2:T(8,128)(2,1)S(1)} %get-tuple-element.29, bf16[256,16,16]{0,2,1:T(8,128)(2,1)S(1)} %copy.29), kind=kOutput, calls=%fused_computation.24 | convolution fusion | flops 75497472 | bytes 4358144 | tf_op jit(solution)/shard_map/itj,itpk->jpk/dot_general | solution.py:297
  85.7 0.6 copy.30
  86.3 1.0 %fusion.36 = f32[16,64]{1,0:T(8,128)} fusion(f32[32,8,128]{2,1,0:T(8,128)S(1)} %copy-done.6, f32[256,64]{0,1:T(8,128)S(1)} %fusion.40), kind=kOutput, calls=%fused_computation.50 | convolution fusion | flops 3162112 | bytes 200704 | tf_op jit(solution)/shard_map/dot_general | solution.py:288
  87.4 0.6 div.40
  (40 shorter events, 2.3 us)
Async XLA Ops:
  0.6 0.8 copy-start
  0.6 6.1 %copy-start.1 = (bf16[8,2,8192]{2,1,0:T(2,128)(2,1)S(1)}, bf16[8,2,8192]{2,1,0:T(2,128)(2,1)}, u32[]{:S(2)}) copy-start(bf16[8,2,8192]{2,1,0:T(2,128)(2,1)} %param.8) | copy-start | bytes 786436
  6.9 1.3 %copy-start.3 = (bf16[16,2,8192]{2,1,0:T(2,128)(2,1)S(1)}, bf16[16,2,8192]{2,1,0:T(2,128)(2,1)}, u32[]{:S(2)}) copy-start(bf16[16,2,8192]{2,1,0:T(2,128)(2,1)} %param.9) | copy-start | bytes 1572868
  7.0 1.6 %copy-start.8 = (s32[8192]{0:T(1024)S(1)}, s32[8192]{0:T(1024)}, u32[]{:S(2)}) copy-start(s32[8192]{0:T(1024)} %param.14) | copy-start | bytes 98308
  7.0 2.7 %copy-start.12 = (f32[64]{0:T(128)S(1)}, f32[64]{0:T(128)}, u32[]{:S(2)}) copy-start(f32[64]{0:T(128)} %param.15) | copy-start | bytes 772
  8.3 3.9 %copy-start.2 = (bf16[8,16,1,8192]{3,1,2,0:T(8,128)(2,1)}, bf16[8,16,1,8192]{3,1,2,0:T(8,128)(2,1)S(1)}, u32[]{:S(2)}) copy-start(bf16[8,16,1,8192]{3,1,2,0:T(8,128)(2,1)S(1)} %get-tuple-element.28) | copy-start | bytes 6291460
  8.3 2.5 %copy-start.11 = (s32[8,16]{1,0:T(8,128)S(1)}, s32[8,16]{1,0:T(8,128)}, u32[]{:S(2)}) copy-start(s32[8,16]{1,0:T(8,128)} %param.11) | copy-start | bytes 1540
  12.2 0.6 copy-start.5
  33.6 0.6 copy-start.4
  34.2 2.9 %copy-start.9 = (s32[8192]{0:T(1024)S(1)}, s32[8192]{0:T(1024)}, u32[]{:S(2)}) copy-start(s32[8192]{0:T(1024)} %param.14) | copy-start | bytes 98308
  38.5 38.0 %copy-start.10 = (s32[8192]{0:T(1024)S(1)}, s32[8192]{0:T(1024)}, u32[]{:S(2)}) copy-start(s32[8192]{0:T(1024)} %param.14) | copy-start | bytes 98308
  83.4 2.9 %copy-start.6 = (f32[32,8,128]{2,1,0:T(8,128)S(1)}, f32[32,8,128]{2,1,0:T(8,128)}, u32[]{:S(2)}) copy-start(f32[32,8,128]{2,1,0:T(8,128)} %get-tuple-element.10) | copy-start | bytes 393220
  83.4 3.9 %copy-start.7 = (f32[16,8,128]{2,1,0:T(8,128)S(1)}, f32[16,8,128]{2,1,0:T(8,128)}, u32[]{:S(2)}) copy-start(f32[16,8,128]{2,1,0:T(8,128)} %get-tuple-element.11) | copy-start | bytes 196612

commit v5 on v4

--- a/solution.py
+++ b/solution.py
@@ -199,6 +199,48 @@
     )(half_rows, small, part_rows)
 
 
+def _sums_kernel(post_ref, part_ref, ctf_ref, cos_ref, sin_ref, real_out, imag_out):
+    dom_n, rows, width = part_ref.shape
+    count = rows // 2
+    trans = cos_ref.shape[0]
+    cosine = cos_ref[...][None]
+    sine_part = sin_ref[...][None]
+
+    def body(d, carry):
+        acc_real, acc_imag = carry
+        block = part_ref[d].astype(jnp.float32)
+        real = block[:count][:, None, :]
+        imag = block[count:][:, None, :]
+        factor = ctf_ref[d][:, None, :]
+        image_real = (factor * (real * cosine - imag * sine_part)).astype(jnp.bfloat16)
+        image_imag = (factor * (real * sine_part + imag * cosine)).astype(jnp.bfloat16)
+        weights = post_ref[d]
+        acc_real = acc_real + jnp.dot(
+            weights, image_real.reshape(count * trans, width), preferred_element_type=jnp.float32
+        )
+        acc_imag = acc_imag + jnp.dot(
+            weights, image_imag.reshape(count * trans, width), preferred_element_type=jnp.float32
+        )
+        return acc_real, acc_imag
+
+    zeros = jnp.zeros(real_out.shape, jnp.float32)
+    acc_real, acc_imag = lax.fori_loop(0, dom_n, body, (zeros, zeros))
+    real_out[...] = acc_real
+    imag_out[...] = acc_imag
+
+
+def column_sums(post_all, columns, ctf_cols, cos_cols, sin_cols):
+    out = jax.ShapeDtypeStruct((post_all.shape[1], columns.shape[2]), jnp.float32)
+    vmem = pl.BlockSpec(memory_space=pltpu.VMEM)
+    real, imag = pl.pallas_call(
+        _sums_kernel,
+        out_shape=(out, out),
+        in_specs=[vmem] * 5,
+        out_specs=(vmem, vmem),
+    )(post_all, columns, ctf_cols, cos_cols, sin_cols)
+    return jnp.stack([real, imag], axis=1)
+
+
 def make_images(planes, ctf_pix, cosine, sine_part):
     real_part = planes[:, 0][:, None, :]
     imag_part = planes[:, 1][:, None, :]
@@ -274,11 +316,10 @@
     term_rows = jnp.pad(terms, (0, term_cols * part_dev - shells)).reshape(part_dev, term_cols)
     small = jnp.concatenate([weight_rows, term_rows], axis=1)
     small = jnp.pad(small, ((0, 0), (0, -(-small.shape[1] // 128) * 128 - small.shape[1])))
-    half_rows = post_half.reshape(-1, 128)
+    half_rows = jnp.transpose(post_half, (2, 0, 1)).reshape(ori_dev, part_dev * trans_count)
     half_all, small_all, columns, orient_small = spread(
-        half_rows, small, particles.reshape(part_dev * 2, pixels), dom_size, orient_size, width, 2
-    )
-    post_all = half_all.reshape(dom_size * part_dev, trans_count, ori_dev)
+        half_rows, small, jnp.transpose(particles, (1, 0, 2)).reshape(2 * part_dev, pixels), dom_size, orient_size, width, 2
+    )
     weight_all = small_all[:, :, :ori_dev].reshape(dom_size * part_dev, ori_dev)
     shell_total = jnp.sum(
         orient_small[:, :, ori_dev : ori_dev + term_cols].reshape(orient_size, part_dev * term_cols)[:, :shells],
@@ -292,10 +333,8 @@
     ctf_cols = jnp.dot(ctf_all, pick_cols.T, precision=highest)
     cos_cols = lax.dynamic_slice_in_dim(cosines, start_pix, width, 1)
     sin_cols = lax.dynamic_slice_in_dim(sine_rows, start_pix, width, 1)
-    col_planes = columns.reshape(dom_size * part_dev, 2, width).astype(jnp.float32)
-    col_images = make_images(col_planes, ctf_cols, cos_cols, sin_cols)
-    image_sums = jnp.einsum(
-        "itj,itpk->jpk", post_all, col_images, preferred_element_type=jnp.float32
+    image_sums = column_sums(
+        half_all, columns, ctf_cols.reshape(dom_size, part_dev, width), cos_cols, sin_cols
     )
 
     divisor = part_dev * dom_size * pixels / shells

time: 88.5 us -> 92.3 us (1.043)
  Pallas kernels: 50 us -> 57.2 us
  local copies, waits for them, and re-layouts: 12.8 us -> 9.15 us
    pallas_call x0 -> x1, Pallas kernels: none -> 7.27 us  [column_sums(): pl.pallas_call(_sums_kernel, out_shape=(out, out), in_specs=[vmem] * 5, o...]
    reshape x4 -> x1, local copies, waits for them, and re-layouts: 4.06 us -> 0.67 us  [on_device(): jnp.transpose(post_half, (2, 0, 1)).reshape(ori_dev, part_dev * trans_count)]
    another operation x2, other arithmetic: 4.92 us -> 2.01 us
    dot_general x1 -> x0, matrix products: 2.28 us -> none  [on_device(): jnp.einsum('itj,itpk->jpk', post_all, col_images, preferred_element_type=...]
    unnamed x28 -> x31, local copies, waits for them, and re-layouts: 3.47 us -> 2.08 us
    convert_element_type x1 -> x0, local copies, waits for them, and re-layouts: 1.21 us -> none  [on_device(): columns.reshape(dom_size * part_dev, 2, width).astype(jnp.float32)]
    reduce_max x1, other arithmetic: 0.95 us -> 2.04 us  [on_device(): peak = jnp.max(peaks, axis=0)]
    convert_element_type x1, other arithmetic: 0.01 us -> 0.93 us  [on_device(): post_half = posterior.astype(jnp.bfloat16)]
where the time goes in v5:
time: 92.3 us; the launch traced here: 91.6 us
  Pallas kernels  57.2 us (62%)
  matrix products  14 us (15%)
  other arithmetic  10.3 us (11%)
  local copies, waits for them, and re-layouts  9.15 us (10%)
  between operations  0.93 us (1%)
    pallas_call x1, Pallas kernels, spread(): pl.pallas_call(functools.partial(_spread_kernel, dom_n, orient_n, width),...  32.3 us
    pallas_call x1, Pallas kernels, exchange(): pl.pallas_call(functools.partial(_exchange_kernel, axis, n, widths), out_...  17.6 us
    pallas_call x1, Pallas kernels, column_sums(): pl.pallas_call(_sums_kernel, out_shape=(out, out), in_specs=[vmem] * 5, o...  7.27 us
    cos x1, local copies, waits for them, and re-layouts, on_device(): cosines = jnp.cos(phases)  2.8 us
    dot_general x1, matrix products, on_device(): jnp.einsum('itj,itpk->jpk', post_half, images, preferred_element_type=jnp...  2.78 us
    unnamed x31, local copies, waits for them, and re-layouts  2.08 us
    reduce_max x1, other arithmetic, on_device(): peak = jnp.max(peaks, axis=0)  2.04 us
    dot_general x1, matrix products, on_device(): ctf_weights = jnp.dot(weight_all.T, ctf_all * ctf_all, precision=highest)  1.85 us

profile of v5, /device:TPU:1, one launch (start us, length us, event | category | flops | bytes accessed | tf_op | source)
XLA Modules:
  0.0 91.6 jit_solution(18038269662611311611)
XLA Ops:
  0.7 0.7 copy-done
  1.4 1.0 %fusion.29 = f32[256,64]{0,1:T(8,128)S(1)} fusion(f32[64,64]{1,0:T(8,128)S(1)} %copy-done, s32[256]{0:T(256)} %param.12), kind=kOutput, calls=%fused_computation.44 | convolution fusion | flops 12599296 | bytes 82944 | tf_op jit(solution)/shard_map/dot_general | solution.py:277
  2.4 1.6 %fusion.6 = f32[8,8192]{1,0:T(8,128)S(1)} fusion(s32[8192]{0:T(1024)} %param.14, f32[256,64]{0,1:T(8,128)S(1)} %fusion.29, s32[]{:T(128)S(6)} %select_n.15), kind=kOutput, calls=%fused_computation.11 | convolution fusion | flops 50855936 | bytes 327684 | tf_op jit(solution)/shard_map/dot_general | solution.py:279
  3.9 2.8 %fusion.60 = (f32[16,8192]{1,0:T(8,128)S(1)}, f32[16,8192]{1,0:T(8,128)S(1)}) fusion(f32[16,8192]{1,0:T(8,128)} %param.10), kind=kLoop, calls=%fused_computation.92 | loop fusion | bytes 1572864 | tf_op jit(solution)/shard_map/cos | solution.py:288
  7.0 1.3 %multiply_convert_fusion.1 = (bf16[8,16,1,8192]{3,1,2,0:T(8,128)(2,1)S(1)}, bf16[8,16,1,8192]{3,1,2,0:T(8,128)(2,1)S(1)}) fusion(f32[16,8192]{1,0:T(8,128)S(1)} %get-tuple-element.36, f32[8,8192]{1,0:T(8,128)S(1)} %get-tuple-element.34, f32[16,8192]{1,0:T(8,128)S(1)} %get-tuple-element.35, f32[8,8192]{1,0:T(8,128)S(1)} %get-tuple-element.33, ...), kind=kLoop, calls=%fused_computation.4 | loop fusion | flops 10485760 | bytes 6029312 | tf_op jit(solution)/shard_map/convert
  8.6 1.1 %fusion.4 = f32[16,64]{1,0:T(8,128)S(1)} fusion(f32[16,8192]{1,0:T(8,128)S(1)} %fusion.16, s32[8192]{0:T(1024)S(1)} %copy-done.6), kind=kOutput, calls=%fused_computation.9 | convolution fusion | flops 101187584 | bytes 561152 | tf_op jit(solution)/shard_map/dot_general | solution.py:283
  10.1 0.7 fusion.5
  10.8 1.4 %fusion.39 = (f32[8]{0:T(128)S(1)}, f32[8,16,16,1]{2,1,3,0:T(8,128)S(1)}) fusion(f32[8,16]{1,0:T(8,128)S(1)} %convolution_multiply_fusion.1, pred[8,16]{1,0:T(8,128)(4,1)S(1)} %broadcast_compare_fusion, f32[8192]{0:T(1024)S(1)} %bitcast.103, bf16[16,2,8192]{2,1,0:T(2,128)(2,1)S(1)} %copy-done.4, bf16[8,16,1,8192]{3,1,2,0:T(8,128)(2,1)S(1)} %get-tuple-element.32, ...), kind=kOutput, calls=%fused_computation.59 | convolution fusion | flops 69998584 | bytes 4760224 | tf_op jit(solution)/shard_map/itpk,jpk->itj/dot_general | solution.py:292
  12.2 0.6 copy-done.3
  13.0 0.6 select_maximum_fusion.1.refs_0_
  13.6 17.6 %shard_map.111 = f32[16,8,128]{2,1,0:T(8,128)} custom-call(f32[8,128]{1,0:T(8,128)} %select_maximum_fusion.1.refs_0_), custom_call_target="tpu_custom_call" | custom-call | tf_op jit(solution)/shard_map/pallas_call | solution.py:74
  31.3 2.0 %slice_reduce_fusion.1 = (f32[8]{0:T(128)}, f32[16,1,8]{2,1,0:T(1,128)}, f32[16,1,8]{2,1,0:T(1,128)S(1)}) fusion(f32[16,8,128]{2,1,0:T(8,128)} %shard_map.111), kind=kLoop, calls=%fused_computation.90 | loop fusion | flops 120 | bytes 2080 | tf_op jit(solution)/shard_map/reduce_max | solution.py:301
  33.3 0.8 copy.27
  34.1 0.7 copy.28
  34.7 0.9 fusion.50
  35.6 1.1 %fusion.59 = (f32[8]{0:T(128)S(1)}, f32[8,16]{1,0:T(8,128)S(1)}, f32[8,16,16]{2,1,0:T(8,128)S(1)}) fusion(f32[8]{0:T(128)S(1)} %fusion.50, f32[8]{0:T(128)} %get-tuple-element.37, f32[8,16]{1,0:T(8,128)S(1)} %convolution_multiply_fusion.1, f32[8,16,16,1]{2,1,3,0:T(8,128)} %copy-done.3, pred[8,16]{1,0:T(8,128)(4,1)} %copy-done.11), kind=kLoop, calls=%fused_computation.91 | loop fusion | flops 12152 | bytes 17632 | tf_op jit(solution)/shard_map/reduce_sum | solution.py:309
  36.7 2.8 %fusion.7 = f32[8192]{0:T(1024)S(1)} fusion(bf16[8,16,1,8192]{3,1,2,0:T(8,128)(2,1)} %copy-done.2, bf16[8,16,1,8192]{3,1,2,0:T(8,128)(2,1)S(1)} %get-tuple-element.31, bf16[16,2,8192]{2,1,0:T(2,128)(2,1)} %param.9, f32[8,16,16]{2,1,0:T(8,128)S(1)} %get-tuple-element.30), kind=kOutput, calls=%fused_computation.14 | convolution fusion | flops 76277760 | bytes 4759552 | tf_op jit(solution)/shard_map/itj,itpk->jpk/dot_general | solution.py:311
  39.7 1.1 %fusion.10 = f32[64]{0:T(128)S(1)} fusion(f32[8,8192]{1,0:T(8,128)S(1)} %multiply_reduce_fusion, s32[8192]{0:T(1024)S(1)} %copy-done.6, f32[8]{0:T(128)S(1)} %get-tuple-element.28), kind=kOutput, calls=%fused_computation.20 | convolution fusion | flops 50856896 | bytes 295200 | tf_op jit(solution)/shard_map/dot_general | solution.py:308
  41.0 1.0 %fusion.14 = f32[64]{0:T(128)S(1)} fusion(f32[64]{0:T(128)S(1)} %fusion.8, f32[64]{0:T(128)S(1)} %fusion.10, f32[8192,1]{0,1:T(1,128)S(1)} %bitcast.102, s32[8192]{0:T(1024)S(1)} %copy-done.6), kind=kOutput, calls=%fused_computation.24 | convolution fusion | flops 6815936 | bytes 66304 | tf_op jit(solution)/shard_map/dot_general | solution.py:312
  42.2 0.7 select_maximum_fusion.small_ref
  42.9 0.9 %fusion.37 = bf16[16,8,16]{0,2,1:T(8,128)(2,1)S(1)} fusion(f32[8,16,16,1]{2,1,3,0:T(8,128)} %copy-done.3, f32[8]{0:T(128)} %copy-done.13, f32[8]{0:T(128)S(1)} %copy-done.12, f32[16,8]{0,1:T(8,128)S(1)} %bitcast.97, pred[16,8]{0,1:T(8,128)(4,1)S(1)} %fusion.67), kind=kLoop, calls=%fused_computation.57 | loop fusion | flops 10240 | bytes 12992 | tf_op jit(solution)/shard_map/convert_element_type | solution.py:304
  43.8 0.7 copy.37.half_ref
  44.5 0.8 copy.51
  45.3 32.3 %shard_map.112 = (bf16[32,16,128]{2,1,0:T(8,128)(2,1)}, f32[32,8,128]{2,1,0:T(8,128)}, bf16[32,16,256]{2,1,0:T(8,128)(2,1)}, f32[16,8,128]{2,1,0:T(8,128)}) custom-call(bf16[16,128]{1,0:T(8,128)(2,1)} %copy.37.half_ref, f32[8,128]{1,0:T(8,128)} %select_maximum_fusion.small_ref, bf16[16,8192]{1,0:T(8,128)(2,1)} %bitcast.95), custom_call_target="tpu_custom_call" | custom-call | tf_op jit(solution)/shard_map/pallas_call | solution.py:182
  77.7 0.6 constant_dynamic-slice_fusion
  78.6 1.0 %convolution_bitcast_fusion.1.ctf_ref = f32[32,8,256]{2,1,0:T(8,128)} fusion(f32[256,64]{0,1:T(8,128)S(1)} %fusion.29, pred[8192,64]{0,1:T(32,128)(4,1)S(1)} %iota_compare_fusion, s32[]{:T(128)S(6)} %select_n.18), kind=kOutput, calls=%fused_computation.15 | convolution fusion | flops 50331648 | bytes 344068 | tf_op jit(solution)/shard_map/dot_general | solution.py:333
  79.6 7.3 %shard_map.113 = (f32[16,256]{1,0:T(8,128)}, f32[16,256]{1,0:T(8,128)}) custom-call(bf16[32,16,128]{2,1,0:T(8,128)(2,1)} %get-tuple-element.10.post_ref, bf16[32,16,256]{2,1,0:T(8,128)(2,1)} %get-tuple-element.11.part_ref, f32[32,8,256]{2,1,0:T(8,128)} %convolution_bitcast_fusion.1.ctf_ref, f32[16,256]{1,0:T(8,128)} %get-tuple-element.43.cos_ref, ...), custom_call_target="tpu_custom_call" | custom-call | tf_op jit(solution)/shard_map/pallas_call | solution.py:235
  86.8 0.7 pad_maximum_fusion.5
  87.6 0.6 copy.33
  88.2 1.9 %fusion.26 = f32[16,64]{1,0:T(8,128)} fusion(f32[32,8,128]{2,1,0:T(8,128)} %get-tuple-element.14, f32[256,64]{0,1:T(8,128)S(1)} %fusion.29), kind=kOutput, calls=%fused_computation.40 | convolution fusion | flops 3162112 | bytes 200704 | tf_op jit(solution)/shard_map/dot_general | solution.py:329
  90.1 0.9 %slice_reduce_fusion = f32[8,8]{1,0:T(8,128)S(1)} fusion(f32[16,8,128]{2,1,0:T(8,128)} %get-tuple-element.15), kind=kLoop, calls=%fused_computation.52 | loop fusion | flops 960 | bytes 4352 | tf_op jit(solution)/shard_map/reduce_sum | solution.py:324
  91.0 0.6 div.47
  (40 shorter events, 1.9 us)
Async XLA Ops:
  0.6 0.8 copy-start
  0.6 6.1 %copy-start.1 = (bf16[8,2,8192]{2,1,0:T(2,128)(2,1)S(1)}, bf16[8,2,8192]{2,1,0:T(2,128)(2,1)}, u32[]{:S(2)}) copy-start(bf16[8,2,8192]{2,1,0:T(2,128)(2,1)} %param.8) | copy-start | bytes 786436
  6.9 1.3 %copy-start.4 = (bf16[16,2,8192]{2,1,0:T(2,128)(2,1)S(1)}, bf16[16,2,8192]{2,1,0:T(2,128)(2,1)}, u32[]{:S(2)}) copy-start(bf16[16,2,8192]{2,1,0:T(2,128)(2,1)} %param.9) | copy-start | bytes 1572868
  7.0 1.6 %copy-start.6 = (s32[8192]{0:T(1024)S(1)}, s32[8192]{0:T(1024)}, u32[]{:S(2)}) copy-start(s32[8192]{0:T(1024)} %param.14) | copy-start | bytes 98308
  7.0 2.7 %copy-start.14 = (f32[64]{0:T(128)S(1)}, f32[64]{0:T(128)}, u32[]{:S(2)}) copy-start(f32[64]{0:T(128)} %param.15) | copy-start | bytes 772
  7.0 3.0 %copy-start.9 = (s32[8,16]{1,0:T(8,128)S(1)}, s32[8,16]{1,0:T(8,128)}, u32[]{:S(2)}) copy-start(s32[8,16]{1,0:T(8,128)} %param.11) | copy-start | bytes 1540
  8.3 3.9 %copy-start.2 = (bf16[8,16,1,8192]{3,1,2,0:T(8,128)(2,1)}, bf16[8,16,1,8192]{3,1,2,0:T(8,128)(2,1)S(1)}, u32[]{:S(2)}) copy-start(bf16[8,16,1,8192]{3,1,2,0:T(8,128)(2,1)S(1)} %get-tuple-element.32) | copy-start | bytes 6291460
  9.7 1.1 %copy-start.7 = (f32[16,64]{1,0:T(8,128)}, f32[16,64]{1,0:T(8,128)S(1)}, u32[]{:S(2)}) copy-start(f32[16,64]{1,0:T(8,128)S(1)} %fusion.4) | copy-start | bytes 12292
  10.0 2.1 %copy-start.11 = (pred[8,16]{1,0:T(8,128)(4,1)}, pred[8,16]{1,0:T(8,128)(4,1)S(1)}, u32[]{:S(2)}) copy-start(pred[8,16]{1,0:T(8,128)(4,1)S(1)} %broadcast_compare_fusion) | copy-start | bytes 388
  12.2 0.6 copy-start.3
  35.6 1.1 %copy-start.13 = (f32[8]{0:T(128)}, f32[8]{0:T(128)S(1)}, u32[]{:S(2)}) copy-start(f32[8]{0:T(128)S(1)} %fusion.50) | copy-start | bytes 100
  36.7 2.8 %copy-start.5 = (f32[8,16,16]{2,1,0:T(8,128)}, f32[8,16,16]{2,1,0:T(8,128)S(1)}, u32[]{:S(2)}) copy-start(f32[8,16,16]{2,1,0:T(8,128)S(1)} %get-tuple-element.30) | copy-start | bytes 24580
  36.7 4.1 %copy-start.8 = (f32[16,64]{1,0:T(8,128)S(1)}, f32[16,64]{1,0:T(8,128)}, u32[]{:S(2)}) copy-start(f32[16,64]{1,0:T(8,128)} %copy-done.7) | copy-start | bytes 12292
  36.7 6.2 %copy-start.10 = (s32[8,16]{1,0:T(8,128)S(1)}, s32[8,16]{1,0:T(8,128)}, u32[]{:S(2)}) copy-start(s32[8,16]{1,0:T(8,128)} %param.11) | copy-start | bytes 1540
  36.7 6.2 %copy-start.12 = (f32[8]{0:T(128)S(1)}, f32[8]{0:T(128)}, u32[]{:S(2)}) copy-start(f32[8]{0:T(128)} %get-tuple-element.37) | copy-start | bytes 100

commit v6 on v4

--- a/solution.py
+++ b/solution.py
@@ -82,9 +82,9 @@
     )(*[x for x, _ in payloads])
 
 
-def _spread_kernel(dom_n, orient_n, width, half_ref, small_ref, part_ref,
-                   half_out, small_out, part_out, terms_out,
-                   half_held, small_held, part_held, summed, terms_held,
+def _spread_kernel(dom_n, orient_n, half_ref, small_ref,
+                   half_out, small_out, terms_out,
+                   half_held, small_held, summed, terms_held,
                    send_sem, recv_sem, orient_send, orient_recv):
     me = lax.axis_index("dom")
     mine = lax.axis_index("orient")
@@ -104,16 +104,13 @@
     lax.fori_loop(1, orient_n, greet_orient, 0)
     pl.semaphore_wait(barrier, dom_n + orient_n - 2)
 
-    def columns(peer):
-        return part_ref.at[:, pl.ds(pl.multiple_of(peer * width, width), width)]
-
-    sources = (lambda peer: half_ref, lambda peer: small_ref, columns)
-    held = (half_held, small_held, part_held)
+    sources = (half_ref, small_ref)
+    held = (half_held, small_held)
 
     def copy(index, k):
         peer = lax.rem(me + k, dom_n)
         return pltpu.make_async_remote_copy(
-            src_ref=sources[index](peer),
+            src_ref=sources[index],
             dst_ref=held[index].at[me],
             send_sem=send_sem.at[index, k],
             recv_sem=recv_sem.at[index, k],
@@ -122,13 +119,13 @@
         )
 
     def start(k, carry):
-        for index in (1, 0, 2):
+        for index in (1, 0):
             copy(index, k).start()
         return carry
 
     lax.fori_loop(1, dom_n, start, 0)
-    for index in range(3):
-        held[index][me] = sources[index](me)[...]
+    for index in range(2):
+        held[index][me] = sources[index][...]
 
     def finish(index):
         def body(k, carry):
@@ -158,7 +155,6 @@
 
     lax.fori_loop(1, orient_n, orient_start, 0)
     terms_held[mine] = summed[...]
-    finish(2)
 
     def orient_finish(k, carry):
         orient_copy(k).wait()
@@ -167,36 +163,33 @@
     lax.fori_loop(1, orient_n, orient_finish, 0)
     half_out[...] = half_held[...]
     small_out[...] = small_held[...]
-    part_out[...] = part_held[...]
     terms_out[...] = terms_held[...]
 
 
-def spread(half_rows, small, part_rows, dom_n, orient_n, width, collective_id):
+def spread(half_rows, small, dom_n, orient_n, collective_id):
     shapes = (
         jax.ShapeDtypeStruct((dom_n,) + half_rows.shape, half_rows.dtype),
         jax.ShapeDtypeStruct((dom_n,) + small.shape, small.dtype),
-        jax.ShapeDtypeStruct((dom_n, part_rows.shape[0], width), part_rows.dtype),
         jax.ShapeDtypeStruct((orient_n,) + small.shape, small.dtype),
     )
     vmem = pl.BlockSpec(memory_space=pltpu.VMEM)
     return pl.pallas_call(
-        functools.partial(_spread_kernel, dom_n, orient_n, width),
+        functools.partial(_spread_kernel, dom_n, orient_n),
         out_shape=shapes,
-        in_specs=[vmem] * 3,
-        out_specs=(vmem,) * 4,
+        in_specs=[vmem] * 2,
+        out_specs=(vmem,) * 3,
         scratch_shapes=[
             pltpu.VMEM(shapes[0].shape, shapes[0].dtype),
             pltpu.VMEM(shapes[1].shape, shapes[1].dtype),
+            pltpu.VMEM(small.shape, small.dtype),
             pltpu.VMEM(shapes[2].shape, shapes[2].dtype),
-            pltpu.VMEM(small.shape, small.dtype),
-            pltpu.VMEM(shapes[3].shape, shapes[3].dtype),
-            pltpu.SemaphoreType.DMA((3, dom_n)),
-            pltpu.SemaphoreType.DMA((3, dom_n)),
+            pltpu.SemaphoreType.DMA((2, dom_n)),
+            pltpu.SemaphoreType.DMA((2, dom_n)),
             pltpu.SemaphoreType.DMA((orient_n,)),
             pltpu.SemaphoreType.DMA((orient_n,)),
         ],
         compiler_params=pltpu.CompilerParams(collective_id=collective_id, has_side_effects=True),
-    )(half_rows, small, part_rows)
+    )(half_rows, small)
 
 
 def make_images(planes, ctf_pix, cosine, sine_part):
@@ -225,6 +218,9 @@
     orient_size = lax.axis_size("orient")
     width = pixels // dom_size
     dom_index = lax.axis_index("dom")
+
+    part_rows = particles.reshape(part_dev * 2, dom_size, width)
+    columns = lax.all_to_all(part_rows, "dom", 1, 0, tiled=True).reshape(dom_size, part_dev * 2, width)
 
     shell_pick = (shell_index[:, None] == jnp.arange(shells, dtype=jnp.int32)[None, :]).astype(
         jnp.float32
@@ -275,9 +271,7 @@
     small = jnp.concatenate([weight_rows, term_rows], axis=1)
     small = jnp.pad(small, ((0, 0), (0, -(-small.shape[1] // 128) * 128 - small.shape[1])))
     half_rows = post_half.reshape(-1, 128)
-    half_all, small_all, columns, orient_small = spread(
-        half_rows, small, particles.reshape(part_dev * 2, pixels), dom_size, orient_size, width, 2
-    )
+    half_all, small_all, orient_small = spread(half_rows, small, dom_size, orient_size, 2)
     post_all = half_all.reshape(dom_size * part_dev, trans_count, ori_dev)
     weight_all = small_all[:, :, :ori_dev].reshape(dom_size * part_dev, ori_dev)
     shell_total = jnp.sum(

time: 88.5 us -> 93.9 us (1.061)
  starting transfers between devices: 0 us -> 10.5 us
  Pallas kernels: 50 us -> 43.5 us
  other arithmetic: 9.63 us -> 11.9 us
  local copies, waits for them, and re-layouts: 12.8 us -> 11.7 us
    all_to_all x0 -> x1, starting transfers between devices: none -> 10.5 us  [on_device(): lax.all_to_all(part_rows, 'dom', 1, 0, tiled=True)]
    pallas_call x1, Pallas kernels: 32.3 us -> 26.5 us  [spread(): pl.pallas_call(functools.partial(_spread_kernel, dom_n, orient_n), out_sh...]
    dot_general x1, matrix products: 2.28 us -> 0.8 us  [on_device(): jnp.einsum('itj,itpk->jpk', post_all, col_images, preferred_element_type=...]
    unnamed x28 -> x30, local copies, waits for them, and re-layouts: 3.47 us -> 2.02 us
    reshape x1 -> x2, local copies, waits for them, and re-layouts: 0.79 us -> 2.06 us  [on_device(): part_rows = particles.reshape(part_dev * 2, dom_size, width)]
    another operation x2, other arithmetic: 4.92 us -> 3.7 us
    convert_element_type x1, other arithmetic: 0.16 us -> 1.17 us  [on_device(): planes = particles.astype(jnp.float32)]
    cos x1, local copies, waits for them, and re-layouts: 2.8 us -> 1.84 us  [on_device(): cosines = jnp.cos(phases)]
  transfers between devices with their start and end apart: 0 -> 1, of which waited for: 0 -> 0; matrix products, arithmetic and copies ran while one was open for 0% -> 33% of each run, Pallas kernels for 0% -> 47%
where the time goes in v6:
time: 93.9 us; the launch traced here: 93.3 us
  Pallas kernels  43.5 us (46%)
  matrix products  14.7 us (16%)
  other arithmetic  11.9 us (13%)
  local copies, waits for them, and re-layouts  11.7 us (12%)
  starting transfers between devices  10.5 us (11%)
    pallas_call x1, Pallas kernels, spread(): pl.pallas_call(functools.partial(_spread_kernel, dom_n, orient_n), out_sh...  26.5 us
    pallas_call x1, Pallas kernels, exchange(): pl.pallas_call(functools.partial(_exchange_kernel, axis, n, widths), out_...  17.1 us
    all_to_all x1, starting transfers between devices, on_device(): lax.all_to_all(part_rows, 'dom', 1, 0, tiled=True)  10.5 us
    another operation x2, other arithmetic  3.7 us
    dot_general x1, matrix products, on_device(): jnp.einsum('itj,itpk->jpk', post_half, images, preferred_element_type=jnp...  3.35 us
    reshape x2, local copies, waits for them, and re-layouts, on_device(): post_all = half_all.reshape(dom_size * part_dev, trans_count, ori_dev)  2.77 us
    reshape x2, local copies, waits for them, and re-layouts, on_device(): part_rows = particles.reshape(part_dev * 2, dom_size, width)  2.06 us
    unnamed x30, local copies, waits for them, and re-layouts  2.02 us
  transfers between devices with their start and end apart: 1, of which 0 were waited for; matrix products, arithmetic and copies ran while one was open for 33% of the time, Pallas kernels for 47%

profile of v6, /device:TPU:1, one launch (start us, length us, event | category | flops | bytes accessed | tf_op | source)
XLA Modules:
  0.0 93.3 jit_solution(1315967692023677756)
XLA Ops:
  0.7 1.2 %reshape.100 = bf16[16,32,256]{2,1,0:T(8,128)(2,1)S(1)} reshape(bf16[8,2,8192]{2,1,0:T(2,128)(2,1)} %param.8) | data formatting | bytes 524288 | tf_op jit(solution)/shard_map/reshape | solution.py:222
  1.9 0.9 copy.30
  2.7 10.5 %all-to-all-start = ((bf16[16,32,256]{2,0,1:T(8,128)(2,1)}), bf16[16,32,256]{2,0,1:T(8,128)(2,1)S(1)}, u32[]{:S(2)}, u32[]{:S(2)}) async-start(bf16[16,32,256]{2,0,1:T(8,128)(2,1)} %copy.30), calls=%async_computation | async-start | bytes 524288 | tf_op jit(solution)/shard_map/all_to_all | solution.py:223
  13.3 1.2 %copy_convert_fusion = f32[8,2,8192]{2,0,1:T(8,128)S(1)} fusion(bf16[8,2,8192]{2,1,0:T(2,128)(2,1)} %param.8), kind=kLoop, calls=%fused_computation.50 | loop fusion | flops 131072 | bytes 786432 | tf_op jit(solution)/shard_map/convert_element_type | solution.py:241
  14.4 0.9 multiply_reduce_fusion
  15.3 1.8 %fusion.66 = (f32[16,8192]{1,0:T(8,128)S(1)}, f32[16,8192]{1,0:T(8,128)S(1)}) fusion(f32[16,8192]{1,0:T(8,128)S(1)} %copy-done.3), kind=kLoop, calls=%fused_computation.96 | loop fusion | bytes 1572864 | tf_op jit(solution)/shard_map/cos | solution.py:242
  17.2 0.8 slice_bitcast_fusion.1
  18.3 1.1 %fusion.8 = f32[16,64]{1,0:T(8,128)S(1)} fusion(f32[16,8192]{1,0:T(8,128)S(1)} %fusion.26, s32[8192]{0:T(1024)S(1)} %copy-done.9), kind=kOutput, calls=%fused_computation.15 | convolution fusion | flops 101187584 | bytes 561152 | tf_op jit(solution)/shard_map/dot_general | solution.py:237
  19.4 1.4 %fusion.9 = f32[1,8192]{1,0:T(1,128)} fusion(s32[8192]{0:T(1024)S(1)} %copy-done.9, f32[64]{0:T(128)S(1)} %copy-done.12), kind=kOutput, calls=%fused_computation.16 | convolution fusion | flops 6815744 | bytes 65792 | tf_op jit(solution)/shard_map/dot_general | solution.py:234
  21.1 0.8 fusion.10
  22.2 2.3 %multiply_convert_fusion.3 = (bf16[8,16,1,8192]{3,1,2,0:T(8,128)(2,1)S(1)}, bf16[8,16,1,8192]{3,1,2,0:T(8,128)(2,1)S(1)}) fusion(f32[16,8192]{1,0:T(8,128)S(1)} %get-tuple-element.34, f32[8,8192]{1,0:T(8,128)} %get-tuple-element.32, f32[16,8192]{1,0:T(8,128)S(1)} %get-tuple-element.33, f32[8,8192]{1,0:T(8,128)} %get-tuple-element.31, f32[8,8192]{1,0:T(8,128)S(1)} %fusion.10), kind=kLoop, calls=%fused_computation.10 | loop fusion | flops 10485760 | bytes 6029312 | tf_op jit(solution)/shard_map/convert.5
  24.5 1.4 %fusion.67 = (f32[8]{0:T(128)S(1)}, f32[8,16,16]{2,1,0:T(8,128)S(1)}) fusion(f32[8,16]{1,0:T(8,128)S(1)} %convolution_multiply_fusion.1, f32[8192]{0:T(1024)S(1)} %bitcast.85, bf16[16,2,8192]{2,1,0:T(2,128)(2,1)S(1)} %copy-done.5, bf16[8,16,1,8192]{3,1,2,0:T(8,128)(2,1)S(1)} %get-tuple-element.26, bf16[8,16,1,8192]{3,1,2,0:T(8,128)(2,1)S(1)} %get-tuple-element.25, ...), kind=kOutput, calls=%fused_computation.97 | convolution fusion | flops 69998584 | bytes 4760224 | tf_op jit(solution)/shard_map/itpk,jpk->itj/dot_general | solution.py:246
  25.9 0.6 copy-done.7
  26.8 0.6 select_maximum_fusion.1.refs_0_
  27.4 17.1 %shard_map.111 = f32[16,8,128]{2,1,0:T(8,128)} custom-call(f32[8,128]{1,0:T(8,128)} %select_maximum_fusion.1.refs_0_), custom_call_target="tpu_custom_call" | custom-call | tf_op jit(solution)/shard_map/pallas_call | solution.py:74
  44.5 1.0 %slice_reduce_fusion.1 = (f32[8]{0:T(128)S(1)}, f32[16,1,8]{2,1,0:T(1,128)S(1)}, f32[16,1,8]{2,1,0:T(1,128)S(1)}) fusion(f32[16,8,128]{2,1,0:T(8,128)} %shard_map.111), kind=kLoop, calls=%fused_computation.93 | loop fusion | flops 120 | bytes 2080 | tf_op jit(solution)/shard_map/reduce_max | solution.py:255
  45.7 1.1 %fusion.64 = (f32[8]{0:T(128)S(1)}, f32[8,16]{1,0:T(8,128)S(1)}, f32[8,16,16]{2,1,0:T(8,128)S(1)}) fusion(f32[8]{0:T(128)S(1)} %fusion.54, f32[8,16,16]{2,1,0:T(8,128)} %copy-done.7, f32[8]{0:T(128)S(1)} %get-tuple-element.35), kind=kLoop, calls=%fused_computation.94 | loop fusion | flops 8056 | bytes 16992 | tf_op jit(solution)/shard_map/reduce_sum | solution.py:263
  46.8 0.6 copy-done.6
  47.5 3.4 %fusion.11 = f32[8192]{0:T(1024)} fusion(bf16[8,16,1,8192]{3,1,2,0:T(8,128)(2,1)} %copy-done.2, bf16[8,16,1,8192]{3,1,2,0:T(8,128)(2,1)S(1)} %get-tuple-element.25, bf16[16,2,8192]{2,1,0:T(2,128)(2,1)} %param.9, bf16[8,16,16]{2,1,0:T(8,128)(2,1)S(1)} %convert_element_type.35), kind=kOutput, calls=%fused_computation.20 | convolution fusion | flops 76275712 | bytes 4755456 | tf_op jit(solution)/shard_map/itj,itpk->jpk/dot_general | solution.py:265
  50.8 0.7 reshape.97.half_ref
  51.5 1.1 %iota_compare_fusion = pred[8192,64]{0,1:T(32,128)(4,1)S(1)} fusion(s32[8192]{0:T(1024)} %param.14), kind=kLoop, calls=%fused_computation.12 | loop fusion | flops 524288 | bytes 557056 | tf_op jit(solution)/shard_map/eq | solution.py:225
  52.8 2.0 %fusion.20 = f32[64]{0:T(128)S(1)} fusion(f32[8,8192]{1,0:T(8,128)} %multiply_reduce_fusion, s32[8192]{0:T(1024)} %param.14, f32[8]{0:T(128)S(1)} %get-tuple-element.22), kind=kOutput, calls=%fused_computation.29 | convolution fusion | flops 50856896 | bytes 295200 | tf_op jit(solution)/shard_map/dot_general | solution.py:262
  54.9 1.8 %fusion.24 = f32[64]{0:T(128)S(1)} fusion(f32[64]{0:T(128)S(1)} %fusion.18, f32[64]{0:T(128)S(1)} %fusion.20, f32[8192,1]{0,1:T(1,128)} %bitcast.86, s32[8192]{0:T(1024)} %param.14), kind=kOutput, calls=%fused_computation.33 | convolution fusion | flops 6815936 | bytes 66304 | tf_op jit(solution)/shard_map/dot_general | solution.py:266
  56.8 0.7 select_maximum_fusion.small_ref
  57.4 26.5 %shard_map.112 = (bf16[32,16,128]{2,1,0:T(8,128)(2,1)}, f32[32,8,128]{2,1,0:T(8,128)}, f32[16,8,128]{2,1,0:T(8,128)}) custom-call(bf16[16,128]{1,0:T(8,128)(2,1)} %reshape.97.half_ref, f32[8,128]{1,0:T(8,128)} %select_maximum_fusion.small_ref), custom_call_target="tpu_custom_call" | custom-call | tf_op jit(solution)/shard_map/pallas_call | solution.py:176
  83.9 1.0 %slice_reduce_fusion = f32[8,8]{1,0:T(8,128)S(1)} fusion(f32[16,8,128]{2,1,0:T(8,128)} %get-tuple-element.9), kind=kLoop, calls=%fused_computation.57 | loop fusion | flops 960 | bytes 4352 | tf_op jit(solution)/shard_map/reduce_sum | solution.py:277
  84.9 1.9 %reshape.99 = bf16[256,16,16]{2,1,0:T(8,128)(2,1)S(1)} reshape(bf16[32,16,128]{2,1,0:T(8,128)(2,1)} %get-tuple-element.7) | data formatting | bytes 262144 | tf_op jit(solution)/shard_map/reshape | solution.py:275
  86.9 0.8 copy.31
  88.3 1.0 %fusion.36 = f32[16,64]{1,0:T(8,128)} fusion(f32[32,8,128]{2,1,0:T(8,128)S(1)} %copy-done.8, f32[256,64]{0,1:T(8,128)S(1)} %fusion.40), kind=kOutput, calls=%fused_computation.51 | convolution fusion | flops 3162112 | bytes 200704 | tf_op jit(solution)/shard_map/dot_general | solution.py:282
  90.4 1.4 %multiply_convert_fusion.1 = (bf16[256,16,1,256]{3,0,1,2:T(8,128)(2,1)S(1)}, bf16[256,16,1,256]{3,0,1,2:T(8,128)(2,1)S(1)}) fusion(f32[16,256]{1,0:T(8,128)S(1)} %get-tuple-element.40, f32[256,256]{1,0:T(8,128)S(1)} %get-tuple-element.42, f32[16,256]{1,0:T(8,128)S(1)} %get-tuple-element.41, f32[256,256]{1,0:T(8,128)S(1)} %get-tuple-element.43, ...), kind=kLoop, calls=%fused_computation.8 | loop fusion | flops 10485760 | bytes 5013504 | tf_op jit(solution)/shard_map/convert.3
  91.8 0.8 fusion.15
  92.6 0.6 copy.32
  (46 shorter events, 3.6 us)
Async XLA Ops:
  0.6 20.2 %copy-start = (f32[64,64]{1,0:T(8,128)S(1)}, f32[64,64]{1,0:T(8,128)}, u32[]{:S(2)}) copy-start(f32[64,64]{1,0:T(8,128)} %param.13) | copy-start | bytes 49156
  0.6 13.8 %copy-start.1 = (bf16[8,2,8192]{2,1,0:T(2,128)(2,1)S(1)}, bf16[8,2,8192]{2,1,0:T(2,128)(2,1)}, u32[]{:S(2)}) copy-start(bf16[8,2,8192]{2,1,0:T(2,128)(2,1)} %param.8) | copy-start | bytes 786436
  0.7 14.6 %copy-start.3 = (f32[16,8192]{1,0:T(8,128)S(1)}, f32[16,8192]{1,0:T(8,128)}, u32[]{:S(2)}) copy-start(f32[16,8192]{1,0:T(8,128)} %param.10) | copy-start | bytes 1572868
  2.7 86.8 %all-to-all-start = ((bf16[16,32,256]{2,0,1:T(8,128)(2,1)}), bf16[16,32,256]{2,0,1:T(8,128)(2,1)S(1)}, u32[]{:S(2)}, u32[]{:S(2)}) async-start(bf16[16,32,256]{2,0,1:T(8,128)(2,1)} %copy.30), calls=%async_computation | async-start | bytes 524288 | tf_op jit(solution)/shard_map/all_to_all | solution.py:223
  13.2 4.8 %copy-start.4 = (bf16[16,2,8192]{2,1,0:T(2,128)(2,1)S(1)}, bf16[16,2,8192]{2,1,0:T(2,128)(2,1)}, u32[]{:S(2)}) copy-start(bf16[16,2,8192]{2,1,0:T(2,128)(2,1)} %param.9) | copy-start | bytes 1572868
  14.4 3.9 %copy-start.9 = (s32[8192]{0:T(1024)S(1)}, s32[8192]{0:T(1024)}, u32[]{:S(2)}) copy-start(s32[8192]{0:T(1024)} %param.14) | copy-start | bytes 98308
  15.3 4.1 %copy-start.12 = (f32[64]{0:T(128)S(1)}, f32[64]{0:T(128)}, u32[]{:S(2)}) copy-start(f32[64]{0:T(128)} %param.15) | copy-start | bytes 772
  15.3 5.5 %copy-start.11 = (s32[256]{0:T(256)S(1)}, s32[256]{0:T(256)}, u32[]{:S(2)}) copy-start(s32[256]{0:T(256)} %param.12) | copy-start | bytes 3076
  17.2 5.0 %copy-start.10 = (s32[8,16]{1,0:T(8,128)S(1)}, s32[8,16]{1,0:T(8,128)}, u32[]{:S(2)}) copy-start(s32[8,16]{1,0:T(8,128)} %param.11) | copy-start | bytes 1540
  22.2 2.3 %copy-start.5 = (bf16[16,2,8192]{2,1,0:T(2,128)(2,1)S(1)}, bf16[16,2,8192]{2,1,0:T(2,128)(2,1)}, u32[]{:S(2)}) copy-start(bf16[16,2,8192]{2,1,0:T(2,128)(2,1)} %param.9) | copy-start | bytes 1572868
  22.2 2.3 %copy-start.13 = (f32[1,8192]{1,0:T(1,128)S(1)}, f32[1,8192]{1,0:T(1,128)}, u32[]{:S(2)}) copy-start(f32[1,8192]{1,0:T(1,128)} %fusion.9) | copy-start | bytes 98308
  24.5 1.4 %copy-start.2 = (bf16[8,16,1,8192]{3,1,2,0:T(8,128)(2,1)}, bf16[8,16,1,8192]{3,1,2,0:T(8,128)(2,1)S(1)}, u32[]{:S(2)}) copy-start(bf16[8,16,1,8192]{3,1,2,0:T(8,128)(2,1)S(1)} %get-tuple-element.26) | copy-start | bytes 6291460
  25.9 0.6 copy-start.7
  46.8 0.6 copy-start.6
  83.9 4.4 %copy-start.8 = (f32[32,8,128]{2,1,0:T(8,128)S(1)}, f32[32,8,128]{2,1,0:T(8,128)}, u32[]{:S(2)}) copy-start(f32[32,8,128]{2,1,0:T(8,128)} %get-tuple-element.8) | copy-start | bytes 393220

commit v7 on v4

--- a/solution.py
+++ b/solution.py
@@ -80,6 +80,97 @@
         + [pltpu.SemaphoreType.DMA((count, n)), pltpu.SemaphoreType.DMA((count, n))],
         compiler_params=pltpu.CompilerParams(collective_id=collective_id, has_side_effects=True),
     )(*[x for x, _ in payloads])
+
+
+def _score_kernel(orient_n, real_ref, imag_ref, ctf_ref, cos_ref, sin_ref, wr_ref, wi_ref,
+                  quad_ref, mask_ref, scores_out, stats_out, stats, held, send_sem, recv_sem):
+    me = lax.axis_index("orient")
+    barrier = pltpu.get_barrier_semaphore()
+
+    def greet(k, carry):
+        peer = lax.rem(me + k, orient_n)
+        pl.semaphore_signal(barrier, inc=1, device_id={"orient": peer}, device_id_type=MESH_ID)
+        return carry
+
+    lax.fori_loop(1, orient_n, greet, 0)
+
+    trans = cos_ref.shape[0]
+    real = real_ref[...]
+    imag = imag_ref[...]
+    factor = ctf_ref[...]
+    quad = quad_ref[...]
+    allowed = mask_ref[...] == 1
+    dims = (((1,), (1,)), ((), ()))
+
+    def score(t, peak):
+        cosine = cos_ref[pl.ds(t, 1), :]
+        sine_part = sin_ref[pl.ds(t, 1), :]
+        image_real = (factor * (real * cosine - imag * sine_part)).astype(jnp.bfloat16)
+        image_imag = (factor * (real * sine_part + imag * cosine)).astype(jnp.bfloat16)
+        cross = lax.dot_general(image_real, wr_ref[...], dims, preferred_element_type=jnp.float32)
+        cross = cross + lax.dot_general(image_imag, wi_ref[...], dims, preferred_element_type=jnp.float32)
+        value = jnp.where(allowed, cross - quad, -1e30)
+        scores_out[t] = value
+        return jnp.maximum(peak, jnp.max(value, axis=1, keepdims=True))
+
+    rows = quad.shape[0]
+    peak = lax.fori_loop(0, trans, score, jnp.full((rows, 1), -jnp.inf, jnp.float32))
+
+    def add(t, total):
+        return total + jnp.sum(jnp.exp(scores_out[t] - peak), axis=1, keepdims=True)
+
+    total = lax.fori_loop(0, trans, add, jnp.zeros((rows, 1), jnp.float32))
+    lane = lax.broadcasted_iota(jnp.int32, stats.shape, 1)
+    stats[...] = jnp.where(lane == 0, peak, jnp.where(lane == 1, total, 0.0))
+    pl.semaphore_wait(barrier, orient_n - 1)
+
+    def copy(k):
+        peer = lax.rem(me + k, orient_n)
+        return pltpu.make_async_remote_copy(
+            src_ref=stats,
+            dst_ref=held.at[me],
+            send_sem=send_sem.at[k],
+            recv_sem=recv_sem.at[k],
+            device_id={"orient": peer},
+            device_id_type=MESH_ID,
+        )
+
+    def start(k, carry):
+        copy(k).start()
+        return carry
+
+    lax.fori_loop(1, orient_n, start, 0)
+    held[me] = stats[...]
+
+    def finish(k, carry):
+        copy(k).wait()
+        return carry
+
+    lax.fori_loop(1, orient_n, finish, 0)
+    stats_out[...] = held[...]
+
+
+def local_scores(real, imag, factor, cosines, sine_rows, w_real, w_imag, quadratic, mask, orient_n, collective_id):
+    rows = real.shape[0]
+    trans = cosines.shape[0]
+    stats_shape = (rows, 128)
+    vmem = pl.BlockSpec(memory_space=pltpu.VMEM)
+    return pl.pallas_call(
+        functools.partial(_score_kernel, orient_n),
+        out_shape=(
+            jax.ShapeDtypeStruct((trans, rows, quadratic.shape[1]), jnp.float32),
+            jax.ShapeDtypeStruct((orient_n,) + stats_shape, jnp.float32),
+        ),
+        in_specs=[vmem] * 9,
+        out_specs=(vmem, vmem),
+        scratch_shapes=[
+            pltpu.VMEM(stats_shape, jnp.float32),
+            pltpu.VMEM((orient_n,) + stats_shape, jnp.float32),
+            pltpu.SemaphoreType.DMA((orient_n,)),
+            pltpu.SemaphoreType.DMA((orient_n,)),
+        ],
+        compiler_params=pltpu.CompilerParams(collective_id=collective_id, has_side_effects=True),
+    )(real, imag, factor, cosines, sine_rows, w_real, w_imag, quadratic, mask)
 
 
 def _spread_kernel(dom_n, orient_n, width, half_ref, small_ref, part_ref,
@@ -246,16 +337,13 @@
     cosines = jnp.cos(phases)
     sine_rows = jnp.sin(phases)
 
-    images = make_images(planes, ctf_pix, cosines, sine_rows)
-    cross = jnp.einsum("itpk,jpk->itj", images, weighted, preferred_element_type=jnp.float32)
-    scores = cross - quadratic[:, None, :]
-    scores = jnp.where((mask == 1)[:, None, :], scores, -1e30)
-    local_peak = jnp.max(scores, axis=(1, 2))
-    local_total = jnp.sum(jnp.exp(scores - local_peak[:, None, None]), axis=(1, 2))
-
-    (stats,) = exchange([(pad_rows(jnp.stack([local_peak, local_total]), 128), None)], "orient", orient_size, 1)
-    peaks = stats[:, 0, :part_dev]
-    totals = stats[:, 1, :part_dev]
+    by_trans, stats = local_scores(
+        planes[:, 0], planes[:, 1], ctf_pix, cosines, sine_rows,
+        weighted[:, 0], weighted[:, 1], quadratic, mask, orient_size, 1,
+    )
+    scores = jnp.transpose(by_trans, (1, 0, 2))
+    peaks = stats[:, :, 0]
+    totals = stats[:, :, 1]
     peak = jnp.max(peaks, axis=0)
     total = jnp.sum(totals * jnp.exp(peaks - peak[None, :]), axis=0)
     posterior = jnp.exp(scores - peak[:, None, None]) / total[:, None, None]
@@ -266,6 +354,7 @@
     part_norm = jnp.dot(jnp.sum(planes * planes, axis=1), shell_pick, precision=highest)
     term_one = jnp.sum(part_norm * jnp.sum(weight_rows, axis=1)[:, None], axis=0)
     term_three = jnp.sum(ctf_part * ref_norm, axis=0)
+    images = make_images(planes, ctf_pix, cosines, sine_rows)
     local_sums = jnp.einsum("itj,itpk->jpk", post_half, images, preferred_element_type=jnp.float32)
     term_two = -2.0 * jnp.dot(jnp.sum(local_sums * refs_wide, axis=(0, 1)), shell_pick, precision=highest)
     terms = term_one + term_two + term_three

time: 88.5 us -> 94.7 us (1.070)
  Pallas kernels: 50 us -> 56.3 us
  matrix products: 14.7 us -> 13 us
  local copies, waits for them, and re-layouts: 12.8 us -> 13.8 us
    pallas_call x1, Pallas kernels: 17.6 us -> 23.8 us  [local_scores(): pl.pallas_call(functools.partial(_score_kernel, orient_n), out_shape=(jax...]
    cos x1 -> x0, local copies, waits for them, and re-layouts: 2.8 us -> none  [on_device(): cosines = jnp.cos(phases)]
    sin x0 -> x1, local copies, waits for them, and re-layouts: none -> 2.63 us  [on_device(): sine_rows = jnp.sin(phases)]
    squeeze x0 -> x2, local copies, waits for them, and re-layouts: none -> 1.71 us  [the longest x1 0.86 us: on_device(): planes[:, 1]]
    dot_general x1, matrix products: 2.75 us -> 1.09 us  [on_device(): jnp.einsum('itj,itpk->jpk', post_half, images, preferred_element_type=jnp...]
    dot_general x1 -> x0, matrix products: 1.37 us -> none  [on_device(): jnp.einsum('itpk,jpk->itj', images, weighted, preferred_element_type=jnp....]
    reduce_sum x1, other arithmetic: 0.31 us -> 1.43 us  [on_device(): jnp.sum(refs_wide * refs_wide, axis=1)]
    unnamed x28 -> x33, local copies, waits for them, and re-layouts: 3.47 us -> 2.83 us
where the time goes in v7:
time: 94.7 us; the launch traced here: 94.2 us
  Pallas kernels  56.3 us (59%)
  local copies, waits for them, and re-layouts  13.8 us (15%)
  matrix products  13 us (14%)
  other arithmetic  10.1 us (11%)
    pallas_call x1, Pallas kernels, spread(): pl.pallas_call(functools.partial(_spread_kernel, dom_n, orient_n, width),...  32.5 us
    pallas_call x1, Pallas kernels, local_scores(): pl.pallas_call(functools.partial(_score_kernel, orient_n), out_shape=(jax...  23.8 us
    another operation x2, other arithmetic  4.92 us
    unnamed x33, local copies, waits for them, and re-layouts  2.83 us
    sin x1, local copies, waits for them, and re-layouts, on_device(): sine_rows = jnp.sin(phases)  2.63 us
    reshape x2, local copies, waits for them, and re-layouts, on_device(): post_all = half_all.reshape(dom_size * part_dev, trans_count, ori_dev)  2.58 us
    dot_general x1, matrix products, on_device(): jnp.einsum('itj,itpk->jpk', post_all, col_images, preferred_element_type=...  2.28 us

profile of v7, /device:TPU:1, one launch (start us, length us, event | category | flops | bytes accessed | tf_op | source)
XLA Modules:
  0.0 94.2 jit_solution(15234436179539130152)
XLA Ops:
  0.7 0.7 copy-done
  1.4 1.0 %fusion.37 = f32[256,64]{0,1:T(8,128)S(1)} fusion(f32[64,64]{1,0:T(8,128)S(1)} %copy-done, s32[256]{0:T(256)} %param.12), kind=kOutput, calls=%fused_computation.52 | convolution fusion | flops 12599296 | bytes 82944 | tf_op jit(solution)/shard_map/dot_general | solution.py:326
  2.4 1.5 %fusion.11 = f32[1,8192]{1,0:T(1,128)S(1)} fusion(s32[8192]{0:T(1024)} %param.14, f32[64]{0:T(128)} %param.15), kind=kOutput, calls=%fused_computation.17 | convolution fusion | flops 6815744 | bytes 65792 | tf_op jit(solution)/shard_map/dot_general | solution.py:329
  3.9 1.4 %fusion.27 = (f32[16,8192]{1,0:T(8,128)S(1)}, bf16[16,2,8192]{2,0,1:T(8,128)(2,1)S(1)}) fusion(bf16[16,2,8192]{2,1,0:T(2,128)(2,1)} %param.9, f32[8192]{0:T(1024)S(1)} %bitcast.64), kind=kLoop, calls=%fused_computation.33 | loop fusion | flops 1179648 | bytes 1605632 | tf_op jit(solution)/shard_map/reduce_sum | solution.py:332
  5.3 1.1 %fusion.10 = f32[16,64]{1,0:T(8,128)S(1)} fusion(f32[16,8192]{1,0:T(8,128)S(1)} %get-tuple-element.36, s32[8192]{0:T(1024)S(1)} %copy-done.13), kind=kOutput, calls=%fused_computation.16 | convolution fusion | flops 101187584 | bytes 561152 | tf_op jit(solution)/shard_map/dot_general | solution.py:332
  6.4 0.9 convolution_multiply_fusion.1.quad_ref
  7.3 1.5 %fusion.12.ctf_ref = f32[8,8192]{1,0:T(8,128)} fusion(s32[8192]{0:T(1024)S(1)} %copy-done.13, f32[256,64]{0,1:T(8,128)S(1)} %fusion.37, s32[]{:T(128)S(6)} %select_n.8), kind=kOutput, calls=%fused_computation.18 | convolution fusion | flops 50855936 | bytes 327684 | tf_op jit(solution)/shard_map/dot_general | solution.py:328
  8.8 2.6 %fusion.62 = (f32[16,8192]{1,0:T(8,128)}, f32[16,8192]{1,0:T(8,128)}) fusion(f32[16,8192]{1,0:T(8,128)S(1)} %copy-done.9), kind=kLoop, calls=%fused_computation.88 | loop fusion | bytes 1572864 | tf_op jit(solution)/shard_map/sin | solution.py:338
  11.5 0.8 slice_bitcast_fusion
  12.5 0.9 slice_bitcast_fusion.2
  13.4 23.8 %shard_map.111 = (f32[16,8,16]{2,1,0:T(8,128)}, f32[16,8,128]{2,1,0:T(8,128)}) custom-call(f32[8,8192]{1,0:T(8,128)} %get-tuple-element.43.real_ref, f32[8,8192]{1,0:T(8,128)} %get-tuple-element.42.imag_ref, f32[8,8192]{1,0:T(8,128)} %fusion.12.ctf_ref, f32[16,8192]{1,0:T(8,128)} %get-tuple-element.41.cos_ref, f32[16,8192]{1,0:T(8,128)} %get-tuple-element.40.sin_ref, ...), custom_call_target="tpu_custom_call" | custom-call | tf_op jit(solution)/shard_map/pallas_call | solution.py:158
  37.2 1.1 %slice_reduce_fusion.1 = (f32[8]{0:T(128)S(1)}, f32[16,8,1]{2,1,0:T(8,128)S(1)}, f32[16,8,1]{2,1,0:T(8,128)S(1)}) fusion(f32[16,8,128]{2,1,0:T(8,128)} %get-tuple-element.11), kind=kLoop, calls=%fused_computation.85 | loop fusion | flops 120 | bytes 2080 | tf_op jit(solution)/shard_map/reduce_max | solution.py:347
  38.8 1.1 %fusion.60 = (f32[8]{0:T(128)S(1)}, f32[16,8,16]{2,1,0:T(8,128)S(1)}) fusion(f32[8]{0:T(128)S(1)} %fusion.51, f32[16,8,16]{2,1,0:T(8,128)} %get-tuple-element.10, f32[8]{0:T(128)S(1)} %get-tuple-element.44), kind=kLoop, calls=%fused_computation.86 | loop fusion | flops 6136 | bytes 16480 | tf_op jit(solution)/shard_map/reduce_sum | solution.py:355
  39.9 1.3 %multiply_convert_fusion.3 = (bf16[8,16,1,8192]{3,0,1,2:T(8,128)(2,1)S(1)}, bf16[8,16,1,8192]{3,0,1,2:T(8,128)(2,1)S(1)}) fusion(f32[16,8192]{1,0:T(8,128)S(1)} %copy-done.1, f32[8,8192]{1,0:T(8,128)S(1)} %copy-done.4, f32[16,8192]{1,0:T(8,128)S(1)} %copy-done.2, f32[8,8192]{1,0:T(8,128)S(1)} %copy-done.5, f32[8,8192]{1,0:T(8,128)S(1)} %copy-done.6), kind=kLoop, calls=%fused_computation.12 | loop fusion | flops 10485760 | bytes 6029312 | tf_op jit(solution)/shard_map/convert.3
  41.2 1.1 %fusion.13 = f32[8192]{0:T(1024)S(1)} fusion(bf16[8,16,1,8192]{3,0,1,2:T(8,128)(2,1)S(1)} %get-tuple-element.31, bf16[8,16,1,8192]{3,0,1,2:T(8,128)(2,1)S(1)} %get-tuple-element.30, bf16[16,2,8192]{2,1,0:T(2,128)(2,1)S(1)} %copy-done.10, bf16[8,16,16]{2,0,1:T(8,128)(2,1)S(1)} %bitcast_convert_fusion), kind=kOutput, calls=%fused_computation.21 | convolution fusion | flops 76275712 | bytes 4755456 | tf_op jit(solution)/shard_map/itj,itpk->jpk/dot_general | solution.py:358
  42.5 1.1 %fusion.21 = f32[64]{0:T(128)S(1)} fusion(f32[8,8192]{1,0:T(8,128)S(1)} %multiply_reduce_fusion, s32[8192]{0:T(1024)S(1)} %copy-done.13, f32[8]{0:T(128)S(1)} %get-tuple-element.28), kind=kOutput, calls=%fused_computation.27 | convolution fusion | flops 50856896 | bytes 295200 | tf_op jit(solution)/shard_map/dot_general | solution.py:354
  43.8 1.0 %fusion.25 = f32[64]{0:T(128)S(1)} fusion(f32[64]{0:T(128)S(1)} %fusion.19, f32[64]{0:T(128)S(1)} %fusion.21, f32[8192,1]{0,1:T(1,128)S(1)} %bitcast.65, s32[8192]{0:T(1024)S(1)} %copy-done.13), kind=kOutput, calls=%fused_computation.31 | convolution fusion | flops 6815936 | bytes 66304 | tf_op jit(solution)/shard_map/dot_general | solution.py:359
  45.0 0.7 select_maximum_fusion.small_ref
  45.7 0.7 reshape.92.half_ref
  46.3 0.8 reshape.94.part_ref
  47.1 32.5 %shard_map.112 = (bf16[32,16,128]{2,1,0:T(8,128)(2,1)}, f32[32,8,128]{2,1,0:T(8,128)}, bf16[32,16,256]{2,1,0:T(8,128)(2,1)}, f32[16,8,128]{2,1,0:T(8,128)}) custom-call(bf16[16,128]{1,0:T(8,128)(2,1)} %reshape.92.half_ref, f32[8,128]{1,0:T(8,128)} %select_maximum_fusion.small_ref, bf16[16,8192]{1,0:T(8,128)(2,1)} %reshape.94.part_ref), custom_call_target="tpu_custom_call" | custom-call | tf_op jit(solution)/shard_map/pallas_call | solution.py:273
  79.7 1.2 %reshape.97 = f32[256,2,256]{2,1,0:T(2,128)S(1)} reshape(bf16[32,16,256]{2,1,0:T(8,128)(2,1)} %get-tuple-element.13) | data formatting | bytes 786432 | tf_op jit(solution)/shard_map/convert_element_type | solution.py:384
  80.9 0.4 fusion.61
  81.3 0.8 copy_bitcast_fusion
  82.7 3.7 %multiply_convert_fusion.1 = (bf16[256,16,1,256]{3,0,1,2:T(8,128)(2,1)S(1)}, bf16[256,16,1,256]{3,0,1,2:T(8,128)(2,1)}) fusion(f32[16,256]{1,0:T(8,128)S(1)} %get-tuple-element.47, f32[256,256]{1,0:T(8,128)S(1)} %get-tuple-element.49, f32[16,256]{1,0:T(8,128)S(1)} %get-tuple-element.48, f32[256,256]{1,0:T(8,128)} %get-tuple-element.50, f32[256,256]{1,0:T(8,128)S(1)} %fusion.40), kind=kLoop, calls=%fused_computation.10 | loop fusion | flops 10485760 | bytes 5013504 | tf_op jit(solution)/shard_map/convert.1
  86.3 1.7 %reshape.95 = bf16[256,16,16]{2,1,0:T(8,128)(2,1)S(1)} reshape(bf16[32,16,128]{2,1,0:T(8,128)(2,1)} %get-tuple-element.12) | data formatting | bytes 262144 | tf_op jit(solution)/shard_map/reshape | solution.py:370
  88.1 0.8 copy.33
  88.9 2.3 %fusion.16 = f32[16,2,256]{2,0,1:T(8,128)S(1)} fusion(bf16[256,16,1,256]{3,0,1,2:T(8,128)(2,1)} %get-tuple-element.33, bf16[256,16,1,256]{3,0,1,2:T(8,128)(2,1)S(1)} %get-tuple-element.32, bf16[256,16,16]{0,2,1:T(8,128)(2,1)S(1)} %copy.33), kind=kOutput, calls=%fused_computation.22 | convolution fusion | flops 75497472 | bytes 4358144 | tf_op jit(solution)/shard_map/itj,itpk->jpk/dot_general | solution.py:386
  91.2 0.6 copy.35
  91.9 1.0 %fusion.33 = f32[16,64]{1,0:T(8,128)} fusion(f32[32,8,128]{2,1,0:T(8,128)S(1)} %copy-done.11, f32[256,64]{0,1:T(8,128)S(1)} %fusion.37), kind=kOutput, calls=%fused_computation.47 | convolution fusion | flops 3162112 | bytes 200704 | tf_op jit(solution)/shard_map/dot_general | solution.py:377
  92.9 0.6 div.44
  93.5 0.6 copy.34
  (44 shorter events, 1.9 us)
Async XLA Ops:
  0.6 0.8 copy-start
  0.6 4.7 %copy-start.13 = (s32[8192]{0:T(1024)S(1)}, s32[8192]{0:T(1024)}, u32[]{:S(2)}) copy-start(s32[8192]{0:T(1024)} %param.14) | copy-start | bytes 98308
  0.7 5.8 %copy-start.14 = (f32[64]{0:T(128)S(1)}, f32[64]{0:T(128)}, u32[]{:S(2)}) copy-start(f32[64]{0:T(128)} %param.15) | copy-start | bytes 772
  0.7 8.2 %copy-start.9 = (f32[16,8192]{1,0:T(8,128)S(1)}, f32[16,8192]{1,0:T(8,128)}, u32[]{:S(2)}) copy-start(f32[16,8192]{1,0:T(8,128)} %param.10) | copy-start | bytes 1572868
  5.3 7.0 %copy-start.3 = (bf16[8,2,8192]{2,1,0:T(2,128)(2,1)S(1)}, bf16[8,2,8192]{2,1,0:T(2,128)(2,1)}, u32[]{:S(2)}) copy-start(bf16[8,2,8192]{2,1,0:T(2,128)(2,1)} %param.8) | copy-start | bytes 786436
  12.5 27.4 %copy-start.1 = (f32[16,8192]{1,0:T(8,128)S(1)}, f32[16,8192]{1,0:T(8,128)}, u32[]{:S(2)}) copy-start(f32[16,8192]{1,0:T(8,128)} %get-tuple-element.40.sin_ref) | copy-start | bytes 1572868
  12.5 27.4 %copy-start.2 = (f32[16,8192]{1,0:T(8,128)S(1)}, f32[16,8192]{1,0:T(8,128)}, u32[]{:S(2)}) copy-start(f32[16,8192]{1,0:T(8,128)} %get-tuple-element.41.cos_ref) | copy-start | bytes 1572868
  12.5 27.4 %copy-start.6 = (f32[8,8192]{1,0:T(8,128)S(1)}, f32[8,8192]{1,0:T(8,128)}, u32[]{:S(2)}) copy-start(f32[8,8192]{1,0:T(8,128)} %fusion.12.ctf_ref) | copy-start | bytes 786436
  13.4 26.5 %copy-start.4 = (f32[8,8192]{1,0:T(8,128)S(1)}, f32[8,8192]{1,0:T(8,128)}, u32[]{:S(2)}) copy-start(f32[8,8192]{1,0:T(8,128)} %get-tuple-element.42.imag_ref) | copy-start | bytes 786436
  13.4 26.5 %copy-start.5 = (f32[8,8192]{1,0:T(8,128)S(1)}, f32[8,8192]{1,0:T(8,128)}, u32[]{:S(2)}) copy-start(f32[8,8192]{1,0:T(8,128)} %get-tuple-element.43.real_ref) | copy-start | bytes 786436
  39.8 3.7 %copy-start.7 = (f32[16,8,16]{2,1,0:T(8,128)}, f32[16,8,16]{2,1,0:T(8,128)S(1)}, u32[]{:S(2)}) copy-start(f32[16,8,16]{2,1,0:T(8,128)S(1)} %get-tuple-element.29) | copy-start | bytes 24580
  39.9 1.3 %copy-start.10 = (bf16[16,2,8192]{2,1,0:T(2,128)(2,1)S(1)}, bf16[16,2,8192]{2,1,0:T(2,128)(2,1)}, u32[]{:S(2)}) copy-start(bf16[16,2,8192]{2,1,0:T(2,128)(2,1)} %param.9) | copy-start | bytes 1572868
  88.9 2.9 %copy-start.11 = (f32[32,8,128]{2,1,0:T(8,128)S(1)}, f32[32,8,128]{2,1,0:T(8,128)}, u32[]{:S(2)}) copy-start(f32[32,8,128]{2,1,0:T(8,128)} %get-tuple-element.14) | copy-start | bytes 393220
  88.9 3.9 %copy-start.12 = (f32[16,8,128]{2,1,0:T(8,128)S(1)}, f32[16,8,128]{2,1,0:T(8,128)}, u32[]{:S(2)}) copy-start(f32[16,8,128]{2,1,0:T(8,128)} %get-tuple-element.15) | copy-start | bytes 196612
  88.9 4.6 %copy-start.8 = (f32[16,8,16]{2,1,0:T(8,128)S(1)}, f32[16,8,16]{2,1,0:T(8,128)}, u32[]{:S(2)}) copy-start(f32[16,8,16]{2,1,0:T(8,128)} %copy-done.7) | copy-start | bytes 24580

commit v8 on v6

--- a/solution.py
+++ b/solution.py
@@ -80,6 +80,101 @@
         + [pltpu.SemaphoreType.DMA((count, n)), pltpu.SemaphoreType.DMA((count, n))],
         compiler_params=pltpu.CompilerParams(collective_id=collective_id, has_side_effects=True),
     )(*[x for x, _ in payloads])
+
+
+def _stats_kernel(dom_n, orient_n, width, stats_ref, part_ref, stats_out, part_out,
+                  stats_held, part_held, orient_send, orient_recv, dom_send, dom_recv):
+    me = lax.axis_index("dom")
+    mine = lax.axis_index("orient")
+    barrier = pltpu.get_barrier_semaphore()
+
+    def greet_dom(k, carry):
+        peer = lax.rem(me + k, dom_n)
+        pl.semaphore_signal(barrier, inc=1, device_id={"dom": peer}, device_id_type=MESH_ID)
+        return carry
+
+    def greet_orient(k, carry):
+        peer = lax.rem(mine + k, orient_n)
+        pl.semaphore_signal(barrier, inc=1, device_id={"orient": peer}, device_id_type=MESH_ID)
+        return carry
+
+    lax.fori_loop(1, orient_n, greet_orient, 0)
+    lax.fori_loop(1, dom_n, greet_dom, 0)
+    pl.semaphore_wait(barrier, dom_n + orient_n - 2)
+
+    def orient_copy(k):
+        peer = lax.rem(mine + k, orient_n)
+        return pltpu.make_async_remote_copy(
+            src_ref=stats_ref,
+            dst_ref=stats_held.at[mine],
+            send_sem=orient_send.at[k],
+            recv_sem=orient_recv.at[k],
+            device_id={"orient": peer},
+            device_id_type=MESH_ID,
+        )
+
+    def columns(peer):
+        return part_ref.at[:, pl.ds(pl.multiple_of(peer * width, width), width)]
+
+    def dom_copy(k):
+        peer = lax.rem(me + k, dom_n)
+        return pltpu.make_async_remote_copy(
+            src_ref=columns(peer),
+            dst_ref=part_held.at[me],
+            send_sem=dom_send.at[k],
+            recv_sem=dom_recv.at[k],
+            device_id={"dom": peer},
+            device_id_type=MESH_ID,
+        )
+
+    def orient_start(k, carry):
+        orient_copy(k).start()
+        return carry
+
+    def dom_start(k, carry):
+        dom_copy(k).start()
+        return carry
+
+    lax.fori_loop(1, orient_n, orient_start, 0)
+    lax.fori_loop(1, dom_n, dom_start, 0)
+    stats_held[mine] = stats_ref[...]
+    part_held[me] = columns(me)[...]
+
+    def orient_finish(k, carry):
+        orient_copy(k).wait()
+        return carry
+
+    def dom_finish(k, carry):
+        dom_copy(k).wait()
+        return carry
+
+    lax.fori_loop(1, orient_n, orient_finish, 0)
+    lax.fori_loop(1, dom_n, dom_finish, 0)
+    stats_out[...] = stats_held[...]
+    part_out[...] = part_held[...]
+
+
+def stats_and_columns(stats, part_rows, dom_n, orient_n, width, collective_id):
+    shapes = (
+        jax.ShapeDtypeStruct((orient_n,) + stats.shape, stats.dtype),
+        jax.ShapeDtypeStruct((dom_n, part_rows.shape[0], width), part_rows.dtype),
+    )
+    vmem = pl.BlockSpec(memory_space=pltpu.VMEM)
+    return pl.pallas_call(
+        functools.partial(_stats_kernel, dom_n, orient_n, width),
+        out_shape=shapes,
+        in_specs=[vmem] * 2,
+        out_specs=(vmem, vmem),
+        scratch_shapes=[
+            pltpu.VMEM(shapes[0].shape, shapes[0].dtype),
+            pltpu.VMEM(shapes[1].shape, shapes[1].dtype),
+            pltpu.SemaphoreType.DMA((orient_n,)),
+            pltpu.SemaphoreType.DMA((orient_n,)),
+            pltpu.SemaphoreType.DMA((dom_n,)),
+            pltpu.SemaphoreType.DMA((dom_n,)),
+        ],
+        compiler_params=pltpu.CompilerParams(collective_id=collective_id, has_side_effects=True),
+    )(stats, part_rows)
 
 
 def _spread_kernel(dom_n, orient_n, half_ref, small_ref,
@@ -219,9 +314,6 @@
     width = pixels // dom_size
     dom_index = lax.axis_index("dom")
 
-    part_rows = particles.reshape(part_dev * 2, dom_size, width)
-    columns = lax.all_to_all(part_rows, "dom", 1, 0, tiled=True).reshape(dom_size, part_dev * 2, width)
-
     shell_pick = (shell_index[:, None] == jnp.arange(shells, dtype=jnp.int32)[None, :]).astype(
         jnp.float32
     )
@@ -249,7 +341,14 @@
     local_peak = jnp.max(scores, axis=(1, 2))
     local_total = jnp.sum(jnp.exp(scores - local_peak[:, None, None]), axis=(1, 2))
 
-    (stats,) = exchange([(pad_rows(jnp.stack([local_peak, local_total]), 128), None)], "orient", orient_size, 1)
+    stats, columns = stats_and_columns(
+        pad_rows(jnp.stack([local_peak, local_total]), 128),
+        particles.reshape(part_dev * 2, pixels),
+        dom_size,
+        orient_size,
+        width,
+        1,
+    )
     peaks = stats[:, 0, :part_dev]
     totals = stats[:, 1, :part_dev]
     peak = jnp.max(peaks, axis=0)

time: 93.9 us -> 84.1 us (0.90)
  starting transfers between devices: 10.5 us -> 0 us
  Pallas kernels: 43.5 us -> 50.8 us
  other arithmetic: 11.9 us -> 7.38 us
  matrix products: 14.7 us -> 13.2 us
    all_to_all x1 -> x0, starting transfers between devices: 10.5 us -> none  [on_device(): lax.all_to_all(part_rows, 'dom', 1, 0, tiled=True)]
    pallas_call x1, Pallas kernels: 17.1 us -> 25.6 us  [stats_and_columns(): pl.pallas_call(functools.partial(_stats_kernel, dom_n, orient_n, width),...]
    reshape x2 -> x1, local copies, waits for them, and re-layouts: 2.06 us -> 0.8 us  [on_device(): particles.reshape(part_dev * 2, pixels)]
    pallas_call x1, Pallas kernels: 26.5 us -> 25.2 us  [spread(): pl.pallas_call(functools.partial(_spread_kernel, dom_n, orient_n), out_sh...]
    another operation x2, other arithmetic: 3.7 us -> 2.67 us
    convert_element_type x1, other arithmetic: 1.17 us -> 0.16 us  [on_device(): planes = particles.astype(jnp.float32)]
    cos x1, local copies, waits for them, and re-layouts: 1.84 us -> 2.8 us  [on_device(): cosines = jnp.cos(phases)]
    dot_general x1, matrix products: 2.02 us -> 1.06 us  [on_device(): jnp.dot(jnp.sum(planes * planes, axis=1), shell_pick, precision=highest)]
  transfers between devices with their start and end apart: 1 -> 0, of which waited for: 0 -> 0; matrix products, arithmetic and copies ran while one was open for 33% -> 0% of each run, Pallas kernels for 47% -> 0%
where the time goes in v8:
time: 84.1 us; the launch traced here: 83.7 us
  Pallas kernels  50.8 us (60%)
  matrix products  13.2 us (16%)
  local copies, waits for them, and re-layouts  11.3 us (13%)
  other arithmetic  7.38 us (9%)
  between operations  0.96 us (1%)
    pallas_call x1, Pallas kernels, stats_and_columns(): pl.pallas_call(functools.partial(_stats_kernel, dom_n, orient_n, width),...  25.6 us
    pallas_call x1, Pallas kernels, spread(): pl.pallas_call(functools.partial(_spread_kernel, dom_n, orient_n), out_sh...  25.2 us
    cos x1, local copies, waits for them, and re-layouts, on_device(): cosines = jnp.cos(phases)  2.8 us
    reshape x2, local copies, waits for them, and re-layouts, on_device(): post_all = half_all.reshape(dom_size * part_dev, trans_count, ori_dev)  2.77 us
    dot_general x1, matrix products, on_device(): jnp.einsum('itj,itpk->jpk', post_half, images, preferred_element_type=jnp...  2.75 us
    unnamed x30, local copies, waits for them, and re-layouts  2.75 us
    another operation x2, other arithmetic  2.67 us

profile of v8, /device:TPU:1, one launch (start us, length us, event | category | flops | bytes accessed | tf_op | source)
XLA Modules:
  0.0 83.7 jit_solution(7322062683520966849)
XLA Ops:
  0.7 0.7 copy-done
  1.4 1.0 %fusion.40 = f32[256,64]{0,1:T(8,128)S(1)} fusion(f32[64,64]{1,0:T(8,128)S(1)} %copy-done, s32[256]{0:T(256)} %param.12), kind=kOutput, calls=%fused_computation.55 | convolution fusion | flops 12599296 | bytes 82944 | tf_op jit(solution)/shard_map/dot_general | solution.py:323
  2.4 1.6 %fusion.10 = f32[8,8192]{1,0:T(8,128)S(1)} fusion(s32[8192]{0:T(1024)} %param.14, f32[256,64]{0,1:T(8,128)S(1)} %fusion.40, s32[]{:T(128)S(6)} %select_n.12), kind=kOutput, calls=%fused_computation.17 | convolution fusion | flops 50855936 | bytes 327684 | tf_op jit(solution)/shard_map/dot_general | solution.py:325
  3.9 2.8 %fusion.66 = (f32[16,8192]{1,0:T(8,128)S(1)}, f32[16,8192]{1,0:T(8,128)S(1)}) fusion(f32[16,8192]{1,0:T(8,128)} %param.10), kind=kLoop, calls=%fused_computation.95 | loop fusion | bytes 1572864 | tf_op jit(solution)/shard_map/cos | solution.py:334
  7.0 1.3 %multiply_convert_fusion.3 = (bf16[8,16,1,8192]{3,1,2,0:T(8,128)(2,1)S(1)}, bf16[8,16,1,8192]{3,1,2,0:T(8,128)(2,1)S(1)}) fusion(f32[16,8192]{1,0:T(8,128)S(1)} %get-tuple-element.38, f32[8,8192]{1,0:T(8,128)S(1)} %get-tuple-element.36, f32[16,8192]{1,0:T(8,128)S(1)} %get-tuple-element.37, f32[8,8192]{1,0:T(8,128)S(1)} %get-tuple-element.35, ...), kind=kLoop, calls=%fused_computation.10 | loop fusion | flops 10485760 | bytes 6029312 | tf_op jit(solution)/shard_map/convert.3
  8.3 0.3 fusion.26
  8.6 1.1 %fusion.8 = f32[16,64]{1,0:T(8,128)S(1)} fusion(f32[16,8192]{1,0:T(8,128)S(1)} %fusion.26, s32[8192]{0:T(1024)S(1)} %copy-done.9), kind=kOutput, calls=%fused_computation.15 | convolution fusion | flops 101187584 | bytes 561152 | tf_op jit(solution)/shard_map/dot_general | solution.py:329
  10.0 0.8 fusion.9
  10.8 1.4 %fusion.67 = (f32[8]{0:T(128)S(1)}, f32[8,16,16]{2,1,0:T(8,128)S(1)}) fusion(f32[8,16]{1,0:T(8,128)S(1)} %convolution_multiply_fusion.1, f32[8192]{0:T(1024)S(1)} %bitcast.77, bf16[16,2,8192]{2,1,0:T(2,128)(2,1)S(1)} %copy-done.3, bf16[8,16,1,8192]{3,1,2,0:T(8,128)(2,1)S(1)} %get-tuple-element.30, bf16[8,16,1,8192]{3,1,2,0:T(8,128)(2,1)S(1)} %get-tuple-element.29, ...), kind=kOutput, calls=%fused_computation.96 | convolution fusion | flops 69998584 | bytes 4760224 | tf_op jit(solution)/shard_map/itpk,jpk->itj/dot_general | solution.py:338
  12.2 0.6 copy-done.6
  13.0 0.6 select_maximum_fusion.1.stats_ref
  13.6 0.8 reshape.95.part_ref
  14.4 25.6 %shard_map.111 = (f32[16,8,128]{2,1,0:T(8,128)}, bf16[32,16,256]{2,1,0:T(8,128)(2,1)}) custom-call(f32[8,128]{1,0:T(8,128)} %select_maximum_fusion.1.stats_ref, bf16[16,8192]{1,0:T(8,128)(2,1)} %reshape.95.part_ref), custom_call_target="tpu_custom_call" | custom-call | tf_op jit(solution)/shard_map/pallas_call | solution.py:163
  40.0 1.0 %slice_reduce_fusion.1 = (f32[8]{0:T(128)S(1)}, f32[16,1,8]{2,1,0:T(1,128)S(1)}, f32[16,1,8]{2,1,0:T(1,128)S(1)}) fusion(f32[16,8,128]{2,1,0:T(8,128)} %get-tuple-element.9), kind=kLoop, calls=%fused_computation.92 | loop fusion | flops 120 | bytes 2080 | tf_op jit(solution)/shard_map/reduce_max | solution.py:354
  41.2 1.1 %fusion.64 = (f32[8]{0:T(128)S(1)}, f32[8,16]{1,0:T(8,128)S(1)}, f32[8,16,16]{2,1,0:T(8,128)S(1)}) fusion(f32[8]{0:T(128)S(1)} %fusion.54, f32[8,16,16]{2,1,0:T(8,128)} %copy-done.6, f32[8]{0:T(128)S(1)} %get-tuple-element.39), kind=kLoop, calls=%fused_computation.93 | loop fusion | flops 8056 | bytes 16992 | tf_op jit(solution)/shard_map/reduce_sum | solution.py:362
  42.3 0.6 copy-done.5
  43.0 2.8 %fusion.11 = f32[8192]{0:T(1024)S(1)} fusion(bf16[8,16,1,8192]{3,1,2,0:T(8,128)(2,1)} %copy-done.2, bf16[8,16,1,8192]{3,1,2,0:T(8,128)(2,1)S(1)} %get-tuple-element.29, bf16[16,2,8192]{2,1,0:T(2,128)(2,1)} %param.9, bf16[8,16,16]{2,1,0:T(8,128)(2,1)S(1)} %convert_element_type.29), kind=kOutput, calls=%fused_computation.20 | convolution fusion | flops 76275712 | bytes 4755456 | tf_op jit(solution)/shard_map/itj,itpk->jpk/dot_general | solution.py:364
  46.2 1.1 %fusion.20 = f32[64]{0:T(128)S(1)} fusion(f32[8,8192]{1,0:T(8,128)S(1)} %multiply_reduce_fusion, s32[8192]{0:T(1024)S(1)} %copy-done.10, f32[8]{0:T(128)S(1)} %get-tuple-element.26), kind=kOutput, calls=%fused_computation.29 | convolution fusion | flops 50856896 | bytes 295200 | tf_op jit(solution)/shard_map/dot_general | solution.py:361
  47.2 1.1 %fusion.24 = f32[64]{0:T(128)S(1)} fusion(f32[64]{0:T(128)S(1)} %fusion.18, f32[64]{0:T(128)S(1)} %fusion.20, f32[8192,1]{0,1:T(1,128)S(1)} %bitcast.76, s32[8192]{0:T(1024)S(1)} %copy-done.10), kind=kOutput, calls=%fused_computation.33 | convolution fusion | flops 6815936 | bytes 66304 | tf_op jit(solution)/shard_map/dot_general | solution.py:365
  48.4 0.7 select_maximum_fusion.small_ref
  49.1 0.7 reshape.96.half_ref
  49.8 25.2 %shard_map.112 = (bf16[32,16,128]{2,1,0:T(8,128)(2,1)}, f32[32,8,128]{2,1,0:T(8,128)}, f32[16,8,128]{2,1,0:T(8,128)}) custom-call(bf16[16,128]{1,0:T(8,128)(2,1)} %reshape.96.half_ref, f32[8,128]{1,0:T(8,128)} %select_maximum_fusion.small_ref), custom_call_target="tpu_custom_call" | custom-call | tf_op jit(solution)/shard_map/pallas_call | solution.py:271
  75.0 1.9 %reshape.98 = bf16[256,16,16]{2,1,0:T(8,128)(2,1)S(1)} reshape(bf16[32,16,128]{2,1,0:T(8,128)(2,1)} %get-tuple-element.10) | data formatting | bytes 262144 | tf_op jit(solution)/shard_map/reshape | solution.py:374
  76.9 0.8 copy.29
  78.0 0.4 fusion.65
  78.5 0.3 iota_compare_fusion
  78.8 0.3 fusion.43
  79.1 1.4 %multiply_convert_fusion.1 = (bf16[256,16,1,256]{3,0,1,2:T(8,128)(2,1)S(1)}, bf16[256,16,1,256]{3,0,1,2:T(8,128)(2,1)S(1)}) fusion(f32[16,256]{1,0:T(8,128)S(1)} %get-tuple-element.44, f32[256,256]{1,0:T(8,128)S(1)} %get-tuple-element.46, f32[16,256]{1,0:T(8,128)S(1)} %get-tuple-element.45, f32[256,256]{1,0:T(8,128)S(1)} %get-tuple-element.47, ...), kind=kLoop, calls=%fused_computation.8 | loop fusion | flops 10485760 | bytes 5013504 | tf_op jit(solution)/shard_map/convert.1
  80.6 0.8 fusion.15
  81.4 0.6 copy.30
  82.0 1.0 %fusion.36 = f32[16,64]{1,0:T(8,128)} fusion(f32[32,8,128]{2,1,0:T(8,128)S(1)} %copy-done.7, f32[256,64]{0,1:T(8,128)S(1)} %fusion.40), kind=kOutput, calls=%fused_computation.50 | convolution fusion | flops 3162112 | bytes 200704 | tf_op jit(solution)/shard_map/dot_general | solution.py:381
  83.1 0.6 div.40
  (42 shorter events, 2.0 us)
Async XLA Ops:
  0.6 0.8 copy-start
  0.6 6.1 %copy-start.1 = (bf16[8,2,8192]{2,1,0:T(2,128)(2,1)S(1)}, bf16[8,2,8192]{2,1,0:T(2,128)(2,1)}, u32[]{:S(2)}) copy-start(bf16[8,2,8192]{2,1,0:T(2,128)(2,1)} %param.8) | copy-start | bytes 786436
  6.9 1.3 %copy-start.3 = (bf16[16,2,8192]{2,1,0:T(2,128)(2,1)S(1)}, bf16[16,2,8192]{2,1,0:T(2,128)(2,1)}, u32[]{:S(2)}) copy-start(bf16[16,2,8192]{2,1,0:T(2,128)(2,1)} %param.9) | copy-start | bytes 1572868
  7.0 1.6 %copy-start.9 = (s32[8192]{0:T(1024)S(1)}, s32[8192]{0:T(1024)}, u32[]{:S(2)}) copy-start(s32[8192]{0:T(1024)} %param.14) | copy-start | bytes 98308
  7.0 2.7 %copy-start.13 = (f32[64]{0:T(128)S(1)}, f32[64]{0:T(128)}, u32[]{:S(2)}) copy-start(f32[64]{0:T(128)} %param.15) | copy-start | bytes 772
  8.3 3.9 %copy-start.2 = (bf16[8,16,1,8192]{3,1,2,0:T(8,128)(2,1)}, bf16[8,16,1,8192]{3,1,2,0:T(8,128)(2,1)S(1)}, u32[]{:S(2)}) copy-start(bf16[8,16,1,8192]{3,1,2,0:T(8,128)(2,1)S(1)} %get-tuple-element.30) | copy-start | bytes 6291460
  8.3 2.5 %copy-start.12 = (s32[8,16]{1,0:T(8,128)S(1)}, s32[8,16]{1,0:T(8,128)}, u32[]{:S(2)}) copy-start(s32[8,16]{1,0:T(8,128)} %param.11) | copy-start | bytes 1540
  12.2 0.6 copy-start.6
  42.3 0.6 copy-start.5
  43.0 3.2 %copy-start.10 = (s32[8192]{0:T(1024)S(1)}, s32[8192]{0:T(1024)}, u32[]{:S(2)}) copy-start(s32[8192]{0:T(1024)} %param.14) | copy-start | bytes 98308
  45.7 32.0 %copy-start.4 = (bf16[32,16,256]{2,1,0:T(8,128)(2,1)S(1)}, bf16[32,16,256]{2,1,0:T(8,128)(2,1)}, u32[]{:S(2)}) copy-start(bf16[32,16,256]{2,1,0:T(8,128)(2,1)} %get-tuple-element.11) | copy-start | bytes 786436
  76.9 1.6 %copy-start.11 = (s32[8192]{0:T(1024)S(1)}, s32[8192]{0:T(1024)}, u32[]{:S(2)}) copy-start(s32[8192]{0:T(1024)} %param.14) | copy-start | bytes 98308
  80.5 1.5 %copy-start.7 = (f32[32,8,128]{2,1,0:T(8,128)S(1)}, f32[32,8,128]{2,1,0:T(8,128)}, u32[]{:S(2)}) copy-start(f32[32,8,128]{2,1,0:T(8,128)} %get-tuple-element.12) | copy-start | bytes 393220
  80.5 2.4 %copy-start.8 = (f32[16,8,128]{2,1,0:T(8,128)S(1)}, f32[16,8,128]{2,1,0:T(8,128)}, u32[]{:S(2)}) copy-start(f32[16,8,128]{2,1,0:T(8,128)} %get-tuple-element.13) | copy-start | bytes 196612

commit v9 on v8

--- a/solution.py
+++ b/solution.py
@@ -369,9 +369,11 @@
     term_rows = jnp.pad(terms, (0, term_cols * part_dev - shells)).reshape(part_dev, term_cols)
     small = jnp.concatenate([weight_rows, term_rows], axis=1)
     small = jnp.pad(small, ((0, 0), (0, -(-small.shape[1] // 128) * 128 - small.shape[1])))
-    half_rows = post_half.reshape(-1, 128)
+    half_rows = jnp.transpose(post_half, (1, 2, 0)).reshape(trans_count, ori_dev * part_dev)
     half_all, small_all, orient_small = spread(half_rows, small, dom_size, orient_size, 2)
-    post_all = half_all.reshape(dom_size * part_dev, trans_count, ori_dev)
+    post_all = jnp.transpose(
+        half_all.reshape(dom_size, trans_count, ori_dev, part_dev), (1, 2, 0, 3)
+    ).reshape(trans_count, ori_dev, dom_size * part_dev)
     weight_all = small_all[:, :, :ori_dev].reshape(dom_size * part_dev, ori_dev)
     shell_total = jnp.sum(
         orient_small[:, :, ori_dev : ori_dev + term_cols].reshape(orient_size, part_dev * term_cols)[:, :shells],
@@ -388,7 +390,7 @@
     col_planes = columns.reshape(dom_size * part_dev, 2, width).astype(jnp.float32)
     col_images = make_images(col_planes, ctf_cols, cos_cols, sin_cols)
     image_sums = jnp.einsum(
-        "itj,itpk->jpk", post_all, col_images, preferred_element_type=jnp.float32
+        "tji,itpk->jpk", post_all, col_images, preferred_element_type=jnp.float32
     )
 
     divisor = part_dev * dom_size * pixels / shells

time: 84.1 us -> 87.9 us (1.045)
  other arithmetic: 7.38 us -> 10.2 us
    reshape x3 -> x1, local copies, waits for them, and re-layouts: 3.45 us -> 0.67 us  [on_device(): jnp.transpose(post_half, (1, 2, 0)).reshape(trans_count, ori_dev * part_dev)]
    slice x1, local copies, waits for them, and re-layouts: 0.07 us -> 1.36 us  [on_device(): totals = stats[:, 1, :part_dev]]
    pallas_call x0 -> x1, local copies, waits for them, and re-layouts: none -> 1.19 us  [spread(): pl.pallas_call(functools.partial(_spread_kernel, dom_n, orient_n), out_sh...]
    reduce_max x1, other arithmetic: 0.95 us -> 2.04 us  [on_device(): peak = jnp.max(peaks, axis=0)]
    convert_element_type x1, other arithmetic: 0.01 us -> 0.94 us  [on_device(): post_half = posterior.astype(jnp.bfloat16)]
    unnamed x30 -> x34, local copies, waits for them, and re-layouts: 2.75 us -> 2.13 us
where the time goes in v9:
time: 87.9 us; the launch traced here: 87.3 us
  Pallas kernels  50.9 us (58%)
  matrix products  13.3 us (15%)
  local copies, waits for them, and re-layouts  11.8 us (13%)
  other arithmetic  10.2 us (12%)
  between operations  1.01 us (1%)
    pallas_call x1, Pallas kernels, stats_and_columns(): pl.pallas_call(functools.partial(_stats_kernel, dom_n, orient_n, width),...  25.6 us
    pallas_call x1, Pallas kernels, spread(): pl.pallas_call(functools.partial(_spread_kernel, dom_n, orient_n), out_sh...  25.3 us
    cos x1, local copies, waits for them, and re-layouts, on_device(): cosines = jnp.cos(phases)  2.8 us
    dot_general x1, matrix products, on_device(): jnp.einsum('itj,itpk->jpk', post_half, images, preferred_element_type=jnp...  2.79 us
    another operation x2, other arithmetic  2.69 us
    unnamed x34, local copies, waits for them, and re-layouts  2.13 us
    reduce_max x1, other arithmetic, on_device(): peak = jnp.max(peaks, axis=0)  2.04 us

profile of v9, /device:TPU:1, one launch (start us, length us, event | category | flops | bytes accessed | tf_op | source)
XLA Modules:
  0.0 87.3 jit_solution(1134418274267084242)
XLA Ops:
  0.7 0.7 copy-done
  1.4 1.0 %fusion.37 = f32[256,64]{0,1:T(8,128)S(1)} fusion(f32[64,64]{1,0:T(8,128)S(1)} %copy-done, s32[256]{0:T(256)} %param.12), kind=kOutput, calls=%fused_computation.52 | convolution fusion | flops 12599296 | bytes 82944 | tf_op jit(solution)/shard_map/dot_general | solution.py:323
  2.4 1.6 %fusion.10 = f32[8,8192]{1,0:T(8,128)S(1)} fusion(s32[8192]{0:T(1024)} %param.14, f32[256,64]{0,1:T(8,128)S(1)} %fusion.37, s32[]{:T(128)S(6)} %select_n.15), kind=kOutput, calls=%fused_computation.17 | convolution fusion | flops 50855936 | bytes 327684 | tf_op jit(solution)/shard_map/dot_general | solution.py:325
  3.9 2.8 %fusion.71 = (f32[16,8192]{1,0:T(8,128)S(1)}, f32[16,8192]{1,0:T(8,128)S(1)}) fusion(f32[16,8192]{1,0:T(8,128)} %param.10), kind=kLoop, calls=%fused_computation.102 | loop fusion | bytes 1572864 | tf_op jit(solution)/shard_map/cos | solution.py:334
  7.0 1.3 %multiply_convert_fusion.3 = (bf16[8,16,1,8192]{3,1,2,0:T(8,128)(2,1)S(1)}, bf16[8,16,1,8192]{3,1,2,0:T(8,128)(2,1)S(1)}) fusion(f32[16,8192]{1,0:T(8,128)S(1)} %get-tuple-element.38, f32[8,8192]{1,0:T(8,128)S(1)} %get-tuple-element.36, f32[16,8192]{1,0:T(8,128)S(1)} %get-tuple-element.37, f32[8,8192]{1,0:T(8,128)S(1)} %get-tuple-element.35, ...), kind=kLoop, calls=%fused_computation.10 | loop fusion | flops 10485760 | bytes 6029312 | tf_op jit(solution)/shard_map/convert.3
  8.6 1.1 %fusion.8 = f32[16,64]{1,0:T(8,128)S(1)} fusion(f32[16,8192]{1,0:T(8,128)S(1)} %fusion.23, s32[8192]{0:T(1024)S(1)} %copy-done.9), kind=kOutput, calls=%fused_computation.15 | convolution fusion | flops 101187584 | bytes 561152 | tf_op jit(solution)/shard_map/dot_general | solution.py:329
  10.0 0.7 fusion.9
  10.8 1.4 %fusion.48 = (f32[8]{0:T(128)S(1)}, f32[8,16,16,1]{2,1,3,0:T(8,128)S(1)}) fusion(f32[8,16]{1,0:T(8,128)S(1)} %convolution_multiply_fusion.1, pred[8,16]{1,0:T(8,128)(4,1)S(1)} %broadcast_compare_fusion, f32[8192]{0:T(1024)S(1)} %bitcast.107, bf16[16,2,8192]{2,1,0:T(2,128)(2,1)S(1)} %copy-done.4, bf16[8,16,1,8192]{3,1,2,0:T(8,128)(2,1)S(1)} %get-tuple-element.30, ...), kind=kOutput, calls=%fused_computation.68 | convolution fusion | flops 69998584 | bytes 4760224 | tf_op jit(solution)/shard_map/itpk,jpk->itj/dot_general | solution.py:338
  12.2 0.6 copy-done.3
  13.0 0.6 select_maximum_fusion.1.stats_ref
  13.6 0.8 reshape.98.part_ref
  14.4 25.6 %shard_map.111 = (f32[16,8,128]{2,1,0:T(8,128)}, bf16[32,16,256]{2,1,0:T(8,128)(2,1)}) custom-call(f32[8,128]{1,0:T(8,128)} %select_maximum_fusion.1.stats_ref, bf16[16,8192]{1,0:T(8,128)(2,1)} %reshape.98.part_ref), custom_call_target="tpu_custom_call" | custom-call | tf_op jit(solution)/shard_map/pallas_call | solution.py:163
  40.1 2.0 %slice_reduce_fusion.1 = (f32[8]{0:T(128)}, f32[16,1,8]{2,1,0:T(1,128)}, f32[16,1,8]{2,1,0:T(1,128)S(1)}) fusion(f32[16,8,128]{2,1,0:T(8,128)} %get-tuple-element.9), kind=kLoop, calls=%fused_computation.99 | loop fusion | flops 120 | bytes 2080 | tf_op jit(solution)/shard_map/reduce_max | solution.py:354
  42.1 1.4 %copy.30 = f32[16,1,8]{0,2,1:T(8,128)} copy(f32[16,1,8]{2,1,0:T(1,128)} %get-tuple-element.40) | data formatting | bytes 1024 | tf_op jit(solution)/shard_map/slice | solution.py:353
  43.4 0.7 copy.31
  44.1 0.9 %fusion.59 = f32[8]{0:T(128)S(1)} fusion(f32[16,1,8]{0,2,1:T(8,128)} %copy.31, f32[16,1,8]{0,2,1:T(8,128)} %copy.30, f32[8]{0:T(128)} %get-tuple-element.39), kind=kLoop, calls=%fused_computation.85 | loop fusion | flops 376 | bytes 1088 | tf_op jit(solution)/shard_map/reduce_sum | solution.py:355
  45.0 1.1 %fusion.69 = (f32[8]{0:T(128)S(1)}, f32[8,16]{1,0:T(8,128)S(1)}, f32[8,16,16]{2,1,0:T(8,128)S(1)}) fusion(f32[8]{0:T(128)S(1)} %fusion.59, f32[8]{0:T(128)} %get-tuple-element.39, f32[8,16]{1,0:T(8,128)S(1)} %convolution_multiply_fusion.1, f32[8,16,16,1]{2,1,3,0:T(8,128)} %copy-done.3, pred[8,16]{1,0:T(8,128)(4,1)} %copy-done.13), kind=kLoop, calls=%fused_computation.100 | loop fusion | flops 12152 | bytes 17632 | tf_op jit(solution)/shard_map/reduce_sum | solution.py:362
  46.1 2.8 %fusion.11 = f32[8192]{0:T(1024)S(1)} fusion(bf16[8,16,1,8192]{3,1,2,0:T(8,128)(2,1)} %copy-done.2, bf16[8,16,1,8192]{3,1,2,0:T(8,128)(2,1)S(1)} %get-tuple-element.29, bf16[16,2,8192]{2,1,0:T(2,128)(2,1)} %param.9, f32[8,16,16]{2,1,0:T(8,128)S(1)} %get-tuple-element.28), kind=kOutput, calls=%fused_computation.20 | convolution fusion | flops 76277760 | bytes 4759552 | tf_op jit(solution)/shard_map/itj,itpk->jpk/dot_general | solution.py:364
  49.4 1.1 %fusion.17 = f32[64]{0:T(128)S(1)} fusion(f32[8,8192]{1,0:T(8,128)S(1)} %multiply_reduce_fusion, s32[8192]{0:T(1024)S(1)} %copy-done.9, f32[8]{0:T(128)S(1)} %get-tuple-element.26), kind=kOutput, calls=%fused_computation.26 | convolution fusion | flops 50856896 | bytes 295200 | tf_op jit(solution)/shard_map/dot_general | solution.py:361
  50.4 1.1 %fusion.21 = f32[64]{0:T(128)S(1)} fusion(f32[64]{0:T(128)S(1)} %fusion.15, f32[64]{0:T(128)S(1)} %fusion.17, f32[8192,1]{0,1:T(1,128)S(1)} %bitcast.106, s32[8192]{0:T(1024)S(1)} %copy-done.9), kind=kOutput, calls=%fused_computation.30 | convolution fusion | flops 6815936 | bytes 66304 | tf_op jit(solution)/shard_map/dot_general | solution.py:365
  51.6 0.7 select_maximum_fusion.small_ref
  52.3 0.9 %fusion.45 = bf16[16,16,8]{1,0,2:T(8,128)(2,1)S(1)} fusion(f32[8,16,16,1]{2,1,3,0:T(8,128)} %copy-done.3, f32[8]{0:T(128)} %copy-done.14, f32[8]{0:T(128)} %get-tuple-element.39, f32[16,8]{0,1:T(8,128)S(1)} %bitcast.103, pred[16,8]{0,1:T(8,128)(4,1)S(1)} %fusion.78), kind=kLoop, calls=%fused_computation.65 | loop fusion | flops 10240 | bytes 12992 | tf_op jit(solution)/shard_map/convert_element_type | solution.py:357
  53.3 0.7 copy.35.half_ref
  54.0 25.3 %shard_map.112 = (bf16[32,16,128]{2,1,0:T(8,128)(2,1)}, f32[32,8,128]{2,1,0:T(8,128)}, f32[16,8,128]{2,1,0:T(8,128)}) custom-call(bf16[16,128]{1,0:T(8,128)(2,1)} %copy.35.half_ref, f32[8,128]{1,0:T(8,128)} %select_maximum_fusion.small_ref), custom_call_target="tpu_custom_call" | custom-call | tf_op jit(solution)/shard_map/pallas_call | solution.py:271
  79.3 1.2 %copy.36 = bf16[32,16,128]{0,2,1:T(8,128)(2,1)S(1)} copy(bf16[32,16,128]{2,1,0:T(8,128)(2,1)} %get-tuple-element.10) | data formatting | bytes 262144 | tf_op jit(solution)/shard_map/pallas_call | solution.py:271
  80.5 0.7 copy.37
  81.5 0.4 fusion.70
  82.6 1.4 %multiply_convert_fusion.1 = (bf16[256,16,1,256]{3,0,1,2:T(8,128)(2,1)S(1)}, bf16[256,16,1,256]{3,0,1,2:T(8,128)(2,1)S(1)}) fusion(f32[16,256]{1,0:T(8,128)S(1)} %get-tuple-element.44, f32[256,256]{1,0:T(8,128)S(1)} %get-tuple-element.46, f32[16,256]{1,0:T(8,128)S(1)} %get-tuple-element.45, f32[256,256]{1,0:T(8,128)S(1)} %get-tuple-element.47, ...), kind=kLoop, calls=%fused_computation.8 | loop fusion | flops 10485760 | bytes 5013504 | tf_op jit(solution)/shard_map/convert.1
  84.0 0.9 %fusion.12 = f32[16,2,256]{2,0,1:T(8,128)S(1)} fusion(bf16[256,16,1,256]{3,0,1,2:T(8,128)(2,1)S(1)} %get-tuple-element.32, bf16[256,16,1,256]{3,0,1,2:T(8,128)(2,1)S(1)} %get-tuple-element.31, bf16[16,16,32,8]{1,3,2,0:T(8,128)(2,1)S(1)} %copy.37), kind=kOutput, calls=%fused_computation.21 | convolution fusion | flops 75497472 | bytes 4358144 | tf_op jit(solution)/shard_map/tji,itpk->jpk/dot_general | solution.py:392
  84.9 0.7 copy.39
  85.6 1.0 %fusion.34 = f32[16,64]{1,0:T(8,128)} fusion(f32[32,8,128]{2,1,0:T(8,128)S(1)} %copy-done.6, f32[256,64]{0,1:T(8,128)S(1)} %fusion.37), kind=kOutput, calls=%fused_computation.48 | convolution fusion | flops 3162112 | bytes 200704 | tf_op jit(solution)/shard_map/dot_general | solution.py:383
  86.7 0.6 div.47
  (48 shorter events, 2.7 us)
Async XLA Ops:
  0.6 0.8 copy-start
  0.6 6.1 %copy-start.1 = (bf16[8,2,8192]{2,1,0:T(2,128)(2,1)S(1)}, bf16[8,2,8192]{2,1,0:T(2,128)(2,1)}, u32[]{:S(2)}) copy-start(bf16[8,2,8192]{2,1,0:T(2,128)(2,1)} %param.8) | copy-start | bytes 786436
  6.9 1.3 %copy-start.4 = (bf16[16,2,8192]{2,1,0:T(2,128)(2,1)S(1)}, bf16[16,2,8192]{2,1,0:T(2,128)(2,1)}, u32[]{:S(2)}) copy-start(bf16[16,2,8192]{2,1,0:T(2,128)(2,1)} %param.9) | copy-start | bytes 1572868
  7.0 1.6 %copy-start.9 = (s32[8192]{0:T(1024)S(1)}, s32[8192]{0:T(1024)}, u32[]{:S(2)}) copy-start(s32[8192]{0:T(1024)} %param.14) | copy-start | bytes 98308
  7.0 2.7 %copy-start.15 = (f32[64]{0:T(128)S(1)}, f32[64]{0:T(128)}, u32[]{:S(2)}) copy-start(f32[64]{0:T(128)} %param.15) | copy-start | bytes 772
  7.0 3.0 %copy-start.12 = (s32[8,16]{1,0:T(8,128)S(1)}, s32[8,16]{1,0:T(8,128)}, u32[]{:S(2)}) copy-start(s32[8,16]{1,0:T(8,128)} %param.11) | copy-start | bytes 1540
  8.3 3.9 %copy-start.2 = (bf16[8,16,1,8192]{3,1,2,0:T(8,128)(2,1)}, bf16[8,16,1,8192]{3,1,2,0:T(8,128)(2,1)S(1)}, u32[]{:S(2)}) copy-start(bf16[8,16,1,8192]{3,1,2,0:T(8,128)(2,1)S(1)} %get-tuple-element.30) | copy-start | bytes 6291460
  9.7 1.1 %copy-start.10 = (f32[16,64]{1,0:T(8,128)}, f32[16,64]{1,0:T(8,128)S(1)}, u32[]{:S(2)}) copy-start(f32[16,64]{1,0:T(8,128)S(1)} %fusion.8) | copy-start | bytes 12292
  10.0 2.2 %copy-start.13 = (pred[8,16]{1,0:T(8,128)(4,1)}, pred[8,16]{1,0:T(8,128)(4,1)S(1)}, u32[]{:S(2)}) copy-start(pred[8,16]{1,0:T(8,128)(4,1)S(1)} %broadcast_compare_fusion) | copy-start | bytes 388
  12.2 0.6 copy-start.3
  45.0 3.9 %copy-start.14 = (f32[8]{0:T(128)}, f32[8]{0:T(128)S(1)}, u32[]{:S(2)}) copy-start(f32[8]{0:T(128)S(1)} %fusion.59) | copy-start | bytes 100
  46.1 2.8 %copy-start.7 = (f32[8,16,16]{2,1,0:T(8,128)}, f32[8,16,16]{2,1,0:T(8,128)S(1)}, u32[]{:S(2)}) copy-start(f32[8,16,16]{2,1,0:T(8,128)S(1)} %get-tuple-element.28) | copy-start | bytes 24580
  46.1 2.8 %copy-start.11 = (f32[16,64]{1,0:T(8,128)S(1)}, f32[16,64]{1,0:T(8,128)}, u32[]{:S(2)}) copy-start(f32[16,64]{1,0:T(8,128)} %copy-done.10) | copy-start | bytes 12292
  48.9 32.3 %copy-start.5 = (bf16[32,16,256]{2,1,0:T(8,128)(2,1)S(1)}, bf16[32,16,256]{2,1,0:T(8,128)(2,1)}, u32[]{:S(2)}) copy-start(bf16[32,16,256]{2,1,0:T(8,128)(2,1)} %get-tuple-element.11) | copy-start | bytes 786436
  84.0 1.6 %copy-start.6 = (f32[32,8,128]{2,1,0:T(8,128)S(1)}, f32[32,8,128]{2,1,0:T(8,128)}, u32[]{:S(2)}) copy-start(f32[32,8,128]{2,1,0:T(8,128)} %get-tuple-element.12) | copy-start | bytes 393220
  84.0 2.5 %copy-start.8 = (f32[16,8,128]{2,1,0:T(8,128)S(1)}, f32[16,8,128]{2,1,0:T(8,128)}, u32[]{:S(2)}) copy-start(f32[16,8,128]{2,1,0:T(8,128)} %get-tuple-element.13) | copy-start | bytes 196612

commit v10 on v8

--- a/solution.py
+++ b/solution.py
@@ -322,15 +322,24 @@
     ).astype(jnp.float32)
     ctf_all = jnp.dot(group_pick, ctf_table, precision=highest)
     ctf_rows = lax.dynamic_slice_in_dim(ctf_all, dom_index * part_dev, part_dev, 0)
-    ctf_pix = jnp.dot(ctf_rows, shell_pick.T, precision=highest)
-    sigma_pix = jnp.dot(shell_pick, sigma2, precision=highest)
+    per_pixel = jnp.dot(
+        jnp.concatenate([ctf_rows, sigma2[None]], axis=0), shell_pick.T, precision=highest
+    )
+    ctf_pix = per_pixel[:part_dev]
+    sigma_pix = per_pixel[part_dev]
     refs_wide = references.astype(jnp.float32)
     weighted = (refs_wide / sigma_pix).astype(jnp.bfloat16)
-    ref_norm = jnp.dot(jnp.sum(refs_wide * refs_wide, axis=1), shell_pick, precision=highest)
+    planes = particles.astype(jnp.float32)
+    norms = jnp.dot(
+        jnp.concatenate([jnp.sum(refs_wide * refs_wide, axis=1), jnp.sum(planes * planes, axis=1)], axis=0),
+        shell_pick,
+        precision=highest,
+    )
+    ref_norm = norms[:ori_dev]
+    part_norm = norms[ori_dev:]
     energy = ref_norm / sigma2
     ctf_square = ctf_rows * ctf_rows
     quadratic = 0.5 * jnp.dot(ctf_square, energy.T, precision=highest)
-    planes = particles.astype(jnp.float32)
     cosines = jnp.cos(phases)
     sine_rows = jnp.sin(phases)
 
@@ -358,7 +367,6 @@
 
     weight_rows = jnp.sum(posterior, axis=1)
     ctf_part = jnp.dot(weight_rows.T, ctf_square, precision=highest)
-    part_norm = jnp.dot(jnp.sum(planes * planes, axis=1), shell_pick, precision=highest)
     term_one = jnp.sum(part_norm * jnp.sum(weight_rows, axis=1)[:, None], axis=0)
     term_three = jnp.sum(ctf_part * ref_norm, axis=0)
     local_sums = jnp.einsum("itj,itpk->jpk", post_half, images, preferred_element_type=jnp.float32)

time: 84.1 us -> 83.1 us (0.988)
  matrix products: 13.2 us -> 11.3 us
    dot_general x4 -> x2, matrix products: 4.5 us -> 2.66 us  [the longest x1 1.53 us: on_device(): jnp.dot(jnp.concatenate([ctf_rows, sigma2[None]], axis=0), shell_pick.T,...]
    unnamed x30 -> x32, local copies, waits for them, and re-layouts: 2.75 us -> 2.74 us
where the time goes in v10:
time: 83.1 us; the launch traced here: 82.6 us
  Pallas kernels  50.7 us (61%)
  local copies, waits for them, and re-layouts  12.1 us (15%)
  matrix products  11.3 us (14%)
  other arithmetic  7.47 us (9%)
  between operations  0.98 us (1%)
    pallas_call x1, Pallas kernels, stats_and_columns(): pl.pallas_call(functools.partial(_stats_kernel, dom_n, orient_n, width),...  25.6 us
    pallas_call x1, Pallas kernels, spread(): pl.pallas_call(functools.partial(_spread_kernel, dom_n, orient_n), out_sh...  25.2 us
    cos x1, local copies, waits for them, and re-layouts, on_device(): cosines = jnp.cos(phases)  2.8 us
    dot_general x1, matrix products, on_device(): jnp.einsum('itj,itpk->jpk', post_half, images, preferred_element_type=jnp...  2.75 us
    unnamed x32, local copies, waits for them, and re-layouts  2.74 us
    another operation x2, other arithmetic  2.67 us
    reshape x2, local copies, waits for them, and re-layouts, on_device(): post_all = half_all.reshape(dom_size * part_dev, trans_count, ori_dev)  2.58 us

profile of v10, /device:TPU:1, one launch (start us, length us, event | category | flops | bytes accessed | tf_op | source)
XLA Modules:
  0.0 82.6 jit_solution(14553861928057788579)
XLA Ops:
  0.7 0.7 copy-done
  1.4 1.0 %fusion.37 = f32[256,64]{0,1:T(8,128)S(1)} fusion(f32[64,64]{1,0:T(8,128)S(1)} %copy-done, s32[256]{0:T(256)} %param.12), kind=kOutput, calls=%fused_computation.52 | convolution fusion | flops 12599296 | bytes 82944 | tf_op jit(solution)/shard_map/dot_general | solution.py:323
  2.5 1.5 %fusion.8 = f32[9,8192]{1,0:T(8,128)S(1)} fusion(s32[8192]{0:T(1024)} %param.14, f32[1,64]{1,0:T(1,128)} %bitcast.71, f32[8,64]{1,0:T(8,128)S(1)} %copy.34), kind=kOutput, calls=%fused_computation.15 | convolution fusion | flops 57147968 | bytes 329984 | tf_op jit(solution)/shard_map/dot_general | solution.py:325
  4.1 2.8 %fusion.63 = (f32[16,8192]{1,0:T(8,128)S(1)}, f32[16,8192]{1,0:T(8,128)S(1)}) fusion(f32[16,8192]{1,0:T(8,128)} %param.10), kind=kLoop, calls=%fused_computation.94 | loop fusion | bytes 1572864 | tf_op jit(solution)/shard_map/cos | solution.py:343
  7.1 1.3 %multiply_convert_fusion.3 = (bf16[8,16,1,8192]{3,1,2,0:T(8,128)(2,1)S(1)}, bf16[8,16,1,8192]{3,1,2,0:T(8,128)(2,1)S(1)}) fusion(f32[16,8192]{1,0:T(8,128)S(1)} %get-tuple-element.42, f32[8,8192]{1,0:T(8,128)S(1)} %get-tuple-element.40, f32[16,8192]{1,0:T(8,128)S(1)} %get-tuple-element.41, f32[8,8192]{1,0:T(8,128)S(1)} %get-tuple-element.39, ...), kind=kLoop, calls=%fused_computation.10 | loop fusion | flops 10485760 | bytes 6029312 | tf_op jit(solution)/shard_map/convert.3
  8.4 0.3 fusion.22
  8.9 1.1 %fusion.7 = f32[24,64]{1,0:T(8,128)S(1)} fusion(s32[8192]{0:T(1024)S(1)} %copy-done.7, f32[8,8192]{1,0:T(8,128)S(1)} %multiply_reduce_fusion, f32[16,8192]{1,0:T(8,128)S(1)} %fusion.22), kind=kOutput, calls=%fused_computation.14 | convolution fusion | flops 151715840 | bytes 825344 | tf_op jit(solution)/shard_map/dot_general | solution.py:333
  10.3 1.4 %fusion.64 = (f32[8]{0:T(128)S(1)}, f32[8,16,16]{2,1,0:T(8,128)S(1)}) fusion(f32[8,16]{1,0:T(8,128)S(1)} %convolution_multiply_fusion.1, f32[8192]{0:T(1024)S(1)} %bitcast.70, bf16[16,2,8192]{2,1,0:T(2,128)(2,1)S(1)} %copy-done.3, bf16[8,16,1,8192]{3,1,2,0:T(8,128)(2,1)S(1)} %get-tuple-element.34, bf16[8,16,1,8192]{3,1,2,0:T(8,128)(2,1)S(1)} %get-tuple-element.33, ...), kind=kOutput, calls=%fused_computation.95 | convolution fusion | flops 69998584 | bytes 4760224 | tf_op jit(solution)/shard_map/itpk,jpk->itj/dot_general | solution.py:347
  11.7 0.6 copy-done.6
  12.6 0.6 select_maximum_fusion.1.stats_ref
  13.2 0.8 reshape.95.part_ref
  14.0 25.6 %shard_map.111 = (f32[16,8,128]{2,1,0:T(8,128)}, bf16[32,16,256]{2,1,0:T(8,128)(2,1)}) custom-call(f32[8,128]{1,0:T(8,128)} %select_maximum_fusion.1.stats_ref, bf16[16,8192]{1,0:T(8,128)(2,1)} %reshape.95.part_ref), custom_call_target="tpu_custom_call" | custom-call | tf_op jit(solution)/shard_map/pallas_call | solution.py:163
  39.5 1.0 %slice_reduce_fusion.1 = (f32[8]{0:T(128)S(1)}, f32[16,1,8]{2,1,0:T(1,128)S(1)}, f32[16,1,8]{2,1,0:T(1,128)S(1)}) fusion(f32[16,8,128]{2,1,0:T(8,128)} %get-tuple-element.9), kind=kLoop, calls=%fused_computation.91 | loop fusion | flops 120 | bytes 2080 | tf_op jit(solution)/shard_map/reduce_max | solution.py:363
  40.8 1.1 %fusion.61 = (f32[8]{0:T(128)S(1)}, f32[8,16]{1,0:T(8,128)S(1)}, f32[8,16,16]{2,1,0:T(8,128)S(1)}) fusion(f32[8]{0:T(128)S(1)} %fusion.53, f32[8,16,16]{2,1,0:T(8,128)} %copy-done.6, f32[8]{0:T(128)S(1)} %get-tuple-element.43), kind=kLoop, calls=%fused_computation.92 | loop fusion | flops 8056 | bytes 16992 | tf_op jit(solution)/shard_map/reduce_sum | solution.py:370
  41.9 0.6 copy-done.10
  42.5 2.8 %fusion.9 = f32[8192]{0:T(1024)S(1)} fusion(bf16[8,16,1,8192]{3,1,2,0:T(8,128)(2,1)} %copy-done.2, bf16[8,16,1,8192]{3,1,2,0:T(8,128)(2,1)S(1)} %get-tuple-element.33, bf16[16,2,8192]{2,1,0:T(2,128)(2,1)} %param.9, bf16[8,16,16]{2,1,0:T(8,128)(2,1)S(1)} %convert_element_type.29), kind=kOutput, calls=%fused_computation.18 | convolution fusion | flops 76275712 | bytes 4755456 | tf_op jit(solution)/shard_map/itj,itpk->jpk/dot_general | solution.py:372
  45.3 0.2 fusion.16
  45.6 1.0 %fusion.20 = f32[64]{0:T(128)S(1)} fusion(f32[64]{0:T(128)S(1)} %fusion.16, f32[64]{0:T(128)S(1)} %fusion.50, f32[8192,1]{0,1:T(1,128)S(1)} %bitcast.74, s32[8192]{0:T(1024)S(1)} %copy-done.8), kind=kOutput, calls=%fused_computation.29 | convolution fusion | flops 6815936 | bytes 66304 | tf_op jit(solution)/shard_map/dot_general | solution.py:373
  46.8 0.7 select_maximum_fusion.small_ref
  47.4 1.4 %reshape.96.half_ref = bf16[16,128]{1,0:T(8,128)(2,1)} reshape(bf16[8,16,16]{2,1,0:T(8,128)(2,1)} %copy-done.10) | data formatting | bytes 8192 | tf_op jit(solution)/shard_map/reshape | solution.py:380
  48.9 25.2 %shard_map.112 = (bf16[32,16,128]{2,1,0:T(8,128)(2,1)}, f32[32,8,128]{2,1,0:T(8,128)}, f32[16,8,128]{2,1,0:T(8,128)}) custom-call(bf16[16,128]{1,0:T(8,128)(2,1)} %reshape.96.half_ref, f32[8,128]{1,0:T(8,128)} %select_maximum_fusion.small_ref), custom_call_target="tpu_custom_call" | custom-call | tf_op jit(solution)/shard_map/pallas_call | solution.py:271
  74.1 1.8 %reshape.98 = bf16[256,16,16]{2,1,0:T(8,128)(2,1)S(1)} reshape(bf16[32,16,128]{2,1,0:T(8,128)(2,1)} %get-tuple-element.10) | data formatting | bytes 262144 | tf_op jit(solution)/shard_map/reshape | solution.py:382
  75.9 0.8 %copy.41 = bf16[256,16,16]{0,2,1:T(8,128)(2,1)S(1)} copy(bf16[256,16,16]{2,1,0:T(8,128)(2,1)S(1)} %reshape.98) | data formatting | bytes 262144 | tf_op jit(solution)/shard_map/reshape | solution.py:382
  76.7 0.3 reshape.100
  77.0 0.4 fusion.62
  77.4 0.3 iota_compare_fusion
  77.7 0.3 fusion.40
  78.1 1.4 %multiply_convert_fusion.1 = (bf16[256,16,1,256]{3,0,1,2:T(8,128)(2,1)S(1)}, bf16[256,16,1,256]{3,0,1,2:T(8,128)(2,1)S(1)}) fusion(f32[16,256]{1,0:T(8,128)S(1)} %get-tuple-element.48, f32[256,256]{1,0:T(8,128)S(1)} %get-tuple-element.50, f32[16,256]{1,0:T(8,128)S(1)} %get-tuple-element.49, f32[256,256]{1,0:T(8,128)S(1)} %get-tuple-element.51, ...), kind=kLoop, calls=%fused_computation.8 | loop fusion | flops 10485760 | bytes 5013504 | tf_op jit(solution)/shard_map/convert.1
  79.5 0.8 fusion.13
  80.3 0.6 copy.42
  80.9 1.0 %fusion.33 = f32[16,64]{1,0:T(8,128)} fusion(f32[32,8,128]{2,1,0:T(8,128)S(1)} %copy-done.11, f32[256,64]{0,1:T(8,128)S(1)} %fusion.37), kind=kOutput, calls=%fused_computation.47 | convolution fusion | flops 3162112 | bytes 200704 | tf_op jit(solution)/shard_map/dot_general | solution.py:389
  82.0 0.6 div.43
  (47 shorter events, 1.7 us)
Async XLA Ops:
  0.6 0.8 copy-start
  0.6 6.2 %copy-start.1 = (bf16[8,2,8192]{2,1,0:T(2,128)(2,1)S(1)}, bf16[8,2,8192]{2,1,0:T(2,128)(2,1)}, u32[]{:S(2)}) copy-start(bf16[8,2,8192]{2,1,0:T(2,128)(2,1)} %param.8) | copy-start | bytes 786436
  7.1 1.3 %copy-start.3 = (bf16[16,2,8192]{2,1,0:T(2,128)(2,1)S(1)}, bf16[16,2,8192]{2,1,0:T(2,128)(2,1)}, u32[]{:S(2)}) copy-start(bf16[16,2,8192]{2,1,0:T(2,128)(2,1)} %param.9) | copy-start | bytes 1572868
  7.1 1.8 %copy-start.7 = (s32[8192]{0:T(1024)S(1)}, s32[8192]{0:T(1024)}, u32[]{:S(2)}) copy-start(s32[8192]{0:T(1024)} %param.14) | copy-start | bytes 98308
  8.4 3.3 %copy-start.2 = (bf16[8,16,1,8192]{3,1,2,0:T(8,128)(2,1)}, bf16[8,16,1,8192]{3,1,2,0:T(8,128)(2,1)S(1)}, u32[]{:S(2)}) copy-start(bf16[8,16,1,8192]{3,1,2,0:T(8,128)(2,1)S(1)} %get-tuple-element.34) | copy-start | bytes 6291460
  8.4 1.7 %copy-start.14 = (f32[64]{0:T(128)S(1)}, f32[64]{0:T(128)}, u32[]{:S(2)}) copy-start(f32[64]{0:T(128)} %param.15) | copy-start | bytes 772
  8.4 1.9 %copy-start.13 = (s32[8,16]{1,0:T(8,128)S(1)}, s32[8,16]{1,0:T(8,128)}, u32[]{:S(2)}) copy-start(s32[8,16]{1,0:T(8,128)} %param.11) | copy-start | bytes 1540
  11.7 0.6 copy-start.6
  41.9 3.4 %copy-start.5 = (f32[8,16,16]{2,1,0:T(8,128)}, f32[8,16,16]{2,1,0:T(8,128)S(1)}, u32[]{:S(2)}) copy-start(f32[8,16,16]{2,1,0:T(8,128)S(1)} %get-tuple-element.32) | copy-start | bytes 24580
  41.9 0.6 copy-start.10
  42.5 3.1 %copy-start.8 = (s32[8192]{0:T(1024)S(1)}, s32[8192]{0:T(1024)}, u32[]{:S(2)}) copy-start(s32[8192]{0:T(1024)} %param.14) | copy-start | bytes 98308
  45.3 31.4 %copy-start.4 = (bf16[32,16,256]{2,1,0:T(8,128)(2,1)S(1)}, bf16[32,16,256]{2,1,0:T(8,128)(2,1)}, u32[]{:S(2)}) copy-start(bf16[32,16,256]{2,1,0:T(8,128)(2,1)} %get-tuple-element.11) | copy-start | bytes 786436
  75.8 1.6 %copy-start.9 = (s32[8192]{0:T(1024)S(1)}, s32[8192]{0:T(1024)}, u32[]{:S(2)}) copy-start(s32[8192]{0:T(1024)} %param.14) | copy-start | bytes 98308
  79.5 1.5 %copy-start.11 = (f32[32,8,128]{2,1,0:T(8,128)S(1)}, f32[32,8,128]{2,1,0:T(8,128)}, u32[]{:S(2)}) copy-start(f32[32,8,128]{2,1,0:T(8,128)} %get-tuple-element.12) | copy-start | bytes 393220
  79.5 2.4 %copy-start.12 = (f32[16,8,128]{2,1,0:T(8,128)S(1)}, f32[16,8,128]{2,1,0:T(8,128)}, u32[]{:S(2)}) copy-start(f32[16,8,128]{2,1,0:T(8,128)} %get-tuple-element.13) | copy-start | bytes 196612

commit v11 on v10

--- a/solution.py
+++ b/solution.py
@@ -82,8 +82,8 @@
     )(*[x for x, _ in payloads])
 
 
-def _stats_kernel(dom_n, orient_n, width, stats_ref, part_ref, stats_out, part_out,
-                  stats_held, part_held, orient_send, orient_recv, dom_send, dom_recv):
+def _stats_kernel(dom_n, orient_n, width, stats_ref, part_ref, stats_held, part_held,
+                  orient_send, orient_recv, dom_send, dom_recv):
     me = lax.axis_index("dom")
     mine = lax.axis_index("orient")
     barrier = pltpu.get_barrier_semaphore()
@@ -150,8 +150,6 @@
 
     lax.fori_loop(1, orient_n, orient_finish, 0)
     lax.fori_loop(1, dom_n, dom_finish, 0)
-    stats_out[...] = stats_held[...]
-    part_out[...] = part_held[...]
 
 
 def stats_and_columns(stats, part_rows, dom_n, orient_n, width, collective_id):
@@ -166,8 +164,6 @@
         in_specs=[vmem] * 2,
         out_specs=(vmem, vmem),
         scratch_shapes=[
-            pltpu.VMEM(shapes[0].shape, shapes[0].dtype),
-            pltpu.VMEM(shapes[1].shape, shapes[1].dtype),
             pltpu.SemaphoreType.DMA((orient_n,)),
             pltpu.SemaphoreType.DMA((orient_n,)),
             pltpu.SemaphoreType.DMA((dom_n,)),
@@ -178,8 +174,7 @@
 
 
 def _spread_kernel(dom_n, orient_n, half_ref, small_ref,
-                   half_out, small_out, terms_out,
-                   half_held, small_held, summed, terms_held,
+                   half_held, small_held, terms_held, summed,
                    send_sem, recv_sem, orient_send, orient_recv):
     me = lax.axis_index("dom")
     mine = lax.axis_index("orient")
@@ -256,9 +251,6 @@
         return carry
 
     lax.fori_loop(1, orient_n, orient_finish, 0)
-    half_out[...] = half_held[...]
-    small_out[...] = small_held[...]
-    terms_out[...] = terms_held[...]
 
 
 def spread(half_rows, small, dom_n, orient_n, collective_id):
@@ -274,10 +266,7 @@
         in_specs=[vmem] * 2,
         out_specs=(vmem,) * 3,
         scratch_shapes=[
-            pltpu.VMEM(shapes[0].shape, shapes[0].dtype),
-            pltpu.VMEM(shapes[1].shape, shapes[1].dtype),
             pltpu.VMEM(small.shape, small.dtype),
-            pltpu.VMEM(shapes[2].shape, shapes[2].dtype),
             pltpu.SemaphoreType.DMA((2, dom_n)),
             pltpu.SemaphoreType.DMA((2, dom_n)),
             pltpu.SemaphoreType.DMA((orient_n,)),

time: 83.1 us -> 83.1 us (level)
  no operation moved by 1% of the time
where the time goes in v11:
time: 83.1 us; the launch traced here: 82.6 us
  Pallas kernels  50.7 us (61%)
  local copies, waits for them, and re-layouts  12.1 us (15%)
  matrix products  11.3 us (14%)
  other arithmetic  7.47 us (9%)
  between operations  0.98 us (1%)
    pallas_call x1, Pallas kernels, stats_and_columns(): pl.pallas_call(functools.partial(_stats_kernel, dom_n, orient_n, width),...  25.6 us
    pallas_call x1, Pallas kernels, spread(): pl.pallas_call(functools.partial(_spread_kernel, dom_n, orient_n), out_sh...  25.2 us
    cos x1, local copies, waits for them, and re-layouts, on_device(): cosines = jnp.cos(phases)  2.8 us
    dot_general x1, matrix products, on_device(): jnp.einsum('itj,itpk->jpk', post_half, images, preferred_element_type=jnp...  2.75 us
    unnamed x32, local copies, waits for them, and re-layouts  2.74 us
    another operation x2, other arithmetic  2.67 us
    reshape x2, local copies, waits for them, and re-layouts, on_device(): post_all = half_all.reshape(dom_size * part_dev, trans_count, ori_dev)  2.58 us

profile of v11, /device:TPU:1, one launch (start us, length us, event | category | flops | bytes accessed | tf_op | source)
XLA Modules:
  0.0 82.6 jit_solution(14604688327740807744)
XLA Ops:
  0.7 0.7 copy-done
  1.4 1.0 %fusion.37 = f32[256,64]{0,1:T(8,128)S(1)} fusion(f32[64,64]{1,0:T(8,128)S(1)} %copy-done, s32[256]{0:T(256)} %param.12), kind=kOutput, calls=%fused_computation.52 | convolution fusion | flops 12599296 | bytes 82944 | tf_op jit(solution)/shard_map/dot_general | solution.py:312
  2.5 1.5 %fusion.8 = f32[9,8192]{1,0:T(8,128)S(1)} fusion(s32[8192]{0:T(1024)} %param.14, f32[1,64]{1,0:T(1,128)} %bitcast.71, f32[8,64]{1,0:T(8,128)S(1)} %copy.34), kind=kOutput, calls=%fused_computation.15 | convolution fusion | flops 57147968 | bytes 329984 | tf_op jit(solution)/shard_map/dot_general | solution.py:314
  4.1 2.8 %fusion.63 = (f32[16,8192]{1,0:T(8,128)S(1)}, f32[16,8192]{1,0:T(8,128)S(1)}) fusion(f32[16,8192]{1,0:T(8,128)} %param.10), kind=kLoop, calls=%fused_computation.94 | loop fusion | bytes 1572864 | tf_op jit(solution)/shard_map/cos | solution.py:332
  7.1 1.3 %multiply_convert_fusion.3 = (bf16[8,16,1,8192]{3,1,2,0:T(8,128)(2,1)S(1)}, bf16[8,16,1,8192]{3,1,2,0:T(8,128)(2,1)S(1)}) fusion(f32[16,8192]{1,0:T(8,128)S(1)} %get-tuple-element.42, f32[8,8192]{1,0:T(8,128)S(1)} %get-tuple-element.40, f32[16,8192]{1,0:T(8,128)S(1)} %get-tuple-element.41, f32[8,8192]{1,0:T(8,128)S(1)} %get-tuple-element.39, ...), kind=kLoop, calls=%fused_computation.10 | loop fusion | flops 10485760 | bytes 6029312 | tf_op jit(solution)/shard_map/convert.3
  8.4 0.3 fusion.22
  8.9 1.1 %fusion.7 = f32[24,64]{1,0:T(8,128)S(1)} fusion(s32[8192]{0:T(1024)S(1)} %copy-done.7, f32[8,8192]{1,0:T(8,128)S(1)} %multiply_reduce_fusion, f32[16,8192]{1,0:T(8,128)S(1)} %fusion.22), kind=kOutput, calls=%fused_computation.14 | convolution fusion | flops 151715840 | bytes 825344 | tf_op jit(solution)/shard_map/dot_general | solution.py:322
  10.3 1.4 %fusion.64 = (f32[8]{0:T(128)S(1)}, f32[8,16,16]{2,1,0:T(8,128)S(1)}) fusion(f32[8,16]{1,0:T(8,128)S(1)} %convolution_multiply_fusion.1, f32[8192]{0:T(1024)S(1)} %bitcast.70, bf16[16,2,8192]{2,1,0:T(2,128)(2,1)S(1)} %copy-done.3, bf16[8,16,1,8192]{3,1,2,0:T(8,128)(2,1)S(1)} %get-tuple-element.34, bf16[8,16,1,8192]{3,1,2,0:T(8,128)(2,1)S(1)} %get-tuple-element.33, ...), kind=kOutput, calls=%fused_computation.95 | convolution fusion | flops 69998584 | bytes 4760224 | tf_op jit(solution)/shard_map/itpk,jpk->itj/dot_general | solution.py:336
  11.7 0.6 copy-done.6
  12.6 0.6 select_maximum_fusion.1.stats_ref
  13.2 0.8 reshape.95.part_ref
  14.0 25.6 %shard_map.111 = (f32[16,8,128]{2,1,0:T(8,128)}, bf16[32,16,256]{2,1,0:T(8,128)(2,1)}) custom-call(f32[8,128]{1,0:T(8,128)} %select_maximum_fusion.1.stats_ref, bf16[16,8192]{1,0:T(8,128)(2,1)} %reshape.95.part_ref), custom_call_target="tpu_custom_call" | custom-call | tf_op jit(solution)/shard_map/pallas_call | solution.py:161
  39.5 1.0 %slice_reduce_fusion.1 = (f32[8]{0:T(128)S(1)}, f32[16,1,8]{2,1,0:T(1,128)S(1)}, f32[16,1,8]{2,1,0:T(1,128)S(1)}) fusion(f32[16,8,128]{2,1,0:T(8,128)} %get-tuple-element.9), kind=kLoop, calls=%fused_computation.91 | loop fusion | flops 120 | bytes 2080 | tf_op jit(solution)/shard_map/reduce_max | solution.py:352
  40.8 1.1 %fusion.61 = (f32[8]{0:T(128)S(1)}, f32[8,16]{1,0:T(8,128)S(1)}, f32[8,16,16]{2,1,0:T(8,128)S(1)}) fusion(f32[8]{0:T(128)S(1)} %fusion.53, f32[8,16,16]{2,1,0:T(8,128)} %copy-done.6, f32[8]{0:T(128)S(1)} %get-tuple-element.43), kind=kLoop, calls=%fused_computation.92 | loop fusion | flops 8056 | bytes 16992 | tf_op jit(solution)/shard_map/reduce_sum | solution.py:359
  41.9 0.6 copy-done.10
  42.5 2.8 %fusion.9 = f32[8192]{0:T(1024)S(1)} fusion(bf16[8,16,1,8192]{3,1,2,0:T(8,128)(2,1)} %copy-done.2, bf16[8,16,1,8192]{3,1,2,0:T(8,128)(2,1)S(1)} %get-tuple-element.33, bf16[16,2,8192]{2,1,0:T(2,128)(2,1)} %param.9, bf16[8,16,16]{2,1,0:T(8,128)(2,1)S(1)} %convert_element_type.29), kind=kOutput, calls=%fused_computation.18 | convolution fusion | flops 76275712 | bytes 4755456 | tf_op jit(solution)/shard_map/itj,itpk->jpk/dot_general | solution.py:361
  45.3 0.2 fusion.16
  45.6 1.0 %fusion.20 = f32[64]{0:T(128)S(1)} fusion(f32[64]{0:T(128)S(1)} %fusion.16, f32[64]{0:T(128)S(1)} %fusion.50, f32[8192,1]{0,1:T(1,128)S(1)} %bitcast.74, s32[8192]{0:T(1024)S(1)} %copy-done.8), kind=kOutput, calls=%fused_computation.29 | convolution fusion | flops 6815936 | bytes 66304 | tf_op jit(solution)/shard_map/dot_general | solution.py:362
  46.7 0.7 select_maximum_fusion.small_ref
  47.4 1.4 %reshape.96.half_ref = bf16[16,128]{1,0:T(8,128)(2,1)} reshape(bf16[8,16,16]{2,1,0:T(8,128)(2,1)} %copy-done.10) | data formatting | bytes 8192 | tf_op jit(solution)/shard_map/reshape | solution.py:369
  48.9 25.2 %shard_map.112 = (bf16[32,16,128]{2,1,0:T(8,128)(2,1)}, f32[32,8,128]{2,1,0:T(8,128)}, f32[16,8,128]{2,1,0:T(8,128)}) custom-call(bf16[16,128]{1,0:T(8,128)(2,1)} %reshape.96.half_ref, f32[8,128]{1,0:T(8,128)} %select_maximum_fusion.small_ref), custom_call_target="tpu_custom_call" | custom-call | tf_op jit(solution)/shard_map/pallas_call | solution.py:263
  74.1 1.8 %reshape.98 = bf16[256,16,16]{2,1,0:T(8,128)(2,1)S(1)} reshape(bf16[32,16,128]{2,1,0:T(8,128)(2,1)} %get-tuple-element.10) | data formatting | bytes 262144 | tf_op jit(solution)/shard_map/reshape | solution.py:371
  75.8 0.8 %copy.41 = bf16[256,16,16]{0,2,1:T(8,128)(2,1)S(1)} copy(bf16[256,16,16]{2,1,0:T(8,128)(2,1)S(1)} %reshape.98) | data formatting | bytes 262144 | tf_op jit(solution)/shard_map/reshape | solution.py:371
  76.7 0.3 reshape.100
  76.9 0.4 fusion.62
  77.4 0.3 iota_compare_fusion
  77.7 0.3 fusion.40
  78.0 1.4 %multiply_convert_fusion.1 = (bf16[256,16,1,256]{3,0,1,2:T(8,128)(2,1)S(1)}, bf16[256,16,1,256]{3,0,1,2:T(8,128)(2,1)S(1)}) fusion(f32[16,256]{1,0:T(8,128)S(1)} %get-tuple-element.48, f32[256,256]{1,0:T(8,128)S(1)} %get-tuple-element.50, f32[16,256]{1,0:T(8,128)S(1)} %get-tuple-element.49, f32[256,256]{1,0:T(8,128)S(1)} %get-tuple-element.51, ...), kind=kLoop, calls=%fused_computation.8 | loop fusion | flops 10485760 | bytes 5013504 | tf_op jit(solution)/shard_map/convert.1
  79.5 0.8 fusion.13
  80.3 0.6 copy.42
  80.9 1.0 %fusion.33 = f32[16,64]{1,0:T(8,128)} fusion(f32[32,8,128]{2,1,0:T(8,128)S(1)} %copy-done.11, f32[256,64]{0,1:T(8,128)S(1)} %fusion.37), kind=kOutput, calls=%fused_computation.47 | convolution fusion | flops 3162112 | bytes 200704 | tf_op jit(solution)/shard_map/dot_general | solution.py:378
  82.0 0.6 div.43
  (47 shorter events, 1.7 us)
Async XLA Ops:
  0.6 0.8 copy-start
  0.6 6.2 %copy-start.1 = (bf16[8,2,8192]{2,1,0:T(2,128)(2,1)S(1)}, bf16[8,2,8192]{2,1,0:T(2,128)(2,1)}, u32[]{:S(2)}) copy-start(bf16[8,2,8192]{2,1,0:T(2,128)(2,1)} %param.8) | copy-start | bytes 786436
  7.1 1.3 %copy-start.3 = (bf16[16,2,8192]{2,1,0:T(2,128)(2,1)S(1)}, bf16[16,2,8192]{2,1,0:T(2,128)(2,1)}, u32[]{:S(2)}) copy-start(bf16[16,2,8192]{2,1,0:T(2,128)(2,1)} %param.9) | copy-start | bytes 1572868
  7.1 1.8 %copy-start.7 = (s32[8192]{0:T(1024)S(1)}, s32[8192]{0:T(1024)}, u32[]{:S(2)}) copy-start(s32[8192]{0:T(1024)} %param.14) | copy-start | bytes 98308
  8.4 3.3 %copy-start.2 = (bf16[8,16,1,8192]{3,1,2,0:T(8,128)(2,1)}, bf16[8,16,1,8192]{3,1,2,0:T(8,128)(2,1)S(1)}, u32[]{:S(2)}) copy-start(bf16[8,16,1,8192]{3,1,2,0:T(8,128)(2,1)S(1)} %get-tuple-element.34) | copy-start | bytes 6291460
  8.4 1.7 %copy-start.14 = (f32[64]{0:T(128)S(1)}, f32[64]{0:T(128)}, u32[]{:S(2)}) copy-start(f32[64]{0:T(128)} %param.15) | copy-start | bytes 772
  8.4 1.9 %copy-start.13 = (s32[8,16]{1,0:T(8,128)S(1)}, s32[8,16]{1,0:T(8,128)}, u32[]{:S(2)}) copy-start(s32[8,16]{1,0:T(8,128)} %param.11) | copy-start | bytes 1540
  11.7 0.6 copy-start.6
  41.9 3.4 %copy-start.5 = (f32[8,16,16]{2,1,0:T(8,128)}, f32[8,16,16]{2,1,0:T(8,128)S(1)}, u32[]{:S(2)}) copy-start(f32[8,16,16]{2,1,0:T(8,128)S(1)} %get-tuple-element.32) | copy-start | bytes 24580
  41.9 0.6 copy-start.10
  42.5 3.1 %copy-start.8 = (s32[8192]{0:T(1024)S(1)}, s32[8192]{0:T(1024)}, u32[]{:S(2)}) copy-start(s32[8192]{0:T(1024)} %param.14) | copy-start | bytes 98308
  45.3 31.4 %copy-start.4 = (bf16[32,16,256]{2,1,0:T(8,128)(2,1)S(1)}, bf16[32,16,256]{2,1,0:T(8,128)(2,1)}, u32[]{:S(2)}) copy-start(bf16[32,16,256]{2,1,0:T(8,128)(2,1)} %get-tuple-element.11) | copy-start | bytes 786436
  75.8 1.6 %copy-start.9 = (s32[8192]{0:T(1024)S(1)}, s32[8192]{0:T(1024)}, u32[]{:S(2)}) copy-start(s32[8192]{0:T(1024)} %param.14) | copy-start | bytes 98308
  79.5 1.5 %copy-start.11 = (f32[32,8,128]{2,1,0:T(8,128)S(1)}, f32[32,8,128]{2,1,0:T(8,128)}, u32[]{:S(2)}) copy-start(f32[32,8,128]{2,1,0:T(8,128)} %get-tuple-element.12) | copy-start | bytes 393220
  79.5 2.4 %copy-start.12 = (f32[16,8,128]{2,1,0:T(8,128)S(1)}, f32[16,8,128]{2,1,0:T(8,128)}, u32[]{:S(2)}) copy-start(f32[16,8,128]{2,1,0:T(8,128)} %get-tuple-element.13) | copy-start | bytes 196612

commit v12 on v10

--- a/solution.py
+++ b/solution.py
@@ -230,8 +230,9 @@
         lax.fori_loop(1, dom_n, body, 0)
 
     finish(1)
-    summed[...] = jnp.sum(small_held[...], axis=0)
-    finish(0)
+    total = jnp.sum(small_held[...], axis=0)
+    summed[...] = total
+    terms_held[mine] = total
 
     def orient_copy(k):
         peer = lax.rem(mine + k, orient_n)
@@ -249,7 +250,7 @@
         return carry
 
     lax.fori_loop(1, orient_n, orient_start, 0)
-    terms_held[mine] = summed[...]
+    finish(0)
 
     def orient_finish(k, carry):
         orient_copy(k).wait()

time: 83.1 us -> 82.9 us (level)
  no operation moved by 1% of the time
where the time goes in v12:
time: 82.9 us; the launch traced here: 82.3 us
  Pallas kernels  50.5 us (61%)
  local copies, waits for them, and re-layouts  12.1 us (15%)
  matrix products  11.3 us (14%)
  other arithmetic  7.47 us (9%)
  between operations  0.98 us (1%)
    pallas_call x1, Pallas kernels, stats_and_columns(): pl.pallas_call(functools.partial(_stats_kernel, dom_n, orient_n, width),...  25.6 us
    pallas_call x1, Pallas kernels, spread(): pl.pallas_call(functools.partial(_spread_kernel, dom_n, orient_n), out_sh...  24.9 us
    cos x1, local copies, waits for them, and re-layouts, on_device(): cosines = jnp.cos(phases)  2.8 us
    dot_general x1, matrix products, on_device(): jnp.einsum('itj,itpk->jpk', post_half, images, preferred_element_type=jnp...  2.75 us
    unnamed x32, local copies, waits for them, and re-layouts  2.74 us
    another operation x2, other arithmetic  2.67 us
    reshape x2, local copies, waits for them, and re-layouts, on_device(): post_all = half_all.reshape(dom_size * part_dev, trans_count, ori_dev)  2.58 us

profile of v12, /device:TPU:1, one launch (start us, length us, event | category | flops | bytes accessed | tf_op | source)
XLA Modules:
  0.0 82.3 jit_solution(1868577007592557203)
XLA Ops:
  0.7 0.7 copy-done
  1.4 1.0 %fusion.37 = f32[256,64]{0,1:T(8,128)S(1)} fusion(f32[64,64]{1,0:T(8,128)S(1)} %copy-done, s32[256]{0:T(256)} %param.12), kind=kOutput, calls=%fused_computation.52 | convolution fusion | flops 12599296 | bytes 82944 | tf_op jit(solution)/shard_map/dot_general | solution.py:324
  2.5 1.5 %fusion.8 = f32[9,8192]{1,0:T(8,128)S(1)} fusion(s32[8192]{0:T(1024)} %param.14, f32[1,64]{1,0:T(1,128)} %bitcast.71, f32[8,64]{1,0:T(8,128)S(1)} %copy.34), kind=kOutput, calls=%fused_computation.15 | convolution fusion | flops 57147968 | bytes 329984 | tf_op jit(solution)/shard_map/dot_general | solution.py:326
  4.1 2.8 %fusion.63 = (f32[16,8192]{1,0:T(8,128)S(1)}, f32[16,8192]{1,0:T(8,128)S(1)}) fusion(f32[16,8192]{1,0:T(8,128)} %param.10), kind=kLoop, calls=%fused_computation.94 | loop fusion | bytes 1572864 | tf_op jit(solution)/shard_map/cos | solution.py:344
  7.1 1.3 %multiply_convert_fusion.3 = (bf16[8,16,1,8192]{3,1,2,0:T(8,128)(2,1)S(1)}, bf16[8,16,1,8192]{3,1,2,0:T(8,128)(2,1)S(1)}) fusion(f32[16,8192]{1,0:T(8,128)S(1)} %get-tuple-element.42, f32[8,8192]{1,0:T(8,128)S(1)} %get-tuple-element.40, f32[16,8192]{1,0:T(8,128)S(1)} %get-tuple-element.41, f32[8,8192]{1,0:T(8,128)S(1)} %get-tuple-element.39, ...), kind=kLoop, calls=%fused_computation.10 | loop fusion | flops 10485760 | bytes 6029312 | tf_op jit(solution)/shard_map/convert.3
  8.4 0.3 fusion.22
  8.9 1.1 %fusion.7 = f32[24,64]{1,0:T(8,128)S(1)} fusion(s32[8192]{0:T(1024)S(1)} %copy-done.7, f32[8,8192]{1,0:T(8,128)S(1)} %multiply_reduce_fusion, f32[16,8192]{1,0:T(8,128)S(1)} %fusion.22), kind=kOutput, calls=%fused_computation.14 | convolution fusion | flops 151715840 | bytes 825344 | tf_op jit(solution)/shard_map/dot_general | solution.py:334
  10.3 1.4 %fusion.64 = (f32[8]{0:T(128)S(1)}, f32[8,16,16]{2,1,0:T(8,128)S(1)}) fusion(f32[8,16]{1,0:T(8,128)S(1)} %convolution_multiply_fusion.1, f32[8192]{0:T(1024)S(1)} %bitcast.70, bf16[16,2,8192]{2,1,0:T(2,128)(2,1)S(1)} %copy-done.3, bf16[8,16,1,8192]{3,1,2,0:T(8,128)(2,1)S(1)} %get-tuple-element.34, bf16[8,16,1,8192]{3,1,2,0:T(8,128)(2,1)S(1)} %get-tuple-element.33, ...), kind=kOutput, calls=%fused_computation.95 | convolution fusion | flops 69998584 | bytes 4760224 | tf_op jit(solution)/shard_map/itpk,jpk->itj/dot_general | solution.py:348
  11.7 0.6 copy-done.6
  12.6 0.6 select_maximum_fusion.1.stats_ref
  13.2 0.8 reshape.95.part_ref
  14.0 25.6 %shard_map.111 = (f32[16,8,128]{2,1,0:T(8,128)}, bf16[32,16,256]{2,1,0:T(8,128)(2,1)}) custom-call(f32[8,128]{1,0:T(8,128)} %select_maximum_fusion.1.stats_ref, bf16[16,8192]{1,0:T(8,128)(2,1)} %reshape.95.part_ref), custom_call_target="tpu_custom_call" | custom-call | tf_op jit(solution)/shard_map/pallas_call | solution.py:163
  39.5 1.0 %slice_reduce_fusion.1 = (f32[8]{0:T(128)S(1)}, f32[16,1,8]{2,1,0:T(1,128)S(1)}, f32[16,1,8]{2,1,0:T(1,128)S(1)}) fusion(f32[16,8,128]{2,1,0:T(8,128)} %get-tuple-element.9), kind=kLoop, calls=%fused_computation.91 | loop fusion | flops 120 | bytes 2080 | tf_op jit(solution)/shard_map/reduce_max | solution.py:364
  40.8 1.1 %fusion.61 = (f32[8]{0:T(128)S(1)}, f32[8,16]{1,0:T(8,128)S(1)}, f32[8,16,16]{2,1,0:T(8,128)S(1)}) fusion(f32[8]{0:T(128)S(1)} %fusion.53, f32[8,16,16]{2,1,0:T(8,128)} %copy-done.6, f32[8]{0:T(128)S(1)} %get-tuple-element.43), kind=kLoop, calls=%fused_computation.92 | loop fusion | flops 8056 | bytes 16992 | tf_op jit(solution)/shard_map/reduce_sum | solution.py:371
  41.9 0.6 copy-done.10
  42.5 2.8 %fusion.9 = f32[8192]{0:T(1024)S(1)} fusion(bf16[8,16,1,8192]{3,1,2,0:T(8,128)(2,1)} %copy-done.2, bf16[8,16,1,8192]{3,1,2,0:T(8,128)(2,1)S(1)} %get-tuple-element.33, bf16[16,2,8192]{2,1,0:T(2,128)(2,1)} %param.9, bf16[8,16,16]{2,1,0:T(8,128)(2,1)S(1)} %convert_element_type.29), kind=kOutput, calls=%fused_computation.18 | convolution fusion | flops 76275712 | bytes 4755456 | tf_op jit(solution)/shard_map/itj,itpk->jpk/dot_general | solution.py:373
  45.3 0.2 fusion.16
  45.6 1.0 %fusion.20 = f32[64]{0:T(128)S(1)} fusion(f32[64]{0:T(128)S(1)} %fusion.16, f32[64]{0:T(128)S(1)} %fusion.50, f32[8192,1]{0,1:T(1,128)S(1)} %bitcast.74, s32[8192]{0:T(1024)S(1)} %copy-done.8), kind=kOutput, calls=%fused_computation.29 | convolution fusion | flops 6815936 | bytes 66304 | tf_op jit(solution)/shard_map/dot_general | solution.py:374
  46.8 0.7 select_maximum_fusion.small_ref
  47.4 1.4 %reshape.96.half_ref = bf16[16,128]{1,0:T(8,128)(2,1)} reshape(bf16[8,16,16]{2,1,0:T(8,128)(2,1)} %copy-done.10) | data formatting | bytes 8192 | tf_op jit(solution)/shard_map/reshape | solution.py:381
  48.9 24.9 %shard_map.112 = (bf16[32,16,128]{2,1,0:T(8,128)(2,1)}, f32[32,8,128]{2,1,0:T(8,128)}, f32[16,8,128]{2,1,0:T(8,128)}) custom-call(bf16[16,128]{1,0:T(8,128)(2,1)} %reshape.96.half_ref, f32[8,128]{1,0:T(8,128)} %select_maximum_fusion.small_ref), custom_call_target="tpu_custom_call" | custom-call | tf_op jit(solution)/shard_map/pallas_call | solution.py:272
  73.8 1.8 %reshape.98 = bf16[256,16,16]{2,1,0:T(8,128)(2,1)S(1)} reshape(bf16[32,16,128]{2,1,0:T(8,128)(2,1)} %get-tuple-element.10) | data formatting | bytes 262144 | tf_op jit(solution)/shard_map/reshape | solution.py:383
  75.6 0.8 %copy.41 = bf16[256,16,16]{0,2,1:T(8,128)(2,1)S(1)} copy(bf16[256,16,16]{2,1,0:T(8,128)(2,1)S(1)} %reshape.98) | data formatting | bytes 262144 | tf_op jit(solution)/shard_map/reshape | solution.py:383
  76.5 0.3 reshape.100
  76.7 0.4 fusion.62
  77.2 0.3 iota_compare_fusion
  77.5 0.3 fusion.40
  77.8 1.4 %multiply_convert_fusion.1 = (bf16[256,16,1,256]{3,0,1,2:T(8,128)(2,1)S(1)}, bf16[256,16,1,256]{3,0,1,2:T(8,128)(2,1)S(1)}) fusion(f32[16,256]{1,0:T(8,128)S(1)} %get-tuple-element.48, f32[256,256]{1,0:T(8,128)S(1)} %get-tuple-element.50, f32[16,256]{1,0:T(8,128)S(1)} %get-tuple-element.49, f32[256,256]{1,0:T(8,128)S(1)} %get-tuple-element.51, ...), kind=kLoop, calls=%fused_computation.8 | loop fusion | flops 10485760 | bytes 5013504 | tf_op jit(solution)/shard_map/convert.1
  79.2 0.8 fusion.13
  80.0 0.6 copy.42
  80.7 1.0 %fusion.33 = f32[16,64]{1,0:T(8,128)} fusion(f32[32,8,128]{2,1,0:T(8,128)S(1)} %copy-done.11, f32[256,64]{0,1:T(8,128)S(1)} %fusion.37), kind=kOutput, calls=%fused_computation.47 | convolution fusion | flops 3162112 | bytes 200704 | tf_op jit(solution)/shard_map/dot_general | solution.py:390
  81.7 0.6 div.43
  (47 shorter events, 1.7 us)
Async XLA Ops:
  0.6 0.8 copy-start
  0.6 6.2 %copy-start.1 = (bf16[8,2,8192]{2,1,0:T(2,128)(2,1)S(1)}, bf16[8,2,8192]{2,1,0:T(2,128)(2,1)}, u32[]{:S(2)}) copy-start(bf16[8,2,8192]{2,1,0:T(2,128)(2,1)} %param.8) | copy-start | bytes 786436
  7.1 1.3 %copy-start.3 = (bf16[16,2,8192]{2,1,0:T(2,128)(2,1)S(1)}, bf16[16,2,8192]{2,1,0:T(2,128)(2,1)}, u32[]{:S(2)}) copy-start(bf16[16,2,8192]{2,1,0:T(2,128)(2,1)} %param.9) | copy-start | bytes 1572868
  7.1 1.8 %copy-start.7 = (s32[8192]{0:T(1024)S(1)}, s32[8192]{0:T(1024)}, u32[]{:S(2)}) copy-start(s32[8192]{0:T(1024)} %param.14) | copy-start | bytes 98308
  8.4 3.3 %copy-start.2 = (bf16[8,16,1,8192]{3,1,2,0:T(8,128)(2,1)}, bf16[8,16,1,8192]{3,1,2,0:T(8,128)(2,1)S(1)}, u32[]{:S(2)}) copy-start(bf16[8,16,1,8192]{3,1,2,0:T(8,128)(2,1)S(1)} %get-tuple-element.34) | copy-start | bytes 6291460
  8.4 1.7 %copy-start.14 = (f32[64]{0:T(128)S(1)}, f32[64]{0:T(128)}, u32[]{:S(2)}) copy-start(f32[64]{0:T(128)} %param.15) | copy-start | bytes 772
  8.4 1.9 %copy-start.13 = (s32[8,16]{1,0:T(8,128)S(1)}, s32[8,16]{1,0:T(8,128)}, u32[]{:S(2)}) copy-start(s32[8,16]{1,0:T(8,128)} %param.11) | copy-start | bytes 1540
  11.7 0.6 copy-start.6
  41.9 3.4 %copy-start.5 = (f32[8,16,16]{2,1,0:T(8,128)}, f32[8,16,16]{2,1,0:T(8,128)S(1)}, u32[]{:S(2)}) copy-start(f32[8,16,16]{2,1,0:T(8,128)S(1)} %get-tuple-element.32) | copy-start | bytes 24580
  41.9 0.6 copy-start.10
  42.5 3.1 %copy-start.8 = (s32[8192]{0:T(1024)S(1)}, s32[8192]{0:T(1024)}, u32[]{:S(2)}) copy-start(s32[8192]{0:T(1024)} %param.14) | copy-start | bytes 98308
  45.3 31.2 %copy-start.4 = (bf16[32,16,256]{2,1,0:T(8,128)(2,1)S(1)}, bf16[32,16,256]{2,1,0:T(8,128)(2,1)}, u32[]{:S(2)}) copy-start(bf16[32,16,256]{2,1,0:T(8,128)(2,1)} %get-tuple-element.11) | copy-start | bytes 786436
  75.6 1.6 %copy-start.9 = (s32[8192]{0:T(1024)S(1)}, s32[8192]{0:T(1024)}, u32[]{:S(2)}) copy-start(s32[8192]{0:T(1024)} %param.14) | copy-start | bytes 98308
  79.2 1.5 %copy-start.11 = (f32[32,8,128]{2,1,0:T(8,128)S(1)}, f32[32,8,128]{2,1,0:T(8,128)}, u32[]{:S(2)}) copy-start(f32[32,8,128]{2,1,0:T(8,128)} %get-tuple-element.12) | copy-start | bytes 393220
  79.2 2.4 %copy-start.12 = (f32[16,8,128]{2,1,0:T(8,128)S(1)}, f32[16,8,128]{2,1,0:T(8,128)}, u32[]{:S(2)}) copy-start(f32[16,8,128]{2,1,0:T(8,128)} %get-tuple-element.13) | copy-start | bytes 196612

commit v13 on v10

--- a/solution.py
+++ b/solution.py
@@ -114,7 +114,7 @@
         )
 
     def columns(peer):
-        return part_ref.at[:, pl.ds(pl.multiple_of(peer * width, width), width)]
+        return part_ref.at[:, pl.ds(pl.multiple_of(peer * width, width), width // 2)]
 
     def dom_copy(k):
         peer = lax.rem(me + k, dom_n)
@@ -157,7 +157,7 @@
 def stats_and_columns(stats, part_rows, dom_n, orient_n, width, collective_id):
     shapes = (
         jax.ShapeDtypeStruct((orient_n,) + stats.shape, stats.dtype),
-        jax.ShapeDtypeStruct((dom_n, part_rows.shape[0], width), part_rows.dtype),
+        jax.ShapeDtypeStruct((dom_n, part_rows.shape[0], width // 2), part_rows.dtype),
     )
     vmem = pl.BlockSpec(memory_space=pltpu.VMEM)
     return pl.pallas_call(
@@ -177,9 +177,9 @@
     )(stats, part_rows)
 
 
-def _spread_kernel(dom_n, orient_n, half_ref, small_ref,
-                   half_out, small_out, terms_out,
-                   half_held, small_held, summed, terms_held,
+def _spread_kernel(dom_n, orient_n, width, half_ref, small_ref, part_ref,
+                   half_out, small_out, part_out, terms_out,
+                   half_held, small_held, part_held, summed, terms_held,
                    send_sem, recv_sem, orient_send, orient_recv):
     me = lax.axis_index("dom")
     mine = lax.axis_index("orient")
@@ -199,13 +199,18 @@
     lax.fori_loop(1, orient_n, greet_orient, 0)
     pl.semaphore_wait(barrier, dom_n + orient_n - 2)
 
-    sources = (half_ref, small_ref)
-    held = (half_held, small_held)
+    half_width = width // 2
+
+    def columns(peer):
+        return part_ref.at[:, pl.ds(pl.multiple_of(peer * width + half_width, half_width), half_width)]
+
+    sources = (lambda peer: half_ref, lambda peer: small_ref, columns)
+    held = (half_held, small_held, part_held)
 
     def copy(index, k):
         peer = lax.rem(me + k, dom_n)
         return pltpu.make_async_remote_copy(
-            src_ref=sources[index],
+            src_ref=sources[index](peer),
             dst_ref=held[index].at[me],
             send_sem=send_sem.at[index, k],
             recv_sem=recv_sem.at[index, k],
@@ -214,13 +219,13 @@
         )
 
     def start(k, carry):
-        for index in (1, 0):
+        for index in (1, 0, 2):
             copy(index, k).start()
         return carry
 
     lax.fori_loop(1, dom_n, start, 0)
-    for index in range(2):
-        held[index][me] = sources[index][...]
+    for index in range(3):
+        held[index][me] = sources[index](me)[...]
 
     def finish(index):
         def body(k, carry):
@@ -250,6 +255,7 @@
 
     lax.fori_loop(1, orient_n, orient_start, 0)
     terms_held[mine] = summed[...]
+    finish(2)
 
     def orient_finish(k, carry):
         orient_copy(k).wait()
@@ -258,33 +264,36 @@
     lax.fori_loop(1, orient_n, orient_finish, 0)
     half_out[...] = half_held[...]
     small_out[...] = small_held[...]
+    part_out[...] = part_held[...]
     terms_out[...] = terms_held[...]
 
 
-def spread(half_rows, small, dom_n, orient_n, collective_id):
+def spread(half_rows, small, part_rows, dom_n, orient_n, width, collective_id):
     shapes = (
         jax.ShapeDtypeStruct((dom_n,) + half_rows.shape, half_rows.dtype),
         jax.ShapeDtypeStruct((dom_n,) + small.shape, small.dtype),
+        jax.ShapeDtypeStruct((dom_n, part_rows.shape[0], width // 2), part_rows.dtype),
         jax.ShapeDtypeStruct((orient_n,) + small.shape, small.dtype),
     )
     vmem = pl.BlockSpec(memory_space=pltpu.VMEM)
     return pl.pallas_call(
-        functools.partial(_spread_kernel, dom_n, orient_n),
+        functools.partial(_spread_kernel, dom_n, orient_n, width),
         out_shape=shapes,
-        in_specs=[vmem] * 2,
-        out_specs=(vmem,) * 3,
+        in_specs=[vmem] * 3,
+        out_specs=(vmem,) * 4,
         scratch_shapes=[
             pltpu.VMEM(shapes[0].shape, shapes[0].dtype),
             pltpu.VMEM(shapes[1].shape, shapes[1].dtype),
+            pltpu.VMEM(shapes[2].shape, shapes[2].dtype),
             pltpu.VMEM(small.shape, small.dtype),
-            pltpu.VMEM(shapes[2].shape, shapes[2].dtype),
-            pltpu.SemaphoreType.DMA((2, dom_n)),
-            pltpu.SemaphoreType.DMA((2, dom_n)),
+            pltpu.VMEM(shapes[3].shape, shapes[3].dtype),
+            pltpu.SemaphoreType.DMA((3, dom_n)),
+            pltpu.SemaphoreType.DMA((3, dom_n)),
             pltpu.SemaphoreType.DMA((orient_n,)),
             pltpu.SemaphoreType.DMA((orient_n,)),
         ],
         compiler_params=pltpu.CompilerParams(collective_id=collective_id, has_side_effects=True),
-    )(half_rows, small)
+    )(half_rows, small, part_rows)
 
 
 def make_images(planes, ctf_pix, cosine, sine_part):
@@ -350,9 +359,10 @@
     local_peak = jnp.max(scores, axis=(1, 2))
     local_total = jnp.sum(jnp.exp(scores - local_peak[:, None, None]), axis=(1, 2))
 
-    stats, columns = stats_and_columns(
+    part_rows = particles.reshape(part_dev * 2, pixels)
+    stats, columns_a = stats_and_columns(
         pad_rows(jnp.stack([local_peak, local_total]), 128),
-        particles.reshape(part_dev * 2, pixels),
+        part_rows,
         dom_size,
         orient_size,
         width,
@@ -378,7 +388,10 @@
     small = jnp.concatenate([weight_rows, term_rows], axis=1)
     small = jnp.pad(small, ((0, 0), (0, -(-small.shape[1] // 128) * 128 - small.shape[1])))
     half_rows = post_half.reshape(-1, 128)
-    half_all, small_all, orient_small = spread(half_rows, small, dom_size, orient_size, 2)
+    half_all, small_all, columns_b, orient_small = spread(
+        half_rows, small, part_rows, dom_size, orient_size, width, 2
+    )
+    columns = jnp.concatenate([columns_a, columns_b], axis=2)
     post_all = half_all.reshape(dom_size * part_dev, trans_count, ori_dev)
     weight_all = small_all[:, :, :ori_dev].reshape(dom_size * part_dev, ori_dev)
     shell_total = jnp.sum(

time: 83.1 us -> 85.8 us (1.032)
  other arithmetic: 7.47 us -> 11.7 us
  local copies, waits for them, and re-layouts: 12.1 us -> 8.94 us
  matrix products: 11.3 us -> 12.8 us
    pallas_call x1, Pallas kernels: 25.2 us -> 26.7 us  [spread(): pl.pallas_call(functools.partial(_spread_kernel, dom_n, orient_n, width),...]
    dot_general x1, matrix products: 0.8 us -> 2.28 us  [on_device(): jnp.einsum('itj,itpk->jpk', post_all, col_images, preferred_element_type=...]
    pallas_call x1, Pallas kernels: 25.6 us -> 24.1 us  [stats_and_columns(): pl.pallas_call(functools.partial(_stats_kernel, dom_n, orient_n, width),...]
    another operation x2, other arithmetic: 2.67 us -> 3.9 us
    reduce_sum x1, other arithmetic: 0.31 us -> 1.44 us  [on_device(): jnp.sum(refs_wide * refs_wide, axis=1)]
    reshape x2, local copies, waits for them, and re-layouts: 2.58 us -> 1.49 us  [on_device(): post_all = half_all.reshape(dom_size * part_dev, trans_count, ori_dev)]
    reduce_sum x1, other arithmetic: 0.15 us -> 1.13 us  [on_device(): jnp.sum(planes * planes, axis=1)]
    convert_element_type x0 -> x1, other arithmetic: none -> 0.94 us  [on_device(): columns.reshape(dom_size * part_dev, 2, width).astype(jnp.float32)]
where the time goes in v13:
time: 85.8 us; the launch traced here: 85.2 us
  Pallas kernels  50.8 us (59%)
  matrix products  12.8 us (15%)
  other arithmetic  11.7 us (14%)
  local copies, waits for them, and re-layouts  8.94 us (10%)
  between operations  0.97 us (1%)
    pallas_call x1, Pallas kernels, spread(): pl.pallas_call(functools.partial(_spread_kernel, dom_n, orient_n, width),...  26.7 us
    pallas_call x1, Pallas kernels, stats_and_columns(): pl.pallas_call(functools.partial(_stats_kernel, dom_n, orient_n, width),...  24.1 us
    another operation x2, other arithmetic  3.9 us
    dot_general x1, matrix products, on_device(): jnp.einsum('itj,itpk->jpk', post_half, images, preferred_element_type=jnp...  2.78 us
    dot_general x1, matrix products, on_device(): jnp.einsum('itj,itpk->jpk', post_all, col_images, preferred_element_type=...  2.28 us
    unnamed x32, local copies, waits for them, and re-layouts  2.11 us
    cos x1, local copies, waits for them, and re-layouts, on_device(): cosines = jnp.cos(phases)  2.04 us
    dot_general x1, matrix products, on_device(): jnp.dot(jnp.concatenate([jnp.sum(refs_wide * refs_wide, axis=1), jnp.sum(...  1.89 us

profile of v13, /device:TPU:1, one launch (start us, length us, event | category | flops | bytes accessed | tf_op | source)
XLA Modules:
  0.0 85.2 jit_solution(639718230919096181)
XLA Ops:
  0.7 0.7 copy-done
  1.4 1.0 %fusion.37 = f32[256,64]{0,1:T(8,128)S(1)} fusion(f32[64,64]{1,0:T(8,128)S(1)} %copy-done, s32[256]{0:T(256)} %param.12), kind=kOutput, calls=%fused_computation.53 | convolution fusion | flops 12599296 | bytes 82944 | tf_op jit(solution)/shard_map/dot_general | solution.py:332
  2.5 1.1 %multiply_reduce_fusion = f32[8,8192]{1,0:T(8,128)S(1)} fusion(bf16[8,2,8192]{2,1,0:T(2,128)(2,1)} %param.8), kind=kLoop, calls=%fused_computation.39 | loop fusion | flops 327680 | bytes 524288 | tf_op jit(solution)/shard_map/reduce_sum | solution.py:343
  3.6 1.4 %fusion.22 = f32[16,8192]{1,0:T(8,128)S(1)} fusion(bf16[16,2,8192]{2,1,0:T(2,128)(2,1)} %param.9), kind=kLoop, calls=%fused_computation.31 | loop fusion | flops 655360 | bytes 1048576 | tf_op jit(solution)/shard_map/reduce_sum | solution.py:343
  5.0 1.9 %fusion.7 = f32[24,64]{1,0:T(8,128)S(1)} fusion(s32[8192]{0:T(1024)} %param.14, f32[8,8192]{1,0:T(8,128)S(1)} %multiply_reduce_fusion, f32[16,8192]{1,0:T(8,128)S(1)} %fusion.22), kind=kOutput, calls=%fused_computation.14 | convolution fusion | flops 151715840 | bytes 825344 | tf_op jit(solution)/shard_map/dot_general | solution.py:342
  7.2 0.8 fusion.8
  8.0 2.0 %fusion.63 = (f32[16,8192]{1,0:T(8,128)S(1)}, f32[16,8192]{1,0:T(8,128)S(1)}) fusion(f32[16,8192]{1,0:T(8,128)S(1)} %copy-done.3), kind=kLoop, calls=%fused_computation.95 | loop fusion | bytes 1572864 | tf_op jit(solution)/shard_map/cos | solution.py:352
  10.4 1.3 %multiply_convert_fusion.3 = (bf16[8,16,1,8192]{3,1,2,0:T(8,128)(2,1)S(1)}, bf16[8,16,1,8192]{3,1,2,0:T(8,128)(2,1)S(1)}) fusion(f32[16,8192]{1,0:T(8,128)S(1)} %get-tuple-element.44, f32[8,8192]{1,0:T(8,128)S(1)} %get-tuple-element.42, f32[16,8192]{1,0:T(8,128)S(1)} %get-tuple-element.43, f32[8,8192]{1,0:T(8,128)S(1)} %get-tuple-element.41, ...), kind=kLoop, calls=%fused_computation.10 | loop fusion | flops 10485760 | bytes 6029312 | tf_op jit(solution)/shard_map/convert.3
  11.7 1.4 %fusion.64 = (f32[8]{0:T(128)S(1)}, f32[8,16,16]{2,1,0:T(8,128)S(1)}) fusion(f32[8,16]{1,0:T(8,128)S(1)} %convolution_multiply_fusion.1, f32[8192]{0:T(1024)S(1)} %bitcast.70, bf16[16,2,8192]{2,1,0:T(2,128)(2,1)S(1)} %copy-done.4, bf16[8,16,1,8192]{3,1,2,0:T(8,128)(2,1)S(1)} %get-tuple-element.36, bf16[8,16,1,8192]{3,1,2,0:T(8,128)(2,1)S(1)} %get-tuple-element.35, ...), kind=kOutput, calls=%fused_computation.96 | convolution fusion | flops 69998584 | bytes 4760224 | tf_op jit(solution)/shard_map/itpk,jpk->itj/dot_general | solution.py:356
  13.1 0.6 copy-done.6
  13.9 0.6 select_maximum_fusion.1.stats_ref
  14.5 0.8 reshape.95.part_ref
  15.3 24.1 %shard_map.111 = (f32[16,8,128]{2,1,0:T(8,128)}, bf16[32,16,128]{2,1,0:T(8,128)(2,1)}) custom-call(f32[8,128]{1,0:T(8,128)} %select_maximum_fusion.1.stats_ref, bf16[16,8192]{1,0:T(8,128)(2,1)} %reshape.95.part_ref), custom_call_target="tpu_custom_call" | custom-call | tf_op jit(solution)/shard_map/pallas_call | solution.py:163
  39.4 1.0 %slice_reduce_fusion.1 = (f32[8]{0:T(128)S(1)}, f32[16,1,8]{2,1,0:T(1,128)S(1)}, f32[16,1,8]{2,1,0:T(1,128)S(1)}) fusion(f32[16,8,128]{2,1,0:T(8,128)} %get-tuple-element.10), kind=kLoop, calls=%fused_computation.92 | loop fusion | flops 120 | bytes 2080 | tf_op jit(solution)/shard_map/reduce_max | solution.py:373
  40.7 1.1 %fusion.61 = (f32[8]{0:T(128)S(1)}, f32[8,16]{1,0:T(8,128)S(1)}, f32[8,16,16]{2,1,0:T(8,128)S(1)}) fusion(f32[8]{0:T(128)S(1)} %fusion.53, f32[8,16,16]{2,1,0:T(8,128)} %copy-done.6, f32[8]{0:T(128)S(1)} %get-tuple-element.45), kind=kLoop, calls=%fused_computation.93 | loop fusion | flops 8056 | bytes 16992 | tf_op jit(solution)/shard_map/reduce_sum | solution.py:380
  41.8 0.7 reshape.96.half_ref
  42.8 2.8 %fusion.9 = f32[8192]{0:T(1024)S(1)} fusion(bf16[8,16,1,8192]{3,1,2,0:T(8,128)(2,1)} %copy-done.2, bf16[8,16,1,8192]{3,1,2,0:T(8,128)(2,1)S(1)} %get-tuple-element.35, bf16[16,2,8192]{2,1,0:T(2,128)(2,1)} %param.9, bf16[8,16,16]{2,1,0:T(8,128)(2,1)S(1)} %convert_element_type.29), kind=kOutput, calls=%fused_computation.18 | convolution fusion | flops 76275712 | bytes 4755456 | tf_op jit(solution)/shard_map/itj,itpk->jpk/dot_general | solution.py:382
  45.6 1.0 %fusion.20 = f32[64]{0:T(128)S(1)} fusion(f32[64]{0:T(128)S(1)} %fusion.16, f32[64]{0:T(128)S(1)} %fusion.50, f32[8192,1]{0,1:T(1,128)S(1)} %bitcast.74, s32[8192]{0:T(1024)S(1)} %copy-done.9), kind=kOutput, calls=%fused_computation.29 | convolution fusion | flops 6815936 | bytes 66304 | tf_op jit(solution)/shard_map/dot_general | solution.py:383
  46.8 0.7 select_maximum_fusion.small_ref
  47.5 26.7 %shard_map.112 = (bf16[32,16,128]{2,1,0:T(8,128)(2,1)}, f32[32,8,128]{2,1,0:T(8,128)}, bf16[32,16,128]{2,1,0:T(8,128)(2,1)}, f32[16,8,128]{2,1,0:T(8,128)}) custom-call(bf16[16,128]{1,0:T(8,128)(2,1)} %reshape.96.half_ref, f32[8,128]{1,0:T(8,128)} %select_maximum_fusion.small_ref, bf16[16,8192]{1,0:T(8,128)(2,1)} %reshape.95.part_ref), custom_call_target="tpu_custom_call" | custom-call | tf_op jit(solution)/shard_map/pallas_call | solution.py:279
  74.2 0.9 %maximum_convert_fusion = f32[32,16,256]{2,1,0:T(8,128)S(1)} fusion(bf16[32,16,128]{2,1,0:T(8,128)(2,1)} %get-tuple-element.13, bf16[32,16,128]{2,1,0:T(8,128)(2,1)S(1)} %copy-done.11), kind=kLoop, calls=%fused_computation.44 | loop fusion | flops 524288 | bytes 786432 | tf_op jit(solution)/shard_map/convert_element_type | solution.py:409
  75.1 0.3 reshape.100
  75.4 0.4 fusion.62
  75.9 0.3 iota_compare_fusion
  76.2 0.3 fusion.40
  76.5 2.6 %multiply_convert_fusion.1 = (bf16[256,16,1,256]{3,0,1,2:T(8,128)(2,1)S(1)}, bf16[256,16,1,256]{3,0,1,2:T(8,128)(2,1)}) fusion(f32[16,256]{1,0:T(8,128)S(1)} %get-tuple-element.50, f32[256,256]{1,0:T(8,128)S(1)} %get-tuple-element.52, f32[16,256]{1,0:T(8,128)S(1)} %get-tuple-element.51, f32[256,256]{1,0:T(8,128)S(1)} %get-tuple-element.53, ...), kind=kLoop, calls=%fused_computation.8 | loop fusion | flops 10485760 | bytes 5013504 | tf_op jit(solution)/shard_map/convert.1
  79.2 0.7 reshape.98
  79.8 0.8 copy.41
  80.7 2.3 %fusion.13 = f32[16,2,256]{2,0,1:T(8,128)S(1)} fusion(bf16[256,16,1,256]{3,0,1,2:T(8,128)(2,1)} %get-tuple-element.38, bf16[256,16,1,256]{3,0,1,2:T(8,128)(2,1)S(1)} %get-tuple-element.37, bf16[256,16,16]{0,2,1:T(8,128)(2,1)S(1)} %copy.41), kind=kOutput, calls=%fused_computation.22 | convolution fusion | flops 75497472 | bytes 4358144 | tf_op jit(solution)/shard_map/itj,itpk->jpk/dot_general | solution.py:411
  82.9 0.6 copy.42
  83.6 1.0 %fusion.33 = f32[16,64]{1,0:T(8,128)} fusion(f32[32,8,128]{2,1,0:T(8,128)S(1)} %copy-done.10, f32[256,64]{0,1:T(8,128)S(1)} %fusion.37), kind=kOutput, calls=%fused_computation.48 | convolution fusion | flops 3162112 | bytes 200704 | tf_op jit(solution)/shard_map/dot_general | solution.py:402
  84.6 0.6 div.43
  (48 shorter events, 1.8 us)
Async XLA Ops:
  0.6 0.8 copy-start
  0.6 6.6 %copy-start.8 = (s32[8192]{0:T(1024)S(1)}, s32[8192]{0:T(1024)}, u32[]{:S(2)}) copy-start(s32[8192]{0:T(1024)} %param.14) | copy-start | bytes 98308
  0.7 6.3 %copy-start.14 = (f32[64]{0:T(128)S(1)}, f32[64]{0:T(128)}, u32[]{:S(2)}) copy-start(f32[64]{0:T(128)} %param.15) | copy-start | bytes 772
  0.7 7.4 %copy-start.3 = (f32[16,8192]{1,0:T(8,128)S(1)}, f32[16,8192]{1,0:T(8,128)}, u32[]{:S(2)}) copy-start(f32[16,8192]{1,0:T(8,128)} %param.10) | copy-start | bytes 1572868
  3.6 6.5 %copy-start.1 = (bf16[8,2,8192]{2,1,0:T(2,128)(2,1)S(1)}, bf16[8,2,8192]{2,1,0:T(2,128)(2,1)}, u32[]{:S(2)}) copy-start(bf16[8,2,8192]{2,1,0:T(2,128)(2,1)} %param.8) | copy-start | bytes 786436
  10.3 1.3 %copy-start.13 = (s32[8,16]{1,0:T(8,128)S(1)}, s32[8,16]{1,0:T(8,128)}, u32[]{:S(2)}) copy-start(s32[8,16]{1,0:T(8,128)} %param.11) | copy-start | bytes 1540
  10.3 1.3 %copy-start.4 = (bf16[16,2,8192]{2,1,0:T(2,128)(2,1)S(1)}, bf16[16,2,8192]{2,1,0:T(2,128)(2,1)}, u32[]{:S(2)}) copy-start(bf16[16,2,8192]{2,1,0:T(2,128)(2,1)} %param.9) | copy-start | bytes 1572868
  11.6 1.4 %copy-start.2 = (bf16[8,16,1,8192]{3,1,2,0:T(8,128)(2,1)}, bf16[8,16,1,8192]{3,1,2,0:T(8,128)(2,1)S(1)}, u32[]{:S(2)}) copy-start(bf16[8,16,1,8192]{3,1,2,0:T(8,128)(2,1)S(1)} %get-tuple-element.36) | copy-start | bytes 6291460
  13.0 0.6 copy-start.6
  41.8 3.8 %copy-start.5 = (f32[8,16,16]{2,1,0:T(8,128)}, f32[8,16,16]{2,1,0:T(8,128)S(1)}, u32[]{:S(2)}) copy-start(f32[8,16,16]{2,1,0:T(8,128)S(1)} %get-tuple-element.34) | copy-start | bytes 24580
  42.8 2.8 %copy-start.9 = (s32[8192]{0:T(1024)S(1)}, s32[8192]{0:T(1024)}, u32[]{:S(2)}) copy-start(s32[8192]{0:T(1024)} %param.14) | copy-start | bytes 98308
  42.8 31.3 %copy-start.11 = (bf16[32,16,128]{2,1,0:T(8,128)(2,1)S(1)}, bf16[32,16,128]{2,1,0:T(8,128)(2,1)}, u32[]{:S(2)}) copy-start(bf16[32,16,128]{2,1,0:T(8,128)(2,1)} %get-tuple-element.12) | copy-start | bytes 393220
  76.5 2.6 %copy-start.7 = (bf16[32,16,128]{2,1,0:T(8,128)(2,1)S(1)}, bf16[32,16,128]{2,1,0:T(8,128)(2,1)}, u32[]{:S(2)}) copy-start(bf16[32,16,128]{2,1,0:T(8,128)(2,1)} %get-tuple-element.11) | copy-start | bytes 393220
  80.7 2.9 %copy-start.10 = (f32[32,8,128]{2,1,0:T(8,128)S(1)}, f32[32,8,128]{2,1,0:T(8,128)}, u32[]{:S(2)}) copy-start(f32[32,8,128]{2,1,0:T(8,128)} %get-tuple-element.14) | copy-start | bytes 393220
  80.7 3.9 %copy-start.12 = (f32[16,8,128]{2,1,0:T(8,128)S(1)}, f32[16,8,128]{2,1,0:T(8,128)}, u32[]{:S(2)}) copy-start(f32[16,8,128]{2,1,0:T(8,128)} %get-tuple-element.15) | copy-start | bytes 196612

commit v14 on v10

--- a/solution.py
+++ b/solution.py
@@ -83,9 +83,13 @@
 
 
 def _stats_kernel(dom_n, orient_n, width, stats_ref, part_ref, stats_out, part_out,
-                  stats_held, part_held, orient_send, orient_recv, dom_send, dom_recv):
+                  stats_held, part_held, orient_send, orient_recv, dom_send, dom_recv,
+                  pass_send, pass_recv):
     me = lax.axis_index("dom")
     mine = lax.axis_index("orient")
+    core = lax.rem(mine, 2)
+    partner = mine + 1 - 2 * core
+    half = width // 2
     barrier = pltpu.get_barrier_semaphore()
 
     def greet_dom(k, carry):
@@ -113,20 +117,30 @@
             device_id_type=MESH_ID,
         )
 
-    def columns(peer):
-        return part_ref.at[:, pl.ds(pl.multiple_of(peer * width, width), width)]
+    lanes = pl.ds(pl.multiple_of(core * half, half), half)
 
     def dom_copy(k):
         peer = lax.rem(me + k, dom_n)
         return pltpu.make_async_remote_copy(
-            src_ref=columns(peer),
-            dst_ref=part_held.at[me],
+            src_ref=part_ref.at[:, pl.ds(pl.multiple_of(peer * width + core * half, half), half)],
+            dst_ref=part_held.at[me, :, lanes],
             send_sem=dom_send.at[k],
             recv_sem=dom_recv.at[k],
             device_id={"dom": peer},
             device_id_type=MESH_ID,
         )
 
+    def pass_copy(k):
+        source = lax.rem(me + dom_n - k, dom_n)
+        return pltpu.make_async_remote_copy(
+            src_ref=part_held.at[source, :, lanes],
+            dst_ref=part_held.at[source, :, lanes],
+            send_sem=pass_send.at[k],
+            recv_sem=pass_recv.at[k],
+            device_id={"orient": partner},
+            device_id_type=MESH_ID,
+        )
+
     def orient_start(k, carry):
         orient_copy(k).start()
         return carry
@@ -138,14 +152,22 @@
     lax.fori_loop(1, orient_n, orient_start, 0)
     lax.fori_loop(1, dom_n, dom_start, 0)
     stats_held[mine] = stats_ref[...]
-    part_held[me] = columns(me)[...]
+    part_held[me] = part_ref[:, pl.ds(pl.multiple_of(me * width, width), width)]
+
+    def pass_on(k, carry):
+        dom_copy(k).wait_recv()
+        pass_copy(k).start()
+        return carry
+
+    lax.fori_loop(1, dom_n, pass_on, 0)
 
     def orient_finish(k, carry):
         orient_copy(k).wait()
         return carry
 
     def dom_finish(k, carry):
-        dom_copy(k).wait()
+        dom_copy(k).wait_send()
+        pass_copy(k).wait()
         return carry
 
     lax.fori_loop(1, orient_n, orient_finish, 0)
@@ -170,6 +192,8 @@
             pltpu.VMEM(shapes[1].shape, shapes[1].dtype),
             pltpu.SemaphoreType.DMA((orient_n,)),
             pltpu.SemaphoreType.DMA((orient_n,)),
+            pltpu.SemaphoreType.DMA((dom_n,)),
+            pltpu.SemaphoreType.DMA((dom_n,)),
             pltpu.SemaphoreType.DMA((dom_n,)),
             pltpu.SemaphoreType.DMA((dom_n,)),
         ],

time: 83.1 us -> 83.1 us (level)
    pallas_call x1, Pallas kernels: 25.2 us -> 23.9 us  [spread(): pl.pallas_call(functools.partial(_spread_kernel, dom_n, orient_n), out_sh...]
    pallas_call x1, Pallas kernels: 25.6 us -> 26.7 us  [stats_and_columns(): pl.pallas_call(functools.partial(_stats_kernel, dom_n, orient_n, width),...]
where the time goes in v14:
time: 83.1 us; the launch traced here: 82.6 us
  Pallas kernels  50.6 us (61%)
  local copies, waits for them, and re-layouts  12.3 us (15%)
  matrix products  11.3 us (14%)
  other arithmetic  7.47 us (9%)
  between operations  0.98 us (1%)
    pallas_call x1, Pallas kernels, stats_and_columns(): pl.pallas_call(functools.partial(_stats_kernel, dom_n, orient_n, width),...  26.7 us
    pallas_call x1, Pallas kernels, spread(): pl.pallas_call(functools.partial(_spread_kernel, dom_n, orient_n), out_sh...  23.9 us
    cos x1, local copies, waits for them, and re-layouts, on_device(): cosines = jnp.cos(phases)  2.8 us
    reshape x2, local copies, waits for them, and re-layouts, on_device(): post_all = half_all.reshape(dom_size * part_dev, trans_count, ori_dev)  2.77 us
    dot_general x1, matrix products, on_device(): jnp.einsum('itj,itpk->jpk', post_half, images, preferred_element_type=jnp...  2.75 us
    unnamed x32, local copies, waits for them, and re-layouts  2.74 us
    another operation x2, other arithmetic  2.67 us

profile of v14, /device:TPU:1, one launch (start us, length us, event | category | flops | bytes accessed | tf_op | source)
XLA Modules:
  0.0 82.6 jit_solution(12459742788415564853)
XLA Ops:
  0.7 0.7 copy-done
  1.4 1.0 %fusion.37 = f32[256,64]{0,1:T(8,128)S(1)} fusion(f32[64,64]{1,0:T(8,128)S(1)} %copy-done, s32[256]{0:T(256)} %param.12), kind=kOutput, calls=%fused_computation.52 | convolution fusion | flops 12599296 | bytes 82944 | tf_op jit(solution)/shard_map/dot_general | solution.py:347
  2.5 1.5 %fusion.8 = f32[9,8192]{1,0:T(8,128)S(1)} fusion(s32[8192]{0:T(1024)} %param.14, f32[1,64]{1,0:T(1,128)} %bitcast.71, f32[8,64]{1,0:T(8,128)S(1)} %copy.34), kind=kOutput, calls=%fused_computation.15 | convolution fusion | flops 57147968 | bytes 329984 | tf_op jit(solution)/shard_map/dot_general | solution.py:349
  4.1 2.8 %fusion.63 = (f32[16,8192]{1,0:T(8,128)S(1)}, f32[16,8192]{1,0:T(8,128)S(1)}) fusion(f32[16,8192]{1,0:T(8,128)} %param.10), kind=kLoop, calls=%fused_computation.94 | loop fusion | bytes 1572864 | tf_op jit(solution)/shard_map/cos | solution.py:367
  7.1 1.3 %multiply_convert_fusion.3 = (bf16[8,16,1,8192]{3,1,2,0:T(8,128)(2,1)S(1)}, bf16[8,16,1,8192]{3,1,2,0:T(8,128)(2,1)S(1)}) fusion(f32[16,8192]{1,0:T(8,128)S(1)} %get-tuple-element.42, f32[8,8192]{1,0:T(8,128)S(1)} %get-tuple-element.40, f32[16,8192]{1,0:T(8,128)S(1)} %get-tuple-element.41, f32[8,8192]{1,0:T(8,128)S(1)} %get-tuple-element.39, ...), kind=kLoop, calls=%fused_computation.10 | loop fusion | flops 10485760 | bytes 6029312 | tf_op jit(solution)/shard_map/convert.3
  8.4 0.3 fusion.22
  8.9 1.1 %fusion.7 = f32[24,64]{1,0:T(8,128)S(1)} fusion(s32[8192]{0:T(1024)S(1)} %copy-done.7, f32[8,8192]{1,0:T(8,128)S(1)} %multiply_reduce_fusion, f32[16,8192]{1,0:T(8,128)S(1)} %fusion.22), kind=kOutput, calls=%fused_computation.14 | convolution fusion | flops 151715840 | bytes 825344 | tf_op jit(solution)/shard_map/dot_general | solution.py:357
  10.3 1.4 %fusion.64 = (f32[8]{0:T(128)S(1)}, f32[8,16,16]{2,1,0:T(8,128)S(1)}) fusion(f32[8,16]{1,0:T(8,128)S(1)} %convolution_multiply_fusion.1, f32[8192]{0:T(1024)S(1)} %bitcast.70, bf16[16,2,8192]{2,1,0:T(2,128)(2,1)S(1)} %copy-done.3, bf16[8,16,1,8192]{3,1,2,0:T(8,128)(2,1)S(1)} %get-tuple-element.34, bf16[8,16,1,8192]{3,1,2,0:T(8,128)(2,1)S(1)} %get-tuple-element.33, ...), kind=kOutput, calls=%fused_computation.95 | convolution fusion | flops 69998584 | bytes 4760224 | tf_op jit(solution)/shard_map/itpk,jpk->itj/dot_general | solution.py:371
  11.7 0.6 copy-done.6
  12.6 0.6 select_maximum_fusion.1.stats_ref
  13.2 0.8 reshape.95.part_ref
  14.0 26.7 %shard_map.111 = (f32[16,8,128]{2,1,0:T(8,128)}, bf16[32,16,256]{2,1,0:T(8,128)(2,1)}) custom-call(f32[8,128]{1,0:T(8,128)} %select_maximum_fusion.1.stats_ref, bf16[16,8192]{1,0:T(8,128)(2,1)} %reshape.95.part_ref), custom_call_target="tpu_custom_call" | custom-call | tf_op jit(solution)/shard_map/pallas_call | solution.py:185
  40.6 1.0 %slice_reduce_fusion.1 = (f32[8]{0:T(128)S(1)}, f32[16,1,8]{2,1,0:T(1,128)S(1)}, f32[16,1,8]{2,1,0:T(1,128)S(1)}) fusion(f32[16,8,128]{2,1,0:T(8,128)} %get-tuple-element.9), kind=kLoop, calls=%fused_computation.91 | loop fusion | flops 120 | bytes 2080 | tf_op jit(solution)/shard_map/reduce_max | solution.py:387
  41.9 1.1 %fusion.61 = (f32[8]{0:T(128)S(1)}, f32[8,16]{1,0:T(8,128)S(1)}, f32[8,16,16]{2,1,0:T(8,128)S(1)}) fusion(f32[8]{0:T(128)S(1)} %fusion.53, f32[8,16,16]{2,1,0:T(8,128)} %copy-done.6, f32[8]{0:T(128)S(1)} %get-tuple-element.43), kind=kLoop, calls=%fused_computation.92 | loop fusion | flops 8056 | bytes 16992 | tf_op jit(solution)/shard_map/reduce_sum | solution.py:394
  43.0 0.6 copy-done.10
  43.6 2.8 %fusion.9 = f32[8192]{0:T(1024)S(1)} fusion(bf16[8,16,1,8192]{3,1,2,0:T(8,128)(2,1)} %copy-done.2, bf16[8,16,1,8192]{3,1,2,0:T(8,128)(2,1)S(1)} %get-tuple-element.33, bf16[16,2,8192]{2,1,0:T(2,128)(2,1)} %param.9, bf16[8,16,16]{2,1,0:T(8,128)(2,1)S(1)} %convert_element_type.29), kind=kOutput, calls=%fused_computation.18 | convolution fusion | flops 76275712 | bytes 4755456 | tf_op jit(solution)/shard_map/itj,itpk->jpk/dot_general | solution.py:396
  46.4 0.2 fusion.16
  46.7 1.0 %fusion.20 = f32[64]{0:T(128)S(1)} fusion(f32[64]{0:T(128)S(1)} %fusion.16, f32[64]{0:T(128)S(1)} %fusion.50, f32[8192,1]{0,1:T(1,128)S(1)} %bitcast.74, s32[8192]{0:T(1024)S(1)} %copy-done.8), kind=kOutput, calls=%fused_computation.29 | convolution fusion | flops 6815936 | bytes 66304 | tf_op jit(solution)/shard_map/dot_general | solution.py:397
  47.9 0.7 select_maximum_fusion.small_ref
  48.5 1.4 %reshape.96.half_ref = bf16[16,128]{1,0:T(8,128)(2,1)} reshape(bf16[8,16,16]{2,1,0:T(8,128)(2,1)} %copy-done.10) | data formatting | bytes 8192 | tf_op jit(solution)/shard_map/reshape | solution.py:404
  50.0 23.9 %shard_map.112 = (bf16[32,16,128]{2,1,0:T(8,128)(2,1)}, f32[32,8,128]{2,1,0:T(8,128)}, f32[16,8,128]{2,1,0:T(8,128)}) custom-call(bf16[16,128]{1,0:T(8,128)(2,1)} %reshape.96.half_ref, f32[8,128]{1,0:T(8,128)} %select_maximum_fusion.small_ref), custom_call_target="tpu_custom_call" | custom-call | tf_op jit(solution)/shard_map/pallas_call | solution.py:295
  73.9 1.9 %reshape.98 = bf16[256,16,16]{2,1,0:T(8,128)(2,1)S(1)} reshape(bf16[32,16,128]{2,1,0:T(8,128)(2,1)} %get-tuple-element.10) | data formatting | bytes 262144 | tf_op jit(solution)/shard_map/reshape | solution.py:406
  75.9 0.8 %copy.41 = bf16[256,16,16]{0,2,1:T(8,128)(2,1)S(1)} copy(bf16[256,16,16]{2,1,0:T(8,128)(2,1)S(1)} %reshape.98) | data formatting | bytes 262144 | tf_op jit(solution)/shard_map/reshape | solution.py:406
  76.7 0.3 reshape.100
  77.0 0.4 fusion.62
  77.4 0.3 iota_compare_fusion
  77.7 0.3 fusion.40
  78.1 1.4 %multiply_convert_fusion.1 = (bf16[256,16,1,256]{3,0,1,2:T(8,128)(2,1)S(1)}, bf16[256,16,1,256]{3,0,1,2:T(8,128)(2,1)S(1)}) fusion(f32[16,256]{1,0:T(8,128)S(1)} %get-tuple-element.48, f32[256,256]{1,0:T(8,128)S(1)} %get-tuple-element.50, f32[16,256]{1,0:T(8,128)S(1)} %get-tuple-element.49, f32[256,256]{1,0:T(8,128)S(1)} %get-tuple-element.51, ...), kind=kLoop, calls=%fused_computation.8 | loop fusion | flops 10485760 | bytes 5013504 | tf_op jit(solution)/shard_map/convert.1
  79.5 0.8 fusion.13
  80.3 0.6 copy.42
  80.9 1.0 %fusion.33 = f32[16,64]{1,0:T(8,128)} fusion(f32[32,8,128]{2,1,0:T(8,128)S(1)} %copy-done.11, f32[256,64]{0,1:T(8,128)S(1)} %fusion.37), kind=kOutput, calls=%fused_computation.47 | convolution fusion | flops 3162112 | bytes 200704 | tf_op jit(solution)/shard_map/dot_general | solution.py:413
  82.0 0.6 div.43
  (47 shorter events, 1.7 us)
Async XLA Ops:
  0.6 0.8 copy-start
  0.6 6.2 %copy-start.1 = (bf16[8,2,8192]{2,1,0:T(2,128)(2,1)S(1)}, bf16[8,2,8192]{2,1,0:T(2,128)(2,1)}, u32[]{:S(2)}) copy-start(bf16[8,2,8192]{2,1,0:T(2,128)(2,1)} %param.8) | copy-start | bytes 786436
  7.1 1.3 %copy-start.3 = (bf16[16,2,8192]{2,1,0:T(2,128)(2,1)S(1)}, bf16[16,2,8192]{2,1,0:T(2,128)(2,1)}, u32[]{:S(2)}) copy-start(bf16[16,2,8192]{2,1,0:T(2,128)(2,1)} %param.9) | copy-start | bytes 1572868
  7.1 1.8 %copy-start.7 = (s32[8192]{0:T(1024)S(1)}, s32[8192]{0:T(1024)}, u32[]{:S(2)}) copy-start(s32[8192]{0:T(1024)} %param.14) | copy-start | bytes 98308
  8.4 3.3 %copy-start.2 = (bf16[8,16,1,8192]{3,1,2,0:T(8,128)(2,1)}, bf16[8,16,1,8192]{3,1,2,0:T(8,128)(2,1)S(1)}, u32[]{:S(2)}) copy-start(bf16[8,16,1,8192]{3,1,2,0:T(8,128)(2,1)S(1)} %get-tuple-element.34) | copy-start | bytes 6291460
  8.4 1.7 %copy-start.14 = (f32[64]{0:T(128)S(1)}, f32[64]{0:T(128)}, u32[]{:S(2)}) copy-start(f32[64]{0:T(128)} %param.15) | copy-start | bytes 772
  8.4 1.9 %copy-start.13 = (s32[8,16]{1,0:T(8,128)S(1)}, s32[8,16]{1,0:T(8,128)}, u32[]{:S(2)}) copy-start(s32[8,16]{1,0:T(8,128)} %param.11) | copy-start | bytes 1540
  11.7 0.6 copy-start.6
  43.0 3.4 %copy-start.5 = (f32[8,16,16]{2,1,0:T(8,128)}, f32[8,16,16]{2,1,0:T(8,128)S(1)}, u32[]{:S(2)}) copy-start(f32[8,16,16]{2,1,0:T(8,128)S(1)} %get-tuple-element.32) | copy-start | bytes 24580
  43.0 0.6 copy-start.10
  43.6 3.1 %copy-start.8 = (s32[8192]{0:T(1024)S(1)}, s32[8192]{0:T(1024)}, u32[]{:S(2)}) copy-start(s32[8192]{0:T(1024)} %param.14) | copy-start | bytes 98308
  46.4 30.3 %copy-start.4 = (bf16[32,16,256]{2,1,0:T(8,128)(2,1)S(1)}, bf16[32,16,256]{2,1,0:T(8,128)(2,1)}, u32[]{:S(2)}) copy-start(bf16[32,16,256]{2,1,0:T(8,128)(2,1)} %get-tuple-element.11) | copy-start | bytes 786436
  75.8 1.6 %copy-start.9 = (s32[8192]{0:T(1024)S(1)}, s32[8192]{0:T(1024)}, u32[]{:S(2)}) copy-start(s32[8192]{0:T(1024)} %param.14) | copy-start | bytes 98308
  79.5 1.5 %copy-start.11 = (f32[32,8,128]{2,1,0:T(8,128)S(1)}, f32[32,8,128]{2,1,0:T(8,128)}, u32[]{:S(2)}) copy-start(f32[32,8,128]{2,1,0:T(8,128)} %get-tuple-element.12) | copy-start | bytes 393220
  79.5 2.4 %copy-start.12 = (f32[16,8,128]{2,1,0:T(8,128)S(1)}, f32[16,8,128]{2,1,0:T(8,128)}, u32[]{:S(2)}) copy-start(f32[16,8,128]{2,1,0:T(8,128)} %get-tuple-element.13) | copy-start | bytes 196612

commit v15 on v10

--- a/solution.py
+++ b/solution.py
@@ -177,10 +177,8 @@
     )(stats, part_rows)
 
 
-def _spread_kernel(dom_n, orient_n, half_ref, small_ref,
-                   half_out, small_out, terms_out,
-                   half_held, small_held, summed, terms_held,
-                   send_sem, recv_sem, orient_send, orient_recv):
+def _spread_kernel(dom_n, orient_n, lead, packed_ref, packed_out, terms_out,
+                   packed_held, summed, terms_held, send_sem, recv_sem, orient_send, orient_recv):
     me = lax.axis_index("dom")
     mine = lax.axis_index("orient")
     barrier = pltpu.get_barrier_semaphore()
@@ -199,39 +197,30 @@
     lax.fori_loop(1, orient_n, greet_orient, 0)
     pl.semaphore_wait(barrier, dom_n + orient_n - 2)
 
-    sources = (half_ref, small_ref)
-    held = (half_held, small_held)
-
-    def copy(index, k):
+    def copy(k):
         peer = lax.rem(me + k, dom_n)
         return pltpu.make_async_remote_copy(
-            src_ref=sources[index],
-            dst_ref=held[index].at[me],
-            send_sem=send_sem.at[index, k],
-            recv_sem=recv_sem.at[index, k],
+            src_ref=packed_ref,
+            dst_ref=packed_held.at[me],
+            send_sem=send_sem.at[k],
+            recv_sem=recv_sem.at[k],
             device_id={"dom": peer},
             device_id_type=MESH_ID,
         )
 
     def start(k, carry):
-        for index in (1, 0):
-            copy(index, k).start()
+        copy(k).start()
         return carry
 
     lax.fori_loop(1, dom_n, start, 0)
-    for index in range(2):
-        held[index][me] = sources[index][...]
-
-    def finish(index):
-        def body(k, carry):
-            copy(index, k).wait()
-            return carry
-
-        lax.fori_loop(1, dom_n, body, 0)
-
-    finish(1)
-    summed[...] = jnp.sum(small_held[...], axis=0)
-    finish(0)
+    packed_held[me] = packed_ref[...]
+
+    def finish(k, carry):
+        copy(k).wait()
+        return carry
+
+    lax.fori_loop(1, dom_n, finish, 0)
+    summed[...] = jnp.sum(packed_held[:, lead:, :], axis=0)
 
     def orient_copy(k):
         peer = lax.rem(mine + k, orient_n)
@@ -256,35 +245,33 @@
         return carry
 
     lax.fori_loop(1, orient_n, orient_finish, 0)
-    half_out[...] = half_held[...]
-    small_out[...] = small_held[...]
+    packed_out[...] = packed_held[...]
     terms_out[...] = terms_held[...]
 
 
-def spread(half_rows, small, dom_n, orient_n, collective_id):
+def spread(packed, lead, dom_n, orient_n, collective_id):
+    small_shape = (packed.shape[0] - lead, packed.shape[1])
     shapes = (
-        jax.ShapeDtypeStruct((dom_n,) + half_rows.shape, half_rows.dtype),
-        jax.ShapeDtypeStruct((dom_n,) + small.shape, small.dtype),
-        jax.ShapeDtypeStruct((orient_n,) + small.shape, small.dtype),
+        jax.ShapeDtypeStruct((dom_n,) + packed.shape, packed.dtype),
+        jax.ShapeDtypeStruct((orient_n,) + small_shape, packed.dtype),
     )
     vmem = pl.BlockSpec(memory_space=pltpu.VMEM)
     return pl.pallas_call(
-        functools.partial(_spread_kernel, dom_n, orient_n),
+        functools.partial(_spread_kernel, dom_n, orient_n, lead),
         out_shape=shapes,
-        in_specs=[vmem] * 2,
-        out_specs=(vmem,) * 3,
+        in_specs=[vmem],
+        out_specs=(vmem, vmem),
         scratch_shapes=[
             pltpu.VMEM(shapes[0].shape, shapes[0].dtype),
+            pltpu.VMEM(small_shape, packed.dtype),
             pltpu.VMEM(shapes[1].shape, shapes[1].dtype),
-            pltpu.VMEM(small.shape, small.dtype),
-            pltpu.VMEM(shapes[2].shape, shapes[2].dtype),
-            pltpu.SemaphoreType.DMA((2, dom_n)),
-            pltpu.SemaphoreType.DMA((2, dom_n)),
+            pltpu.SemaphoreType.DMA((dom_n,)),
+            pltpu.SemaphoreType.DMA((dom_n,)),
             pltpu.SemaphoreType.DMA((orient_n,)),
             pltpu.SemaphoreType.DMA((orient_n,)),
         ],
         compiler_params=pltpu.CompilerParams(collective_id=collective_id, has_side_effects=True),
-    )(half_rows, small)
+    )(packed)
 
 
 def make_images(planes, ctf_pix, cosine, sine_part):
@@ -378,7 +365,12 @@
     small = jnp.concatenate([weight_rows, term_rows], axis=1)
     small = jnp.pad(small, ((0, 0), (0, -(-small.shape[1] // 128) * 128 - small.shape[1])))
     half_rows = post_half.reshape(-1, 128)
-    half_all, small_all, orient_small = spread(half_rows, small, dom_size, orient_size, 2)
+    lead = half_rows.shape[0]
+    packed_all, orient_small = spread(
+        jnp.concatenate([half_rows.astype(jnp.float32), small], axis=0), lead, dom_size, orient_size, 2
+    )
+    half_all = packed_all[:, :lead, :].astype(jnp.bfloat16)
+    small_all = packed_all[:, lead:, :]
     post_all = half_all.reshape(dom_size * part_dev, trans_count, ori_dev)
     weight_all = small_all[:, :, :ori_dev].reshape(dom_size * part_dev, ori_dev)
     shell_total = jnp.sum(

time: 83.1 us -> 84.7 us (1.019)
  Pallas kernels: 50.7 us -> 52 us
  local copies, waits for them, and re-layouts: 12.1 us -> 10.9 us
  matrix products: 11.3 us -> 12.2 us
    convert_element_type x1, other arithmetic: 0.01 us -> 1.56 us  [on_device(): half_rows.astype(jnp.float32)]
    reshape x1 -> x0, local copies, waits for them, and re-layouts: 1.45 us -> none  [on_device(): half_rows = post_half.reshape(-1, 128)]
    pallas_call x1, Pallas kernels: 25.2 us -> 26.4 us  [spread(): pl.pallas_call(functools.partial(_spread_kernel, dom_n, orient_n, lead),...]
    reshape x2, local copies, waits for them, and re-layouts: 2.58 us -> 1.49 us  [on_device(): post_all = half_all.reshape(dom_size * part_dev, trans_count, ori_dev)]
    slice x0 -> x1, local copies, waits for them, and re-layouts: none -> 0.98 us  [on_device(): half_all = packed_all[:, :lead, :].astype(jnp.bfloat16)]
    convert_element_type x0 -> x1, local copies, waits for them, and re-layouts: none -> 0.93 us  [on_device(): half_rows.astype(jnp.float32)]
    reduce_sum x1, other arithmetic: 1.07 us -> 0.15 us  [on_device(): jnp.sum(weight_rows, axis=1)[:, None]]
    dot_general x1, matrix products: 0.95 us -> 1.85 us  [on_device(): ctf_weights = jnp.dot(weight_all.T, ctf_all * ctf_all, precision=highest)]
where the time goes in v15:
time: 84.7 us; the launch traced here: 84.1 us
  Pallas kernels  52 us (61%)
  matrix products  12.2 us (14%)
  local copies, waits for them, and re-layouts  10.9 us (13%)
  other arithmetic  8.1 us (10%)
  between operations  0.97 us (1%)
    pallas_call x1, Pallas kernels, spread(): pl.pallas_call(functools.partial(_spread_kernel, dom_n, orient_n, lead),...  26.4 us
    pallas_call x1, Pallas kernels, stats_and_columns(): pl.pallas_call(functools.partial(_stats_kernel, dom_n, orient_n, width),...  25.5 us
    cos x1, local copies, waits for them, and re-layouts, on_device(): cosines = jnp.cos(phases)  2.8 us
    dot_general x1, matrix products, on_device(): jnp.einsum('itj,itpk->jpk', post_half, images, preferred_element_type=jnp...  2.78 us
    another operation x2, other arithmetic  2.67 us
    unnamed x28, local copies, waits for them, and re-layouts  2.12 us
    dot_general x1, matrix products, on_device(): ctf_weights = jnp.dot(weight_all.T, ctf_all * ctf_all, precision=highest)  1.85 us

profile of v15, /device:TPU:1, one launch (start us, length us, event | category | flops | bytes accessed | tf_op | source)
XLA Modules:
  0.0 84.1 jit_solution(6353789448588405091)
XLA Ops:
  0.7 0.7 copy-done
  1.4 1.0 %fusion.37 = f32[256,64]{0,1:T(8,128)S(1)} fusion(f32[64,64]{1,0:T(8,128)S(1)} %copy-done, s32[256]{0:T(256)} %param.12), kind=kOutput, calls=%fused_computation.53 | convolution fusion | flops 12599296 | bytes 82944 | tf_op jit(solution)/shard_map/dot_general | solution.py:310
  2.5 1.5 %fusion.8 = f32[9,8192]{1,0:T(8,128)S(1)} fusion(s32[8192]{0:T(1024)} %param.14, f32[1,64]{1,0:T(1,128)} %bitcast.71, f32[8,64]{1,0:T(8,128)S(1)} %copy.34), kind=kOutput, calls=%fused_computation.15 | convolution fusion | flops 57147968 | bytes 329984 | tf_op jit(solution)/shard_map/dot_general | solution.py:312
  4.1 2.8 %fusion.64 = (f32[16,8192]{1,0:T(8,128)S(1)}, f32[16,8192]{1,0:T(8,128)S(1)}) fusion(f32[16,8192]{1,0:T(8,128)} %param.10), kind=kLoop, calls=%fused_computation.98 | loop fusion | bytes 1572864 | tf_op jit(solution)/shard_map/cos | solution.py:330
  7.1 1.3 %multiply_convert_fusion.3 = (bf16[8,16,1,8192]{3,1,2,0:T(8,128)(2,1)S(1)}, bf16[8,16,1,8192]{3,1,2,0:T(8,128)(2,1)S(1)}) fusion(f32[16,8192]{1,0:T(8,128)S(1)} %get-tuple-element.41, f32[8,8192]{1,0:T(8,128)S(1)} %get-tuple-element.39, f32[16,8192]{1,0:T(8,128)S(1)} %get-tuple-element.40, f32[8,8192]{1,0:T(8,128)S(1)} %get-tuple-element.38, ...), kind=kLoop, calls=%fused_computation.10 | loop fusion | flops 10485760 | bytes 6029312 | tf_op jit(solution)/shard_map/convert.5
  8.4 0.3 fusion.22
  8.9 1.1 %fusion.7 = f32[24,64]{1,0:T(8,128)S(1)} fusion(s32[8192]{0:T(1024)S(1)} %copy-done.7, f32[8,8192]{1,0:T(8,128)S(1)} %multiply_reduce_fusion, f32[16,8192]{1,0:T(8,128)S(1)} %fusion.22), kind=kOutput, calls=%fused_computation.14 | convolution fusion | flops 151715840 | bytes 825344 | tf_op jit(solution)/shard_map/dot_general | solution.py:320
  10.3 1.4 %fusion.65 = (f32[8]{0:T(128)S(1)}, f32[8,16,16]{2,1,0:T(8,128)S(1)}) fusion(f32[8,16]{1,0:T(8,128)S(1)} %convolution_multiply_fusion.1, f32[8192]{0:T(1024)S(1)} %bitcast.70, bf16[16,2,8192]{2,1,0:T(2,128)(2,1)S(1)} %copy-done.3, bf16[8,16,1,8192]{3,1,2,0:T(8,128)(2,1)S(1)} %get-tuple-element.33, bf16[8,16,1,8192]{3,1,2,0:T(8,128)(2,1)S(1)} %get-tuple-element.32, ...), kind=kOutput, calls=%fused_computation.99 | convolution fusion | flops 69998584 | bytes 4760224 | tf_op jit(solution)/shard_map/itpk,jpk->itj/dot_general | solution.py:334
  11.7 0.6 copy-done.6
  12.6 0.6 select_maximum_fusion.1.stats_ref
  13.2 0.8 reshape.95.part_ref
  14.0 25.5 %shard_map.111 = (f32[16,8,128]{2,1,0:T(8,128)}, bf16[32,16,256]{2,1,0:T(8,128)(2,1)}) custom-call(f32[8,128]{1,0:T(8,128)} %select_maximum_fusion.1.stats_ref, bf16[16,8192]{1,0:T(8,128)(2,1)} %reshape.95.part_ref), custom_call_target="tpu_custom_call" | custom-call | tf_op jit(solution)/shard_map/pallas_call | solution.py:163
  39.5 1.0 %slice_reduce_fusion.1 = (f32[8]{0:T(128)S(1)}, f32[16,1,8]{2,1,0:T(1,128)S(1)}, f32[16,1,8]{2,1,0:T(1,128)S(1)}) fusion(f32[16,8,128]{2,1,0:T(8,128)} %get-tuple-element.8), kind=kLoop, calls=%fused_computation.95 | loop fusion | flops 120 | bytes 2080 | tf_op jit(solution)/shard_map/reduce_max | solution.py:350
  40.8 1.6 %convert_convert_fusion = (f32[8,16,16]{2,1,0:T(8,128)}, f32[8,16,16]{2,1,0:T(8,128)S(1)}) fusion(f32[8]{0:T(128)S(1)} %fusion.54, f32[8,16,16]{2,1,0:T(8,128)} %copy-done.6, f32[8]{0:T(128)S(1)} %get-tuple-element.42), kind=kLoop, calls=%fused_computation.65 | loop fusion | flops 8192 | bytes 24640 | tf_op jit(solution)/shard_map/convert_element_type | solution.py:370
  42.4 2.8 %fusion.9 = f32[8192]{0:T(1024)S(1)} fusion(bf16[8,16,1,8192]{3,1,2,0:T(8,128)(2,1)} %copy-done.2, bf16[8,16,1,8192]{3,1,2,0:T(8,128)(2,1)S(1)} %get-tuple-element.32, bf16[16,2,8192]{2,1,0:T(2,128)(2,1)} %param.9, f32[8,16,16]{2,1,0:T(8,128)S(1)} %get-tuple-element.31), kind=kOutput, calls=%fused_computation.18 | convolution fusion | flops 76277760 | bytes 4759552 | tf_op jit(solution)/shard_map/itj,itpk->jpk/dot_general | solution.py:359
  45.3 0.2 fusion.16
  45.6 1.0 %fusion.20 = f32[64]{0:T(128)S(1)} fusion(f32[64]{0:T(128)S(1)} %fusion.16, f32[64]{0:T(128)S(1)} %fusion.51, f32[8192,1]{0,1:T(1,128)S(1)} %bitcast.74, s32[8192]{0:T(1024)S(1)} %copy-done.8), kind=kOutput, calls=%fused_computation.29 | convolution fusion | flops 6815936 | bytes 66304 | tf_op jit(solution)/shard_map/dot_general | solution.py:360
  46.9 0.9 %reshape.99 = f32[16,128]{1,0:T(8,128)S(1)} reshape(f32[8,16,16]{2,1,0:T(8,128)} %get-tuple-element.30) | data formatting | bytes 16384 | tf_op jit(solution)/shard_map/convert_element_type | solution.py:370
  47.8 0.6 pad_maximum_fusion.11.packed_ref
  48.4 26.4 %shard_map.112 = (f32[32,24,128]{2,1,0:T(8,128)}, f32[16,8,128]{2,1,0:T(8,128)}) custom-call(f32[24,128]{1,0:T(8,128)} %pad_maximum_fusion.11.packed_ref), custom_call_target="tpu_custom_call" | custom-call | tf_op jit(solution)/shard_map/pallas_call | solution.py:259
  74.8 1.0 %slice.81 = bf16[32,16,128]{2,1,0:T(8,128)(2,1)S(1)} slice(f32[32,24,128]{2,1,0:T(8,128)} %get-tuple-element.9), slice={[0:32], [0:16], [0:128]} | slice | bytes 262144 | tf_op jit(solution)/shard_map/slice | solution.py:372
  75.8 0.7 reshape.97
  76.5 0.8 copy.41
  77.3 0.3 reshape.100
  77.6 0.4 fusion.63
  78.1 0.3 iota_compare_fusion
  78.4 0.3 fusion.40
  78.7 1.4 %multiply_convert_fusion.1 = (bf16[256,16,1,256]{3,0,1,2:T(8,128)(2,1)S(1)}, bf16[256,16,1,256]{3,0,1,2:T(8,128)(2,1)S(1)}) fusion(f32[16,256]{1,0:T(8,128)S(1)} %get-tuple-element.47, f32[256,256]{1,0:T(8,128)S(1)} %get-tuple-element.49, f32[16,256]{1,0:T(8,128)S(1)} %get-tuple-element.48, f32[256,256]{1,0:T(8,128)S(1)} %get-tuple-element.50, ...), kind=kLoop, calls=%fused_computation.8 | loop fusion | flops 10485760 | bytes 5013504 | tf_op jit(solution)/shard_map/convert.2
  80.1 0.8 fusion.13
  80.9 0.6 copy.42
  81.6 1.9 %fusion.33 = f32[16,64]{1,0:T(8,128)} fusion(f32[32,24,128]{2,1,0:T(8,128)} %get-tuple-element.9, f32[256,64]{0,1:T(8,128)S(1)} %fusion.37), kind=kOutput, calls=%fused_computation.48 | convolution fusion | flops 3162112 | bytes 200704 | tf_op jit(solution)/shard_map/dot_general | solution.py:381
  83.5 0.6 div.43
  (45 shorter events, 1.9 us)
Async XLA Ops:
  0.6 0.8 copy-start
  0.6 6.2 %copy-start.1 = (bf16[8,2,8192]{2,1,0:T(2,128)(2,1)S(1)}, bf16[8,2,8192]{2,1,0:T(2,128)(2,1)}, u32[]{:S(2)}) copy-start(bf16[8,2,8192]{2,1,0:T(2,128)(2,1)} %param.8) | copy-start | bytes 786436
  7.1 1.3 %copy-start.3 = (bf16[16,2,8192]{2,1,0:T(2,128)(2,1)S(1)}, bf16[16,2,8192]{2,1,0:T(2,128)(2,1)}, u32[]{:S(2)}) copy-start(bf16[16,2,8192]{2,1,0:T(2,128)(2,1)} %param.9) | copy-start | bytes 1572868
  7.1 1.8 %copy-start.7 = (s32[8192]{0:T(1024)S(1)}, s32[8192]{0:T(1024)}, u32[]{:S(2)}) copy-start(s32[8192]{0:T(1024)} %param.14) | copy-start | bytes 98308
  8.4 3.3 %copy-start.2 = (bf16[8,16,1,8192]{3,1,2,0:T(8,128)(2,1)}, bf16[8,16,1,8192]{3,1,2,0:T(8,128)(2,1)S(1)}, u32[]{:S(2)}) copy-start(bf16[8,16,1,8192]{3,1,2,0:T(8,128)(2,1)S(1)} %get-tuple-element.33) | copy-start | bytes 6291460
  8.4 1.7 %copy-start.12 = (f32[64]{0:T(128)S(1)}, f32[64]{0:T(128)}, u32[]{:S(2)}) copy-start(f32[64]{0:T(128)} %param.15) | copy-start | bytes 772
  8.4 1.9 %copy-start.11 = (s32[8,16]{1,0:T(8,128)S(1)}, s32[8,16]{1,0:T(8,128)}, u32[]{:S(2)}) copy-start(s32[8,16]{1,0:T(8,128)} %param.11) | copy-start | bytes 1540
  11.7 0.6 copy-start.6
  42.4 2.8 %copy-start.5 = (f32[8,16,16]{2,1,0:T(8,128)}, f32[8,16,16]{2,1,0:T(8,128)S(1)}, u32[]{:S(2)}) copy-start(f32[8,16,16]{2,1,0:T(8,128)S(1)} %get-tuple-element.31) | copy-start | bytes 24580
  42.4 3.3 %copy-start.8 = (s32[8192]{0:T(1024)S(1)}, s32[8192]{0:T(1024)}, u32[]{:S(2)}) copy-start(s32[8192]{0:T(1024)} %param.14) | copy-start | bytes 98308
  45.1 32.2 %copy-start.4 = (bf16[32,16,256]{2,1,0:T(8,128)(2,1)S(1)}, bf16[32,16,256]{2,1,0:T(8,128)(2,1)}, u32[]{:S(2)}) copy-start(bf16[32,16,256]{2,1,0:T(8,128)(2,1)} %get-tuple-element.10) | copy-start | bytes 786436
  76.5 1.6 %copy-start.9 = (s32[8192]{0:T(1024)S(1)}, s32[8192]{0:T(1024)}, u32[]{:S(2)}) copy-start(s32[8192]{0:T(1024)} %param.14) | copy-start | bytes 98308
  80.1 3.3 %copy-start.10 = (f32[16,8,128]{2,1,0:T(8,128)S(1)}, f32[16,8,128]{2,1,0:T(8,128)}, u32[]{:S(2)}) copy-start(f32[16,8,128]{2,1,0:T(8,128)} %get-tuple-element.11) | copy-start | bytes 196612

commit v16 on v10

--- a/solution.py
+++ b/solution.py
@@ -114,7 +114,7 @@
         )
 
     def columns(peer):
-        return part_ref.at[:, pl.ds(pl.multiple_of(peer * width, width), width)]
+        return part_ref.at[:, :, pl.ds(pl.multiple_of(peer * width, width), width)]
 
     def dom_copy(k):
         peer = lax.rem(me + k, dom_n)
@@ -157,7 +157,7 @@
 def stats_and_columns(stats, part_rows, dom_n, orient_n, width, collective_id):
     shapes = (
         jax.ShapeDtypeStruct((orient_n,) + stats.shape, stats.dtype),
-        jax.ShapeDtypeStruct((dom_n, part_rows.shape[0], width), part_rows.dtype),
+        jax.ShapeDtypeStruct((dom_n,) + part_rows.shape[:2] + (width,), part_rows.dtype),
     )
     vmem = pl.BlockSpec(memory_space=pltpu.VMEM)
     return pl.pallas_call(
@@ -352,7 +352,7 @@
 
     stats, columns = stats_and_columns(
         pad_rows(jnp.stack([local_peak, local_total]), 128),
-        particles.reshape(part_dev * 2, pixels),
+        particles,
         dom_size,
         orient_size,
         width,

time: 83.1 us -> 81.4 us (0.980)
  local copies, waits for them, and re-layouts: 12.1 us -> 6.39 us
  other arithmetic: 7.47 us -> 10.6 us
  matrix products: 11.3 us -> 12.2 us
    unnamed x32 -> x22, local copies, waits for them, and re-layouts: 2.74 us -> 0.75 us
    convert_element_type x1, other arithmetic: 0.16 us -> 1.3 us  [on_device(): planes = particles.astype(jnp.float32)]
    reshape x2, local copies, waits for them, and re-layouts: 2.58 us -> 1.49 us  [on_device(): post_all = half_all.reshape(dom_size * part_dev, trans_count, ori_dev)]
    reduce_sum x1, other arithmetic: 0.15 us -> 1.14 us  [on_device(): jnp.sum(planes * planes, axis=1)]
    dot_general x1, matrix products: 0.95 us -> 1.89 us  [on_device(): ctf_weights = jnp.dot(weight_all.T, ctf_all * ctf_all, precision=highest)]
    reduce_sum x1, other arithmetic: 0.08 us -> 0.92 us  [on_device(): jnp.sum(orient_small[:, :, ori_dev:ori_dev + term_cols].reshape(orient_si...]
    reduce_sum x1, other arithmetic: 1.07 us -> 0.23 us  [on_device(): jnp.sum(weight_rows, axis=1)[:, None]]
where the time goes in v16:
time: 81.4 us; the launch traced here: 80.9 us
  Pallas kernels  50.8 us (62%)
  matrix products  12.2 us (15%)
  other arithmetic  10.6 us (13%)
  local copies, waits for them, and re-layouts  6.39 us (8%)
  between operations  0.94 us (1%)
    pallas_call x1, Pallas kernels, stats_and_columns(): pl.pallas_call(functools.partial(_stats_kernel, dom_n, orient_n, width),...  25.6 us
    pallas_call x1, Pallas kernels, spread(): pl.pallas_call(functools.partial(_spread_kernel, dom_n, orient_n), out_sh...  25.2 us
    dot_general x1, matrix products, on_device(): jnp.einsum('itj,itpk->jpk', post_half, images, preferred_element_type=jnp...  2.71 us
    another operation x2, other arithmetic  2.67 us
    cos x1, local copies, waits for them, and re-layouts, on_device(): cosines = jnp.cos(phases)  2.04 us
    dot_general x1, matrix products, on_device(): ctf_weights = jnp.dot(weight_all.T, ctf_all * ctf_all, precision=highest)  1.89 us

profile of v16, /device:TPU:1, one launch (start us, length us, event | category | flops | bytes accessed | tf_op | source)
XLA Modules:
  0.0 80.9 jit_solution(7328727683266513451)
XLA Ops:
  0.7 0.7 broadcast_compare_fusion
  1.4 1.0 %fusion.37 = f32[256,64]{0,1:T(8,128)S(1)} fusion(f32[64,64]{1,0:T(8,128)S(1)} %copy-done, s32[256]{0:T(256)} %param.12), kind=kOutput, calls=%fused_computation.53 | convolution fusion | flops 12599296 | bytes 82944 | tf_op jit(solution)/shard_map/dot_general | solution.py:323
  2.5 1.1 %multiply_reduce_fusion = f32[8,8192]{1,0:T(8,128)S(1)} fusion(bf16[8,2,8192]{2,1,0:T(2,128)(2,1)} %part_ref.1), kind=kLoop, calls=%fused_computation.39 | loop fusion | flops 327680 | bytes 524288 | tf_op jit(solution)/shard_map/reduce_sum | solution.py:334
  3.7 1.6 %fusion.8 = f32[9,8192]{1,0:T(8,128)S(1)} fusion(s32[8192]{0:T(1024)} %param.14, f32[1,64]{1,0:T(1,128)} %bitcast.74, f32[8,64]{1,0:T(8,128)S(1)} %copy.34), kind=kOutput, calls=%fused_computation.15 | convolution fusion | flops 57147968 | bytes 329984 | tf_op jit(solution)/shard_map/dot_general | solution.py:325
  5.3 1.3 %copy_convert_fusion = f32[8,2,8192]{2,0,1:T(8,128)S(1)} fusion(bf16[8,2,8192]{2,1,0:T(2,128)(2,1)} %part_ref.1), kind=kLoop, calls=%fused_computation.47 | loop fusion | flops 131072 | bytes 786432 | tf_op jit(solution)/shard_map/convert_element_type | solution.py:332
  6.6 0.3 fusion.22
  7.0 1.1 %fusion.7 = f32[24,64]{1,0:T(8,128)S(1)} fusion(s32[8192]{0:T(1024)S(1)} %copy-done.8, f32[8,8192]{1,0:T(8,128)S(1)} %multiply_reduce_fusion, f32[16,8192]{1,0:T(8,128)S(1)} %fusion.22), kind=kOutput, calls=%fused_computation.14 | convolution fusion | flops 151715840 | bytes 825344 | tf_op jit(solution)/shard_map/dot_general | solution.py:333
  8.3 0.3 iota_compare_fusion
  8.6 0.3 fusion.40
  9.0 2.0 %fusion.63 = (f32[16,8192]{1,0:T(8,128)S(1)}, f32[16,8192]{1,0:T(8,128)S(1)}) fusion(f32[16,8192]{1,0:T(8,128)S(1)} %copy-done.3), kind=kLoop, calls=%fused_computation.95 | loop fusion | bytes 1572864 | tf_op jit(solution)/shard_map/cos | solution.py:343
  11.1 1.3 %multiply_convert_fusion.3 = (bf16[8,16,1,8192]{3,1,2,0:T(8,128)(2,1)S(1)}, bf16[8,16,1,8192]{3,1,2,0:T(8,128)(2,1)S(1)}) fusion(f32[16,8192]{1,0:T(8,128)S(1)} %get-tuple-element.42, f32[8,8192]{1,0:T(8,128)S(1)} %get-tuple-element.40, f32[16,8192]{1,0:T(8,128)S(1)} %get-tuple-element.41, f32[8,8192]{1,0:T(8,128)S(1)} %get-tuple-element.39, ...), kind=kLoop, calls=%fused_computation.10 | loop fusion | flops 10485760 | bytes 6029312 | tf_op jit(solution)/shard_map/convert.3
  12.4 1.4 %fusion.64 = (f32[8]{0:T(128)S(1)}, f32[8,16,16]{2,1,0:T(8,128)S(1)}) fusion(f32[8,16]{1,0:T(8,128)S(1)} %convolution_multiply_fusion.1, f32[8192]{0:T(1024)S(1)} %bitcast.73, bf16[16,2,8192]{2,1,0:T(2,128)(2,1)S(1)} %copy-done.4, bf16[8,16,1,8192]{3,1,2,0:T(8,128)(2,1)S(1)} %get-tuple-element.34, bf16[8,16,1,8192]{3,1,2,0:T(8,128)(2,1)S(1)} %get-tuple-element.33, ...), kind=kOutput, calls=%fused_computation.96 | convolution fusion | flops 69998584 | bytes 4760224 | tf_op jit(solution)/shard_map/itpk,jpk->itj/dot_general | solution.py:347
  13.7 0.2 exponential_reduce_fusion
  13.9 0.6 select_maximum_fusion.1.stats_ref
  14.6 25.6 %shard_map.111 = (f32[16,8,128]{2,1,0:T(8,128)}, bf16[32,8,2,256]{3,2,1,0:T(2,128)(2,1)}) custom-call(f32[8,128]{1,0:T(8,128)} %select_maximum_fusion.1.stats_ref, bf16[8,2,8192]{2,1,0:T(2,128)(2,1)} %part_ref.1), custom_call_target="tpu_custom_call" | custom-call | tf_op jit(solution)/shard_map/pallas_call | solution.py:163
  40.1 1.0 %slice_reduce_fusion.1 = (f32[8]{0:T(128)S(1)}, f32[16,1,8]{2,1,0:T(1,128)S(1)}, f32[16,1,8]{2,1,0:T(1,128)S(1)}) fusion(f32[16,8,128]{2,1,0:T(8,128)} %get-tuple-element.9), kind=kLoop, calls=%fused_computation.92 | loop fusion | flops 120 | bytes 2080 | tf_op jit(solution)/shard_map/reduce_max | solution.py:363
  41.4 0.2 fusion.61
  41.6 0.2 fusion.16
  42.0 2.7 %fusion.9 = f32[8192]{0:T(1024)S(1)} fusion(bf16[8,16,1,8192]{3,1,2,0:T(8,128)(2,1)} %copy-done.1, bf16[8,16,1,8192]{3,1,2,0:T(8,128)(2,1)S(1)} %get-tuple-element.33, bf16[16,2,8192]{2,1,0:T(2,128)(2,1)S(1)} %copy-done.4, bf16[8,16,16]{2,1,0:T(8,128)(2,1)S(1)} %convert_element_type.29), kind=kOutput, calls=%fused_computation.18 | convolution fusion | flops 76275712 | bytes 4755456 | tf_op jit(solution)/shard_map/itj,itpk->jpk/dot_general | solution.py:372
  44.7 0.7 reshape.92.half_ref
  45.4 1.0 %fusion.20 = f32[64]{0:T(128)S(1)} fusion(f32[64]{0:T(128)S(1)} %fusion.16, f32[64]{0:T(128)S(1)} %fusion.50, f32[8192,1]{0,1:T(1,128)S(1)} %bitcast.77, s32[8192]{0:T(1024)S(1)} %copy-done.8), kind=kOutput, calls=%fused_computation.29 | convolution fusion | flops 6815936 | bytes 66304 | tf_op jit(solution)/shard_map/dot_general | solution.py:373
  46.5 0.7 select_maximum_fusion.small_ref
  47.2 25.2 %shard_map.112 = (bf16[32,16,128]{2,1,0:T(8,128)(2,1)}, f32[32,8,128]{2,1,0:T(8,128)}, f32[16,8,128]{2,1,0:T(8,128)}) custom-call(bf16[16,128]{1,0:T(8,128)(2,1)} %reshape.92.half_ref, f32[8,128]{1,0:T(8,128)} %select_maximum_fusion.small_ref), custom_call_target="tpu_custom_call" | custom-call | tf_op jit(solution)/shard_map/pallas_call | solution.py:271
  72.4 1.9 %fusion.33 = f32[16,64]{1,0:T(8,128)} fusion(f32[32,8,128]{2,1,0:T(8,128)} %get-tuple-element.12, f32[256,64]{0,1:T(8,128)S(1)} %fusion.37), kind=kOutput, calls=%fused_computation.48 | convolution fusion | flops 3162112 | bytes 200704 | tf_op jit(solution)/shard_map/dot_general | solution.py:389
  74.3 0.9 %slice_reduce_fusion = f32[8,8]{1,0:T(8,128)S(1)} fusion(f32[16,8,128]{2,1,0:T(8,128)} %get-tuple-element.13), kind=kLoop, calls=%fused_computation.54 | loop fusion | flops 960 | bytes 4352 | tf_op jit(solution)/shard_map/reduce_sum | solution.py:384
  75.3 0.6 div.43
  76.1 0.4 fusion.62
  76.5 0.7 reshape.94
  77.2 0.8 %copy.41 = bf16[256,16,16]{0,2,1:T(8,128)(2,1)S(1)} copy(bf16[256,16,16]{2,1,0:T(8,128)(2,1)S(1)} %reshape.94) | data formatting | bytes 262144 | tf_op jit(solution)/shard_map/reshape | solution.py:382
  78.0 1.4 %multiply_convert_fusion.1 = (bf16[256,16,1,256]{3,0,1,2:T(8,128)(2,1)S(1)}, bf16[256,16,1,256]{3,0,1,2:T(8,128)(2,1)S(1)}) fusion(f32[16,256]{1,0:T(8,128)S(1)} %get-tuple-element.48, f32[256,256]{1,0:T(8,128)S(1)} %get-tuple-element.50, f32[16,256]{1,0:T(8,128)S(1)} %get-tuple-element.49, f32[256,256]{1,0:T(8,128)S(1)} %get-tuple-element.51, ...), kind=kLoop, calls=%fused_computation.8 | loop fusion | flops 10485760 | bytes 5013504 | tf_op jit(solution)/shard_map/convert.1
  79.4 0.8 fusion.13
  80.2 0.6 copy.42
  (38 shorter events, 1.2 us)
Async XLA Ops:
  0.6 0.8 copy-start
  0.6 6.0 %copy-start.4 = (bf16[16,2,8192]{2,1,0:T(2,128)(2,1)S(1)}, bf16[16,2,8192]{2,1,0:T(2,128)(2,1)}, u32[]{:S(2)}) copy-start(bf16[16,2,8192]{2,1,0:T(2,128)(2,1)} %param.9) | copy-start | bytes 1572868
  3.7 3.3 %copy-start.8 = (s32[8192]{0:T(1024)S(1)}, s32[8192]{0:T(1024)}, u32[]{:S(2)}) copy-start(s32[8192]{0:T(1024)} %param.14) | copy-start | bytes 98308
  5.3 2.9 %copy-start.2 = (f32[9,8192]{1,0:T(8,128)}, f32[9,8192]{1,0:T(8,128)S(1)}, u32[]{:S(2)}) copy-start(f32[9,8192]{1,0:T(8,128)S(1)} %fusion.8) | copy-start | bytes 884740
  5.3 2.9 %copy-start.9 = (f32[64]{0:T(128)S(1)}, f32[64]{0:T(128)}, u32[]{:S(2)}) copy-start(f32[64]{0:T(128)} %param.15) | copy-start | bytes 772
  6.6 2.4 %copy-start.3 = (f32[16,8192]{1,0:T(8,128)S(1)}, f32[16,8192]{1,0:T(8,128)}, u32[]{:S(2)}) copy-start(f32[16,8192]{1,0:T(8,128)} %param.10) | copy-start | bytes 1572868
  8.3 2.7 %slice-start.1 = ((f32[9,8192]{1,0:T(8,128)}), f32[8,8192]{1,0:T(8,128)S(1)}, s32[]{:S(2)}) async-start(f32[9,8192]{1,0:T(8,128)} %copy-done.2), calls=%async_computation.1 | async-start | bytes 524288 | tf_op jit(solution)/shard_map/slice | solution.py:328
  11.0 1.3 %slice-start = ((f32[9,8192]{1,0:T(8,128)}), f32[1,8192]{1,0:T(1,128)S(1)}, s32[]{:S(2)}) async-start(f32[9,8192]{1,0:T(8,128)} %copy-done.2), calls=%async_computation | async-start | bytes 65536 | tf_op jit(solution)/shard_map/slice | solution.py:329
  12.3 1.4 %copy-start.1 = (bf16[8,16,1,8192]{3,1,2,0:T(8,128)(2,1)}, bf16[8,16,1,8192]{3,1,2,0:T(8,128)(2,1)S(1)}, u32[]{:S(2)}) copy-start(bf16[8,16,1,8192]{3,1,2,0:T(8,128)(2,1)S(1)} %get-tuple-element.34) | copy-start | bytes 6291460
  41.6 3.1 %copy-start.6 = (f32[8,16,16]{2,1,0:T(8,128)}, f32[8,16,16]{2,1,0:T(8,128)S(1)}, u32[]{:S(2)}) copy-start(f32[8,16,16]{2,1,0:T(8,128)S(1)} %get-tuple-element.32) | copy-start | bytes 24580
  42.0 33.9 %copy-start.5 = (bf16[32,8,2,256]{3,2,1,0:T(2,128)(2,1)S(1)}, bf16[32,8,2,256]{3,2,1,0:T(2,128)(2,1)}, u32[]{:S(2)}) copy-start(bf16[32,8,2,256]{3,2,1,0:T(2,128)(2,1)} %get-tuple-element.11) | copy-start | bytes 786436
  72.4 4.1 %copy-start.7 = (bf16[32,16,128]{2,1,0:T(8,128)(2,1)S(1)}, bf16[32,16,128]{2,1,0:T(8,128)(2,1)}, u32[]{:S(2)}) copy-start(bf16[32,16,128]{2,1,0:T(8,128)(2,1)} %get-tuple-element.10) | copy-start | bytes 393220
